TPU v7x, 32 devices: a whole 2x2x4 slice. The times are simulated.
32 devices in a mesh: groups: 2 (over y), tok: 4 (over z), cache: 2 (over x), rep: 2 (over core).
Axes of the slice: x: 2, y: 2, z: 4, core: 2. Of those that a mesh axis runs over, the one named last changes fastest.
Arguments:
- x_in: bfloat16 [16, 512, 8192], P(('groups', 'rep'), 'tok', 'cache'), parts along dimension 0, may hold values from -6 to 6
- z_in: bfloat16 [16, 512, 8192], P(('groups', 'rep'), 'tok', 'cache'), parts along dimension 0, may hold values from -6 to 6
- b_in: bfloat16 [16, 512, 8, 128], P(('groups', 'rep'), 'tok', 'cache'), parts along dimension 0, may hold values from -6 to 6
- c_in: bfloat16 [16, 512, 8, 128], P(('groups', 'rep'), 'tok', 'cache'), parts along dimension 0, may hold values from -6 to 6
- dt_in: bfloat16 [16, 512, 128], P(('groups', 'rep'), 'tok', 'cache'), parts along dimension 0, may hold values from -2 to 10
- dt_bias: float32 [128], P('cache'), may hold values from -14 to -2
- a_log: float32 [128], P('cache'), may hold values from 0 to 3
- skip_gain: float32 [128], P('cache'), may hold values from 0.5 to 1.5
- norm_w: float32 [8192], P('cache'), may hold values from 0.5 to 1.5
- cache_states: float32 [8, 2, 64, 64, 128], P(('groups', 'cache'), None, 'tok'), parts along dimension 0, may hold values from -0.3 to 0.3
- parent: int32 [16], P('groups'), parts along dimension 0, may hold values from 0 to 3
- state_dev: int32 [8], P('groups'), parts along dimension 0, may hold values from 0 to 1, as said below
- state_slot: int32 [8], P('groups'), parts along dimension 0, may hold values from 0 to 1
- spans: int32 [16], P('groups'), parts along dimension 0, may hold values from 1 to 4
Outputs:
- y_out: bfloat16 [16, 512, 8192], P(('groups', 'rep'), 'tok', 'cache'), parts along dimension 0
- final_states: float32 [16, 128, 64, 128], P(('groups', 'rep'), ('cache', 'tok')), parts along dimension 0
There are 2 independent parts, one for each index of `groups`. A program takes and returns all parts, laid end to end along the dimension named above; an argument that names none is the same for every part. Nothing has to cross between parts.
Inputs may be any that keep to these rules, and one draw needn't show every extreme that they name: state_dev and state_slot together name every pair of a cache index and a slot exactly once.
All inputs are finite; a program needn't handle non-finite values.
Results may differ from a plain program's by a relative error of at most 0.0075.
Values may be sent and summed in bfloat16 or wider, within the bound.
No kernel may reach another device: no remote copies, remote signals or barrier semaphores. Data moves between devices by JAX's collectives and lax.ppermute only.
A program may use at most 128 MiB of HBM per device.

v0:
```python
import jax
import jax.numpy as jnp
from jax import lax
from jax.sharding import PartitionSpec as P

HEADS = 128
HEAD_DIM = 64
GROUPS = 8
SPAN = 128


EPS = 1e-05


def span_scan(x_heads, step_size, b_group, c_group, decay_scale, skip_here, initial):
    requests, length, heads_here = step_size.shape
    blocks = length // SPAN
    head_channel_width = x_heads.shape[2] // heads_here
    x_blocks = x_heads.reshape(requests, blocks, SPAN, heads_here, head_channel_width)
    step_blocks = step_size.reshape(requests, blocks, SPAN, heads_here).transpose(0, 1, 3, 2)
    cum_rate = jnp.cumsum(-decay_scale[:, None] * step_blocks, axis=3)
    b_blocks = b_group.reshape(requests, blocks, SPAN, -1)
    c_blocks = c_group.reshape(requests, blocks, SPAN, -1)
    scores = jnp.einsum("mkin,mkjn->mkij", c_blocks, b_blocks, preferred_element_type=jnp.float32)
    causal = jnp.arange(SPAN)[:, None] >= jnp.arange(SPAN)[None, :]
    spread = cum_rate[..., :, None] - cum_rate[..., None, :]
    decay_mask = jnp.where(causal, jnp.exp(jnp.where(causal, spread, 0.0)), 0.0)
    blend_factors = (scores[:, :, None] * decay_mask * step_blocks[..., None, :]).astype(
        jnp.bfloat16
    )
    diagonal = jnp.einsum(
        "mkhij,mkjhp->mkihp", blend_factors, x_blocks, preferred_element_type=jnp.float32
    )
    weight = jnp.exp(cum_rate[..., -1:] - cum_rate) * step_blocks
    scaled = (b_blocks.astype(jnp.float32)[:, :, None] * weight[..., None]).astype(jnp.bfloat16)
    block_states = jnp.einsum(
        "mkjhp,mkhjn->mkhpn", x_blocks, scaled, preferred_element_type=jnp.float32
    )
    running_totals = cum_rate[..., -1]

    def advance(carried, step_inputs):
        block_total, new_state = step_inputs
        return (jnp.exp(block_total)[..., None, None] * carried + new_state, carried)

    final_state, before = lax.scan(
        advance, initial, (jnp.moveaxis(running_totals, 1, 0), jnp.moveaxis(block_states, 1, 0))
    )
    c_float = c_blocks.astype(jnp.float32)
    carried_in = jnp.einsum("mkin,kmhpn->mkihp", c_float, before, precision=lax.Precision.HIGHEST)
    growth = jnp.exp(cum_rate).transpose(0, 1, 3, 2)[..., None]
    combined = diagonal + carried_in * growth + skip_here[:, None] * x_blocks.astype(jnp.float32)
    return (combined, final_state, c_float, cum_rate, running_totals)


def fetch_parents(cache_states, own_slot, owner_dev):
    owned = owner_dev == lax.axis_index("cache")
    owned_terms = jnp.where(owned[:, None, None, None, None], cache_states[own_slot], 0.0)
    parent_share = lax.psum_scatter(
        owned_terms.astype(jnp.bfloat16), "cache", scatter_dimension=1, tiled=True
    ).astype(jnp.float32)
    return parent_share[:, 0]


def shards(
    x_in,
    z_in,
    b_in,
    c_in,
    dt_in,
    dt_bias,
    a_log,
    skip_gain,
    norm_w,
    cache_states,
    parent,
    state_dev,
    state_slot,
    spans,
):
    token_order = lax.axis_index("tok")
    replica_order = lax.axis_index("rep")
    tok_count = lax.axis_size("tok")
    requests, segment, channel_count = x_in.shape
    heads_here = dt_in.shape[2] // tok_count
    length = segment * tok_count
    x_heads, step_raw = (
        lax.all_to_all(x_in, "tok", split_axis=2, concat_axis=1, tiled=True),
        lax.all_to_all(dt_in, "tok", split_axis=2, concat_axis=1, tiled=True),
    )
    b_full, c_full = (
        lax.all_gather(b_in, "tok", axis=1, tiled=True),
        lax.all_gather(c_in, "tok", axis=1, tiled=True),
    )
    group_pick = token_order * heads_here // (HEADS // GROUPS)
    b_group = lax.dynamic_index_in_dim(b_full, group_pick, axis=2, keepdims=False)
    c_group = lax.dynamic_index_in_dim(c_full, group_pick, axis=2, keepdims=False)
    first_head = token_order * heads_here
    bias_here = lax.dynamic_slice_in_dim(dt_bias, first_head, heads_here)
    decay_scale = jnp.exp(lax.dynamic_slice_in_dim(a_log, first_head, heads_here))
    skip_here = lax.dynamic_slice_in_dim(skip_gain, first_head, heads_here)
    parent_here = lax.dynamic_slice_in_dim(parent, replica_order * requests, requests)
    span_here = lax.dynamic_slice_in_dim(spans, replica_order * requests, requests)
    valid_mask = (jnp.arange(length)[None, :] < span_here[:, None] * SPAN).astype(jnp.float32)
    step_size = jax.nn.softplus(step_raw.astype(jnp.float32) + bias_here) * valid_mask[..., None]
    slot_count = cache_states.shape[0]
    id_match = parent_here[:, None] == jnp.arange(state_dev.shape[0])[None, :]
    holder_row = jnp.sum(
        jnp.where(id_match, state_dev[None, :] * slot_count + state_slot[None, :], 0), axis=1
    )
    owner_dev = holder_row // slot_count
    own_slot = holder_row % slot_count
    initial = fetch_parents(cache_states, own_slot, owner_dev)
    combined, final_state, c_float, cum_rate, running_totals = span_scan(
        x_heads, step_size, b_group, c_group, decay_scale, skip_here, initial
    )
    ssd = combined.astype(jnp.bfloat16).reshape(requests, length, -1)
    returned = lax.all_to_all(ssd, "tok", split_axis=1, concat_axis=2, tiled=True)
    gated = returned.astype(jnp.float32) * jax.nn.silu(z_in.astype(jnp.float32))
    group_width = HEADS * HEAD_DIM // GROUPS
    grouped = gated.reshape(requests, segment, channel_count // group_width, group_width)
    inverse_rms = lax.rsqrt(jnp.mean(grouped * grouped, axis=-1, keepdims=True) + EPS)
    valid_here = lax.dynamic_slice_in_dim(valid_mask, token_order * segment, segment, 1)
    result = (
        (grouped * inverse_rms).reshape(requests, segment, channel_count)
        * norm_w
        * valid_here[..., None]
    )
    return (result.astype(jnp.bfloat16), final_state)


def solution(mesh):
    placed = (
        P(("groups", "rep"), "tok", "cache"),
        P(("groups", "rep"), "tok", "cache"),
        P(("groups", "rep"), "tok", "cache", None),
        P(("groups", "rep"), "tok", "cache", None),
        P(("groups", "rep"), "tok", "cache"),
        P("cache"),
        P("cache"),
        P("cache"),
        P("cache"),
        P(("groups", "cache"), None, "tok", None, None),
        P("groups"),
        P("groups"),
        P("groups"),
        P("groups"),
    )
    return jax.shard_map(
        shards,
        mesh=mesh,
        in_specs=placed,
        out_specs=(
            P(("groups", "rep"), "tok", "cache"),
            P(("groups", "rep"), ("cache", "tok"), None, None),
        ),
        check_vma=False,
    )
```

profile of v0, /device:TPU:16, one launch (start us, length us, event | category | flops | bytes accessed | tf_op | source)
XLA Modules:
  0.0 396.7 jit_solution(4447523708625058947)
XLA Ops:
  8.1 0.9 dynamic_slice.38
  9.0 0.7 multiply_add_fusion.1
  9.9 2.1 gather_fusion
  12.0 3.7 select_convert_fusion
  15.8 0.9 copy.70
  16.7 0.7 copy.71
  17.4 5.2 %all-to-all-start = ((bf16[4,128,64]{1,0,2:T(4,128)(2,1)}), bf16[4,128,64]{1,0,2:T(4,128)(2,1)S(1)}, u32[]{:S(2)}, u32[]{:S(2)}) async-start(bf16[4,128,64]{1,0,2:T(4,128)(2,1)} %copy.71), calls=%async_computation | async-start | bytes 131072 | tf_op jit(solution)/shard_map/all_to_all | solution.py:88
  22.6 7.7 %copy.73 = bf16[4,128,4096]{1,0,2:T(4,128)(2,1)} copy(bf16[4,128,4096]{2,1,0:T(8,128)(2,1)} %param.16) | data formatting | bytes 8388608 | tf_op args[0]
  30.3 5.1 %all-to-all-start.1 = ((bf16[4,128,4096]{1,0,2:T(4,128)(2,1)}), bf16[4,128,4096]{1,0,2:T(4,128)(2,1)}, u32[]{:S(2)}, u32[]{:S(2)}) async-start(bf16[4,128,4096]{1,0,2:T(4,128)(2,1)} %copy.73), calls=%async_computation.1 | async-start | bytes 8388608 | tf_op jit(solution)/shard_map/all_to_all | solution.py:87
  35.4 0.9 copy.69
  37.3 0.6 iota_compare_fusion
  38.1 4.6 %reduce_window_sum.11 = f32[4,4,16,128]{3,2,1,0:T(8,128)S(1)} reduce-window(f32[4,4,16,128]{3,2,1,0:T(8,128)S(1)} %broadcast_multiply_fusion, f32[]{:T(128)} %constant.90.clone.1), window={size=1x1x1x128 pad=0_0x0_0x0_0x127_0}, to_apply=%region_0.1 | reduce-window | flops 4161536 | bytes 262148 | tf_op jit(solution)/shard_map/jit(cumsum)/reduce_window_sum | solution.py:21
  42.9 0.8 exponential_bitcast_fusion.1
  43.7 36.1 %all-reduce.3.cloned.1.call-done = bf16[4,2,16,64,128]{4,3,2,1,0:T(8,128)(2,1)} async-done(((bf16[4,2,16,64,128]{4,3,2,1,0:T(8,128)(2,1)}), bf16[4,2,16,64,128]{4,3,2,1,0:T(8,128)(2,1)}) %all-reduce.3.cloned.1.call-update) | async-done | bytes 2097168
  79.9 2.0 bitcast_convert_fusion
  81.9 15.1 %all-gather.5.cloned.1.call-done = bf16[4,512,4,128]{3,1,0,2:T(8,128)(2,1)} async-done(((bf16[4,128,4,128]{3,1,0,2:T(8,128)(2,1)}), bf16[4,512,4,128]{3,1,0,2:T(8,128)(2,1)}) %all-gather.5.cloned.1.call-update) | async-done | bytes 2097168 | tf_op jit(solution)/shard_map/all_gather | solution.py:91
  97.0 1.1 constant_dynamic-slice_fusion.1
  98.1 1.1 convert_element_type.65
  99.2 81.0 %all-gather.3.cloned.1.call-done = bf16[4,512,4,128]{3,1,0,2:T(8,128)(2,1)} async-done(((bf16[4,128,4,128]{3,1,0,2:T(8,128)(2,1)}), bf16[4,512,4,128]{3,1,0,2:T(8,128)(2,1)}) %all-gather.3.cloned.1.call-update) | async-done | bytes 2097168 | tf_op jit(solution)/shard_map/all_gather | solution.py:92
  180.2 1.1 constant_dynamic-slice_fusion.2
  181.3 1.5 fusion.33
  182.8 2.2 all-to-all-done.1
  185.0 3.1 copy.74
  188.1 2.0 copy-done.5
  190.1 8.1 %fusion.19 = f32[4,4,16,64,128]{4,3,2,0,1:T(8,128)} fusion(bf16[4,4,128,16,64]{2,4,3,1,0:T(8,128)(2,1)S(1)} %bitcast.111, f32[4,4,16,128]{3,2,1,0:T(8,128)S(1)} %get-tuple-element.81, f32[4,4,128,128]{3,2,1,0:T(8,128)S(1)} %copy-done.7), kind=kOutput, calls=%fused_computation.33 | convolution fusion | flops 545259520 | bytes 13762560 | tf_op jit(solution)/shard_map/mkjhp,mkhjn->mkhpn/dot_general | solution.py:36
  198.2 14.2 %while.12 = (s32[]{:T(128)}, f32[4,16,64,128]{3,2,1,0:T(8,128)S(1)}, f32[4,4,16,64,128]{4,3,2,0,1:T(8,128)}, f32[4,4,16]{2,0,1:T(4,128)S(1)}, f32[4,4,16,64,128]{4,3,2,0,1:T(8,128)}, /*index=5*/s32[]{:T(128)}) while((s32[]{:T(128)}, f32[4,16,64,128]{3,2,1,0:T(8,128)S(1)}, f32[4,4,16,64,128]{4,3,2,0,1:T(8,128)}, f32[4,4,16]{2,0,1:T(4,128)S(1)}, ...), condition=%wide.region_4.5_spmd, body=%wide.region_3.4_spmd.sunk | while | flops 1048578 | bytes 10487629 | solution.py:45
  198.2 1.5 bitcast_dynamic-update-slice_fusion.2
  199.8 2.0 bitcast_add_fusion.3
  201.7 1.5 bitcast_dynamic-update-slice_fusion.2
  203.3 2.0 bitcast_add_fusion.3
  205.3 1.5 bitcast_dynamic-update-slice_fusion.2
  206.9 2.0 bitcast_add_fusion.3
  208.9 1.6 bitcast_dynamic-update-slice_fusion.2
  210.5 2.0 bitcast_add_fusion.3
  212.5 7.2 %fusion.34 = f32[4,4,128,16,64]{2,4,3,1,0:T(8,128)S(1)} fusion(bf16[4,4,128,128,1]{3,2,4,1,0:T(8,128)(2,1)S(1)} %bitcast.114, f32[4,4,16,64,128]{4,3,2,0,1:T(8,128)} %get-tuple-element.30), kind=kOutput, calls=%fused_computation.76 | convolution fusion | flops 3221225472 | bytes 17301504 | tf_op jit(solution)/shard_map/mkin,kmhpn->mkihp/dot_general | solution.py:49
  219.8 9.1 %fusion.10 = bf16[4,4,128,16,64]{2,4,3,1,0:T(8,128)(2,1)} fusion(bf16[4,4,128,16,64]{2,4,3,1,0:T(8,128)(2,1)S(1)} %bitcast.112, f32[4,4,128,16,64]{2,4,3,1,0:T(8,128)S(1)} %fusion.34, f32[16]{0:T(128)S(1)} %dynamic_slice.39, f32[4,4,128,16]{2,3,1,0:T(8,128)S(1)} %get-tuple-element.80, f32[4,4,16,128]{3,2,1,0:T(8,128)S(1)} %copy-done.11, ...), kind=kOutput, calls=%fused_computation.23 | convolution fusion | flops 574619648 | bytes 18235456 | tf_op jit(solution)/shard_map/mkhij,mkjhp->mkihp/dot_general | solution.py:31
  228.9 13.0 %copy.85 = bf16[4,4,128,16,64]{4,3,0,2,1:T(8,128)(2,1)} copy(bf16[4,4,128,16,64]{2,4,3,1,0:T(8,128)(2,1)} %fusion.10) | data formatting | bytes 8388608 | tf_op jit(solution)/shard_map/reshape | solution.py:116
  241.9 12.8 %reshape.172 = bf16[4,512,1024]{2,0,1:T(4,128)(2,1)} reshape(bf16[4,4,128,16,64]{4,3,0,2,1:T(8,128)(2,1)} %copy.85) | data formatting | bytes 8388608 | tf_op jit(solution)/shard_map/reshape | solution.py:116
  254.7 8.2 %all-to-all-start.2 = ((bf16[4,512,1024]{2,0,1:T(4,128)(2,1)}), bf16[4,512,1024]{2,0,1:T(4,128)(2,1)}, u32[]{:S(2)}, u32[]{:S(2)}) async-start(bf16[4,512,1024]{2,0,1:T(4,128)(2,1)} %reshape.172), calls=%async_computation.2 | async-start | bytes 8388608 | tf_op jit(solution)/shard_map/all_to_all | solution.py:117
  262.9 6.3 %copy.82 = bf16[4,128,4096]{1,2,0:T(8,128)(2,1)} copy(bf16[4,128,4096]{2,1,0:T(8,128)(2,1)} %param.17) | data formatting | bytes 8388608 | tf_op args[1]
  269.3 83.7 %all-to-all-done.2 = bf16[4,512,1024]{2,0,1:T(4,128)(2,1)} async-done(((bf16[4,512,1024]{2,0,1:T(4,128)(2,1)}), bf16[4,512,1024]{2,0,1:T(4,128)(2,1)}, u32[]{:S(2)}, u32[]{:S(2)}) %all-to-all-start.2) | async-done | bytes 4194336 | tf_op jit(solution)/shard_map/all_to_all | solution.py:117
  353.0 3.6 copy.80
  356.5 4.3 %convert_bitcast_fusion = f32[4,128,4,1024]{3,1,2,0:T(8,128)} fusion(bf16[4,4,128,1024]{3,2,1,0:T(8,128)(2,1)S(1)} %bitcast.110), kind=kLoop, calls=%fused_computation.15 | loop fusion | flops 2097152 | bytes 12582912 | tf_op jit(solution)/shard_map/convert_element_type | solution.py:118
  360.9 8.7 %copy.81 = f32[4,128,4,1024]{1,3,2,0:T(8,128)} copy(f32[4,128,4,1024]{3,1,2,0:T(8,128)} %convert_bitcast_fusion) | data formatting | bytes 16777216 | tf_op jit(solution)/shard_map/convert_element_type | solution.py:118
  369.6 7.2 %bitcast_reduce_fusion = f32[4,128,4]{1,2,0:T(4,128)S(1)} fusion(bf16[4,128,4096]{1,2,0:T(8,128)(2,1)} %copy.82, f32[4,128,4,1024]{1,3,2,0:T(8,128)} %copy.81), kind=kLoop, calls=%fused_computation.20 | loop fusion | flops 16775168 | bytes 12591104 | tf_op jit(solution)/shard_map/reduce_sum | solution.py:121
  376.8 1.0 copy-done.4
  377.8 5.1 %fusion.8 = bf16[4,128,4096]{1,2,0:T(8,128)(2,1)} fusion(f32[4,128]{1,0:T(4,128)S(1)} %fusion.28, f32[4096]{0:T(1024)S(1)} %copy-done.13, f32[4,128,4]{1,2,0:T(4,128)S(1)} %add_rsqrt_fusion, bf16[4,128,4096]{1,2,0:T(8,128)(2,1)S(1)} %copy-done.4, f32[4,128,4,1024]{1,3,2,0:T(8,128)S(1)} %copy-done.3), kind=kLoop, calls=%fused_computation.19 | loop fusion | flops 20971520 | bytes 16803840 | tf_op jit(solution)/shard_map/convert_element_type | solution.py:128
  382.9 6.3 %copy.83 = bf16[4,128,4096]{2,1,0:T(8,128)(2,1)} copy(bf16[4,128,4096]{1,2,0:T(8,128)(2,1)} %fusion.8) | data formatting | bytes 8388608
  (70 shorter events, 1.9 us)
Async XLA Ops:
  8.0 1.9 copy-start
  8.0 7.8 %copy-start.9 = (bf16[4,128,4,128]{3,2,1,0:T(4,128)(2,1)S(1)}, bf16[4,128,4,128]{3,2,1,0:T(4,128)(2,1)}, u32[]{:S(2)}) copy-start(bf16[4,128,4,128]{3,2,1,0:T(4,128)(2,1)} %param.18) | copy-start | bytes 1572868
  8.0 8.7 %copy-start.12 = (bf16[4,128,64]{1,2,0:T(8,128)(2,1)S(1)}, bf16[4,128,64]{1,2,0:T(8,128)(2,1)}, u32[]{:S(2)}) copy-start(bf16[4,128,64]{1,2,0:T(8,128)(2,1)} %param.20) | copy-start | bytes 196612
  8.0 71.9 %all-reduce.3.cloned.1.call-start = ((), (), s32[]{:S(2)}) async-start(), calls=%async_computation.5 | async-start | bytes 4194304
  15.7 81.3 %all-gather.5.cloned.1.call-start = ((), (), s32[]{:S(2)}) async-start(), calls=%async_computation.4 | async-start | bytes 2621440 | tf_op jit(solution)/shard_map/all_gather | solution.py:91
  17.4 12.9 %all-to-all-start = ((bf16[4,128,64]{1,0,2:T(4,128)(2,1)}), bf16[4,128,64]{1,0,2:T(4,128)(2,1)S(1)}, u32[]{:S(2)}, u32[]{:S(2)}) async-start(bf16[4,128,64]{1,0,2:T(4,128)(2,1)} %copy.71), calls=%async_computation | async-start | bytes 131072 | tf_op jit(solution)/shard_map/all_to_all | solution.py:88
  22.6 12.8 %copy-start.10 = (bf16[4,128,4,128]{3,2,1,0:T(4,128)(2,1)S(1)}, bf16[4,128,4,128]{3,2,1,0:T(4,128)(2,1)}, u32[]{:S(2)}) copy-start(bf16[4,128,4,128]{3,2,1,0:T(4,128)(2,1)} %param.19) | copy-start | bytes 1572868
  22.6 13.7 %copy-start.15 = (f32[64]{0:T(128)S(1)}, f32[64]{0:T(128)}, u32[]{:S(2)}) copy-start(f32[64]{0:T(128)} %param.21) | copy-start | bytes 772
  22.6 13.8 %copy-start.16 = (f32[64]{0:T(128)S(1)}, f32[64]{0:T(128)}, u32[]{:S(2)}) copy-start(f32[64]{0:T(128)} %param.23) | copy-start | bytes 772
  22.6 13.9 %copy-start.19 = (u32[32]{0:T(128)S(1)}, u32[32]{0:T(128)}, u32[]{:S(2)}) copy-start(u32[32]{0:T(128)} %constant.102) | copy-start | bytes 388
  22.6 14.5 %copy-start.17 = (f32[64]{0:T(128)S(1)}, f32[64]{0:T(128)}, u32[]{:S(2)}) copy-start(f32[64]{0:T(128)} %param.22) | copy-start | bytes 772
  22.6 14.6 %copy-start.18 = (s32[8]{0:T(128)S(1)}, s32[8]{0:T(128)}, u32[]{:S(2)}) copy-start(s32[8]{0:T(128)} %param.29) | copy-start | bytes 100
  30.3 154.7 %all-to-all-start.1 = ((bf16[4,128,4096]{1,0,2:T(4,128)(2,1)}), bf16[4,128,4096]{1,0,2:T(4,128)(2,1)}, u32[]{:S(2)}, u32[]{:S(2)}) async-start(bf16[4,128,4096]{1,0,2:T(4,128)(2,1)} %copy.73), calls=%async_computation.1 | async-start | bytes 8388608 | tf_op jit(solution)/shard_map/all_to_all | solution.py:87
  35.4 144.8 %all-gather.3.cloned.1.call-start = ((), (), s32[]{:S(2)}) async-start(), calls=%async_computation.3 | async-start | bytes 2621440 | tf_op jit(solution)/shard_map/all_gather | solution.py:92
  185.0 5.1 %copy-start.7 = (f32[4,4,128,128]{3,2,1,0:T(8,128)S(1)}, f32[4,4,128,128]{3,2,1,0:T(8,128)}, u32[]{:S(2)}) copy-start(f32[4,4,128,128]{3,2,1,0:T(8,128)} %convert_element_type.65) | copy-start | bytes 3145732
  188.0 2.0 copy-start.5
  212.4 7.3 %copy-start.2 = (f32[4,16,64,128]{3,2,1,0:T(8,128)}, f32[4,16,64,128]{3,2,1,0:T(8,128)S(1)}, u32[]{:S(2)}) copy-start(f32[4,16,64,128]{3,2,1,0:T(8,128)S(1)} %get-tuple-element.69) | copy-start | bytes 6291460
  212.5 7.3 %copy-start.6 = (bf16[4,128,4,1024]{1,3,2,0:T(8,128)(2,1)S(1)}, bf16[4,128,4,1024]{1,3,2,0:T(8,128)(2,1)}, u32[]{:S(2)}) copy-start(bf16[4,128,4,1024]{1,3,2,0:T(8,128)(2,1)} %copy-done.5) | copy-start | bytes 12582916
  212.5 7.3 %copy-start.8 = (f32[4,4,128,128]{3,2,1,0:T(8,128)S(1)}, f32[4,4,128,128]{3,2,1,0:T(8,128)}, u32[]{:S(2)}) copy-start(f32[4,4,128,128]{3,2,1,0:T(8,128)} %fusion.33) | copy-start | bytes 3145732
  212.5 7.3 %copy-start.11 = (f32[4,4,16,128]{3,2,1,0:T(8,128)S(1)}, f32[4,4,16,128]{3,2,1,0:T(8,128)}, u32[]{:S(2)}) copy-start(f32[4,4,16,128]{3,2,1,0:T(8,128)} %get-tuple-element.82) | copy-start | bytes 393220
  212.5 7.3 %copy-start.14 = (pred[128,128]{1,0:T(8,128)(4,1)S(1)}, pred[128,128]{1,0:T(8,128)(4,1)}, u32[]{:S(2)}) copy-start(pred[128,128]{1,0:T(8,128)(4,1)} %iota_compare_fusion) | copy-start | bytes 49156
  254.7 98.3 %all-to-all-start.2 = ((bf16[4,512,1024]{2,0,1:T(4,128)(2,1)}), bf16[4,512,1024]{2,0,1:T(4,128)(2,1)}, u32[]{:S(2)}, u32[]{:S(2)}) async-start(bf16[4,512,1024]{2,0,1:T(4,128)(2,1)} %reshape.172), calls=%async_computation.2 | async-start | bytes 8388608 | tf_op jit(solution)/shard_map/all_to_all | solution.py:117
  369.6 7.2 %copy-start.3 = (f32[4,128,4,1024]{1,3,2,0:T(8,128)S(1)}, f32[4,128,4,1024]{1,3,2,0:T(8,128)}, u32[]{:S(2)}) copy-start(f32[4,128,4,1024]{1,3,2,0:T(8,128)} %copy.81) | copy-start | bytes 25165828
  369.6 8.2 %copy-start.4 = (bf16[4,128,4096]{1,2,0:T(8,128)(2,1)S(1)}, bf16[4,128,4096]{1,2,0:T(8,128)(2,1)}, u32[]{:S(2)}) copy-start(bf16[4,128,4096]{1,2,0:T(8,128)(2,1)} %copy.82) | copy-start | bytes 12582916
  369.6 8.2 %copy-start.13 = (f32[4096]{0:T(1024)S(1)}, f32[4096]{0:T(1024)}, u32[]{:S(2)}) copy-start(f32[4096]{0:T(1024)} %param.24) | copy-start | bytes 49156
  377.8 11.5 %copy-start.1 = (f32[2,2,16,64,128]{4,3,2,1,0:T(8,128)S(1)}, f32[2,2,16,64,128]{4,3,2,1,0:T(8,128)}, u32[]{:S(2)}) copy-start(f32[2,2,16,64,128]{4,3,2,1,0:T(8,128)} %param.25) | copy-start | bytes 6291460
Sparse Core Ops, SparseCore 0:
  15.8 64.0 all-reduce.2
Sparse Core Ops, SparseCore 1:
  17.8 79.2 all-gather.4
  98.5 81.7 all-gather.2
where the time goes:
time: 403 us; the launch traced here: 397 us
  waiting for transfers between devices  218 us (54%)
  local copies, waits for them, and re-layouts  79.3 us (20%)
  other arithmetic  38.7 us (10%)
  matrix products  26 us (6%)
  starting transfers between devices  18.6 us (5%)
  between operations  15.8 us (4%)
    all_to_all x1, waiting for transfers between devices, shards(): lax.all_to_all(ssd, 'tok', split_axis=1, concat_axis=2, tiled=True)  83.7 us
    all_gather x1, waiting for transfers between devices, shards(): lax.all_gather(c_in, 'tok', axis=1, tiled=True)  81 us
    unnamed x4, waiting for transfers between devices  36.2 us
    unnamed x47, local copies, waits for them, and re-layouts  26.5 us
    reshape x2, local copies, waits for them, and re-layouts, shards(): ssd = combined.astype(jnp.bfloat16).reshape(requests, length, -1)  25.8 us
    all_gather x1, waiting for transfers between devices, shards(): lax.all_gather(b_in, 'tok', axis=1, tiled=True)  15.1 us
    dot_general x1, matrix products, span_scan(): jnp.einsum('mkhij,mkjhp->mkihp', blend_factors, x_blocks, preferred_eleme...  9.13 us
    convert_element_type x1, local copies, waits for them, and re-layouts, shards(): gated = returned.astype(jnp.float32) * jax.nn.silu(z_in.astype(jnp.float32))  8.71 us
  transfers between devices with their start and end apart: 6, of which 5 were waited for; matrix products, arithmetic and copies ran while one was open for 8% of the time, Pallas kernels for 0%

commit v1 on v0

v1 whole, which is shorter than its diff:
```python
import functools

import jax
import jax.numpy as jnp
from jax import lax
from jax.experimental import pallas as pl
from jax.experimental.pallas import tpu as pltpu
from jax.sharding import PartitionSpec as P

HEADS = 128
HEAD_DIM = 64
GROUPS = 8
STATE = 128
SPAN = 128
EPS = 1e-05

PER_GROUP = HEADS // GROUPS
GROUP_LANES = PER_GROUP * HEAD_DIM
PAIR_LANES = 2 * HEAD_DIM
PAIRS = PER_GROUP // 2
REQ_CHUNK = 2
HOP = 2

F32 = jnp.float32
BF16 = jnp.bfloat16


def cost(flops, nbytes, trans=0):
    return pl.CostEstimate(flops=flops, bytes_accessed=nbytes, transcendentals=trans)


def low_half(rows):
    return lax.broadcasted_iota(jnp.int32, (rows, PAIR_LANES), 1) < HEAD_DIM


def spread_pair(values, q, low):
    return jnp.where(low, values[:, 2 * q : 2 * q + 1], values[:, 2 * q + 1 : 2 * q + 2])


def prep_body(valid_ref, dt_ref, bias_ref, alog_ref, cum_ref, cum_t_ref, step_t_ref, weight_ref, growth_ref, total_ref):
    requests, span, heads_here = dt_ref.shape
    rows = lax.broadcasted_iota(jnp.int32, (span, span), 0)
    cols = lax.broadcasted_iota(jnp.int32, (span, span), 1)
    lower = (rows >= cols).astype(F32)
    rate = -jnp.exp(alog_ref[...])
    for r in range(requests):
        raw = dt_ref[r].astype(F32) + bias_ref[...]
        positive = jnp.maximum(raw, 0.0) + jnp.log1p(jnp.exp(-jnp.abs(raw)))
        step = positive * valid_ref[r].astype(F32)
        cum = jnp.dot(lower, rate * step, precision=lax.Precision.HIGHEST, preferred_element_type=F32)
        total = cum[span - 1 : span, :]
        weight = jnp.exp(total - cum) * step
        growth = jnp.exp(cum)
        total_ref[r] = total
        cum_t = cum.T
        step_t = step.T
        for g in range(heads_here // PER_GROUP):
            here = slice(g * PER_GROUP, (g + 1) * PER_GROUP)
            cum_ref[r, g] = cum[:, here]
            weight_ref[r, g] = weight[:, here]
            growth_ref[r, g] = growth[:, here]
            cum_t_ref[r, g] = cum_t[here, :]
            step_t_ref[r, g] = step_t[here, :]


def prepare(valid, dt_in, bias, a_log):
    requests, span, heads_here = dt_in.shape
    groups = heads_here // PER_GROUP
    columns = jax.ShapeDtypeStruct((requests, groups, span, PER_GROUP), F32)
    as_rows = jax.ShapeDtypeStruct((requests, groups, PER_GROUP, span), F32)
    vmem = pl.BlockSpec(memory_space=pltpu.VMEM)
    return pl.pallas_call(
        prep_body,
        out_shape=(columns, as_rows, as_rows, columns, columns, jax.ShapeDtypeStruct((requests, 1, heads_here), F32)),
        in_specs=[pl.BlockSpec(memory_space=pltpu.SMEM), vmem, vmem, vmem],
        out_specs=(vmem,) * 6,
        cost_estimate=cost(20_000_000, 4_000_000),
        name="prep",
    )(valid, dt_in, bias, a_log)


def block_body(x_ref, b_ref, weight_ref, out_ref):
    weight = weight_ref[...].reshape(weight_ref.shape[-2:])
    low = low_half(weight.shape[0])
    scaled = []
    for q in range(PAIRS):
        lanes = slice(q * PAIR_LANES, (q + 1) * PAIR_LANES)
        scaled.append((x_ref[0, :, lanes].astype(F32) * spread_pair(weight, q, low)).astype(BF16))
    scaled = jnp.concatenate(scaled, axis=1)
    states = lax.dot_general(b_ref[0], scaled, (((0,), (0,)), ((), ())), preferred_element_type=F32)
    out_ref[...] = states.astype(BF16).reshape(out_ref.shape)


def block_states(x_in, b_flat, weight):
    requests, span, width = x_in.shape
    groups = width // GROUP_LANES
    parts = requests // REQ_CHUNK

    def at(i, j):
        return ((i % parts) * REQ_CHUNK + j, (i // parts + 1) % groups)

    return pl.pallas_call(
        block_body,
        grid=(groups * parts, REQ_CHUNK),
        out_shape=jax.ShapeDtypeStruct((groups * parts, REQ_CHUNK, STATE, GROUP_LANES), BF16),
        in_specs=[
            pl.BlockSpec((1, span, GROUP_LANES), lambda i, j: (at(i, j)[0], 0, at(i, j)[1])),
            pl.BlockSpec((1, span, STATE), lambda i, j: (at(i, j)[0], 0, at(i, j)[1])),
            pl.BlockSpec((1, 1, span, PER_GROUP), lambda i, j: (at(i, j)[0], at(i, j)[1], 0, 0)),
        ],
        out_specs=pl.BlockSpec((1, 1, STATE, GROUP_LANES), lambda i, j: (i, j, 0, 0)),
        cost_estimate=cost(600_000_000, 12_000_000),
        name="block_states",
    )(x_in, b_flat, weight)


def local_body(valid_ref, x_ref, b_ref, c_ref, cum_ref, cum_t_ref, step_t_ref, skip_ref, out_ref):
    span = x_ref.shape[1]

    @pl.when(valid_ref[pl.program_id(0)] > 0)
    def _():
        rows = lax.broadcasted_iota(jnp.int32, (span, span), 0)
        cols = lax.broadcasted_iota(jnp.int32, (span, span), 1)
        causal = rows >= cols
        low = low_half(span)
        scores = lax.dot_general(c_ref[0], b_ref[0], (((1,), (1,)), ((), ())), preferred_element_type=F32)
        cum = cum_ref[0, 0]
        cum_t = cum_t_ref[0, 0]
        step_t = step_t_ref[0, 0]

        def mix(h):
            spread = cum[:, h : h + 1] - cum_t[h : h + 1, :]
            decay = jnp.exp(jnp.where(causal, spread, -jnp.inf))
            return (scores * decay * step_t[h : h + 1, :]).astype(BF16)

        for q in range(PAIRS):
            lanes = slice(q * PAIR_LANES, (q + 1) * PAIR_LANES)
            x_pair = x_ref[0, :, lanes]
            nothing = jnp.zeros_like(x_pair)
            both = jnp.concatenate([jnp.where(low, x_pair, nothing), jnp.where(low, nothing, x_pair)], axis=0)
            blend = jnp.concatenate([mix(2 * q), mix(2 * q + 1)], axis=1)
            diagonal = jnp.dot(blend, both, preferred_element_type=F32)
            out_ref[0, :, lanes] = diagonal + skip_ref[:, lanes] * x_pair.astype(F32)


def local_part(g, valid, x_in, b_flat, c_flat, cum, cum_t, step_t, skip_lanes):
    requests, span, _ = x_in.shape
    column = pl.BlockSpec((1, 1, span, PER_GROUP), lambda r, v: (r, g, 0, 0))
    as_row = pl.BlockSpec((1, 1, PER_GROUP, span), lambda r, v: (r, g, 0, 0))
    return pl.pallas_call(
        local_body,
        grid_spec=pltpu.PrefetchScalarGridSpec(
            num_scalar_prefetch=1,
            grid=(requests,),
            in_specs=[
                pl.BlockSpec((1, span, GROUP_LANES), lambda r, v: (r, 0, g)),
                pl.BlockSpec((1, span, STATE), lambda r, v: (r, 0, g)),
                pl.BlockSpec((1, span, STATE), lambda r, v: (r, 0, g)),
                column,
                as_row,
                as_row,
                pl.BlockSpec((1, GROUP_LANES), lambda r, v: (0, g)),
            ],
            out_specs=pl.BlockSpec((1, span, GROUP_LANES), lambda r, v: (r, 0, 0)),
        ),
        out_shape=jax.ShapeDtypeStruct((requests, span, GROUP_LANES), F32),
        cost_estimate=cost(1_000_000_000, 10_000_000),
        name="local_part",
    )(valid, x_in, b_flat, c_flat, cum, cum_t, step_t, skip_lanes)


def out_body(
    ahead_of, init_of, unit_lanes, group, part, scalars, local_ref, c_ref, growth_ref, z_ref, gain_ref, before_ref, *refs
):
    n_ahead = len({i for i in ahead_of if i is not None})
    n_init = len({i for i in init_of if i is not None})
    ahead_refs, init_refs = refs[:n_ahead], refs[n_ahead : n_ahead + n_init]
    out_ref, ahead_buf, init_buf, sems = refs[-4:]
    me = scalars[0]
    i = pl.program_id(0)
    span = local_ref.shape[1]

    @pl.when(i == 0)
    def _():
        for device in range(len(ahead_of)):

            @pl.when(me == device)
            def _(device=device):
                copies = []
                if ahead_of[device] is None:
                    ahead_buf[...] = jnp.zeros_like(ahead_buf)
                else:
                    copies.append(pltpu.make_async_copy(ahead_refs[ahead_of[device]], ahead_buf, sems.at[0]))
                if init_of[device] is None:
                    init_buf[...] = jnp.zeros_like(init_buf)
                else:
                    source = init_refs[init_of[device]].at[pl.ds(part * REQ_CHUNK, REQ_CHUNK)]
                    copies.append(pltpu.make_async_copy(source, init_buf, sems.at[1]))
                for copy in copies:
                    copy.start()
                for copy in copies:
                    copy.wait()

    valid = scalars[1 + part * REQ_CHUNK + i]

    @pl.when(valid == 0)
    def _():
        out_ref[...] = jnp.zeros_like(out_ref)

    @pl.when(valid > 0)
    def _():
        low = low_half(span)
        started = before_ref[0] * init_buf[i].astype(F32)
        lane = lax.broadcasted_iota(jnp.int32, (1, GROUP_LANES), 1) + group * GROUP_LANES
        started = jnp.where(lane >= me * unit_lanes, started, 0.0)
        state = (ahead_buf[i].astype(F32) + started).astype(BF16)
        carried = jnp.dot(c_ref[0], state, preferred_element_type=F32)
        growth = growth_ref[0, 0]
        gated = []
        squares = jnp.zeros((span, PAIR_LANES), F32)
        for q in range(PAIRS):
            lanes = slice(q * PAIR_LANES, (q + 1) * PAIR_LANES)
            summed = local_ref[0, :, lanes] + carried[:, lanes] * spread_pair(growth, q, low)
            gate = z_ref[0, :, lanes].astype(F32)
            value = summed.astype(BF16).astype(F32) * (gate / (1.0 + jnp.exp(-gate)))
            gated.append(value)
            squares = squares + value * value
        inverse = lax.rsqrt(jnp.sum(squares, axis=1, keepdims=True) * (1.0 / GROUP_LANES) + EPS)
        for q in range(PAIRS):
            lanes = slice(q * PAIR_LANES, (q + 1) * PAIR_LANES)
            out_ref[0, :, lanes] = (gated[q] * inverse * gain_ref[:, lanes]).astype(BF16)


def out_chunk(scalars, group, part, unit_lanes, local, c_flat, growth, z_in, gain, before, ahead_of, ahead, init_of, inits, y_so_far):
    requests, span, width = z_in.shape
    any_spec = pl.BlockSpec(memory_space=pl.ANY)

    def row(i, s):
        return part * REQ_CHUNK + i

    operands = [local, c_flat, growth, z_in, gain, before, *ahead, *inits]
    in_specs = [
        pl.BlockSpec((1, span, GROUP_LANES), lambda i, s: (row(i, s), 0, 0)),
        pl.BlockSpec((1, span, STATE), lambda i, s: (row(i, s), 0, group)),
        pl.BlockSpec((1, 1, span, PER_GROUP), lambda i, s: (row(i, s), group, 0, 0)),
        pl.BlockSpec((1, span, GROUP_LANES), lambda i, s: (row(i, s), 0, group)),
        pl.BlockSpec((1, GROUP_LANES), lambda i, s: (0, group)),
        pl.BlockSpec((1, 1, GROUP_LANES), lambda i, s: (row(i, s), 0, group)),
    ] + [any_spec] * (len(ahead) + len(inits))
    aliases = {}
    if y_so_far is not None:
        aliases = {1 + len(operands): 0}
        operands.append(y_so_far)
        in_specs.append(any_spec)
    buffer = pltpu.VMEM((REQ_CHUNK, STATE, GROUP_LANES), BF16)
    return pl.pallas_call(
        functools.partial(out_body, ahead_of, init_of, unit_lanes, group, part),
        grid_spec=pltpu.PrefetchScalarGridSpec(
            num_scalar_prefetch=1,
            grid=(REQ_CHUNK,),
            in_specs=in_specs,
            out_specs=pl.BlockSpec((1, span, GROUP_LANES), lambda i, s: (row(i, s), 0, group)),
            scratch_shapes=[buffer, buffer, pltpu.SemaphoreType.DMA((2,))],
        ),
        out_shape=jax.ShapeDtypeStruct((requests, span, width), BF16),
        input_output_aliases=aliases,
        cost_estimate=cost(200_000_000, 4_000_000),
        name="out_chunk",
    )(scalars, *operands)


def kept_rows(cache_states):
    holders = lax.axis_size("cache")
    me = lax.axis_index("cache")
    pieces = [lax.dynamic_index_in_dim(cache_states, me, 1, keepdims=False).astype(BF16)]
    for shift in range(1, holders):
        towards = lax.rem(me + shift, holders)
        piece = lax.dynamic_index_in_dim(cache_states, towards, 1, keepdims=False).astype(BF16)
        pairs = [(i, (i + shift) % holders) for i in range(holders)]
        pieces.append(lax.ppermute(piece, "cache", pairs))
    return jnp.concatenate(pieces, axis=0)


def shards(
    x_in, z_in, b_in, c_in, dt_in, dt_bias, a_log, skip_gain, norm_w, cache_states, parent, state_dev, state_slot, spans
):
    me = lax.axis_index("tok")
    toks = lax.axis_size("tok")
    requests, span, width = x_in.shape
    heads_here = dt_in.shape[2]
    groups = width // GROUP_LANES
    parts = requests // REQ_CHUNK
    chunks = groups * parts
    unit = width // toks
    assert span == SPAN and GROUP_LANES % unit == 0

    replica = lax.axis_index("rep")
    parent_here = lax.dynamic_slice_in_dim(parent, replica * requests, requests)
    span_here = lax.dynamic_slice_in_dim(spans, replica * requests, requests)
    valid = (me < span_here).astype(jnp.int32)
    scalars = jnp.concatenate([me.astype(jnp.int32)[None], valid])

    rows = kept_rows(cache_states)
    holders, slots = lax.axis_size("cache"), cache_states.shape[0]
    owner, slot = state_dev[parent_here], state_slot[parent_here]
    place = lax.rem(lax.axis_index("cache") - owner + holders, holders) * slots + slot
    initial = rows[place].reshape(requests, unit, STATE).transpose(0, 2, 1)

    cum, cum_t, step_t, weight, growth, total = prepare(valid, dt_in, dt_bias[None], a_log[None])
    b_flat = b_in.reshape(requests, span, groups * STATE)
    c_flat = c_in.reshape(requests, span, groups * STATE)
    states = block_states(x_in, b_flat, weight)

    totals = lax.all_gather(total[:, 0], "tok")
    order = jnp.arange(toks)[:, None, None]

    def per_lane(exponent):
        return jnp.repeat(jnp.exp(exponent), HEAD_DIM, axis=1)

    def by_chunk(lanes):
        split = lanes.reshape(parts, REQ_CHUNK, groups, GROUP_LANES).transpose(2, 0, 1, 3)
        return jnp.roll(split, -1, axis=0).reshape(chunks, REQ_CHUNK, 1, GROUP_LANES)

    through = by_chunk(per_lane(total[:, 0]))
    before = per_lane(jnp.sum(jnp.where(order < me, totals, 0.0), axis=0))
    before_through = by_chunk(per_lane(jnp.sum(jnp.where(order <= me, totals, 0.0), axis=0)))
    after = by_chunk(per_lane(jnp.sum(jnp.where(order > me, totals, 0.0), axis=0)))

    def unit_slice(by_chunks, which):
        split = by_chunks.reshape(groups, requests, -1, GROUP_LANES)
        lane = which * unit
        place = lax.rem(lane // GROUP_LANES + groups - 1, groups)
        return lax.dynamic_slice(
            split, (place, 0, 0, lax.rem(lane, GROUP_LANES)), (1, requests, split.shape[2], unit)
        )[0]

    own = initial
    if unit < GROUP_LANES:
        blank = jnp.zeros((requests, STATE, GROUP_LANES), BF16)
        own = lax.dynamic_update_slice(blank, initial, (0, 0, lax.rem(me * unit, GROUP_LANES)))
    own = own.reshape(parts, REQ_CHUNK, STATE, GROUP_LANES)
    own_group = (me * unit) // GROUP_LANES

    def pick(values, c):
        return lax.dynamic_index_in_dim(values, c, 0, keepdims=False)

    received, passed = {}, {}

    def pass_on(h):
        if h in passed:
            return passed[h]
        early = h < HOP and (toks > 1) and (h // parts + 1) % groups != 0
        if early:
            passed[h] = states[h]
            return passed[h]
        c = jnp.clip(h - HOP * me, 0, chunks - 1)
        group = lax.rem(c // parts + 1, groups)
        value = pick(states, c).astype(F32)
        if h - HOP in received:
            value = value + pick(through, c) * received[h - HOP].astype(F32)
        mine = pick(before_through, c) * pick(own, lax.rem(c, parts)).astype(F32)
        value = value + jnp.where(group == own_group, mine, 0.0)
        passed[h] = value.astype(BF16)
        return passed[h]

    for h in range(chunks + HOP * (toks - 2)):
        pairs = [(k, k + 1) for k in range(toks - 1) if 0 <= h - HOP * k < chunks]
        received[h] = lax.ppermute(pass_on(h), "tok", pairs)

    backward = [(k, k - 1) for k in range(1, toks)]
    arrived = []
    sent = initial
    for s in range(toks):
        if s:
            which = jnp.clip(s - toks + me, 0, toks - 1)
            later = unit_slice(after, which) * unit_slice(states, which).astype(F32) + arrived[-1].astype(F32)
            sent = jnp.where(s >= toks - me, later.astype(BF16), arrived[-1])
        arrived.append(lax.ppermute(sent, "tok", backward))

    inits = [initial] + arrived[: toks - 1]
    if unit < GROUP_LANES:
        stacked = jnp.stack(inits)[lax.rem(jnp.arange(toks) - me + toks, toks)]
        inits = [stacked.transpose(1, 2, 0, 3).reshape(requests, STATE, width)]

    ends = []
    for part in range(parts):
        value = None
        for device in range(toks):
            chunk = ((device * unit // GROUP_LANES + groups - 1) % groups) * parts + part
            candidate = pass_on(chunk + HOP * device)
            value = candidate if value is None else jnp.where(me == device, candidate, value)
        ends.append(value)
    ends = jnp.concatenate(ends, axis=0)
    if unit < GROUP_LANES:
        ends = lax.dynamic_slice_in_dim(ends, lax.rem(me * unit, GROUP_LANES), unit, 2)
    final = unit_slice(after, me) * ends.astype(F32) + arrived[-1].astype(F32)
    final_state = final.transpose(0, 2, 1).reshape(requests, unit // HEAD_DIM, HEAD_DIM, STATE)

    skip_lanes = jnp.repeat(skip_gain, HEAD_DIM)[None]
    local = {}
    y_out = None
    for j in range(chunks):
        group, part = (j // parts + 1) % groups, j % parts
        if group not in local:
            local[group] = local_part(group, valid, x_in, b_flat, c_flat, cum, cum_t, step_t, skip_lanes)
        ahead_of = [None] + list(range(toks - 1))
        ahead = [received[j + HOP * k] for k in range(toks - 1)]
        if unit < GROUP_LANES:
            init_of, these = [0] * toks, inits
        else:
            holder = group * GROUP_LANES // unit
            init_of = [holder - k if k <= holder else None for k in range(toks)]
            these = inits[: holder + 1]
        y_out = out_chunk(
            scalars, group, part, unit, local[group], c_flat, growth, z_in, norm_w[None], before[:, None],
            ahead_of, ahead, init_of, these, y_out,
        )
    return (y_out, final_state)


def solution(mesh):
    placed = (
        P(("groups", "rep"), "tok", "cache"),
        P(("groups", "rep"), "tok", "cache"),
        P(("groups", "rep"), "tok", "cache", None),
        P(("groups", "rep"), "tok", "cache", None),
        P(("groups", "rep"), "tok", "cache"),
        P("cache"),
        P("cache"),
        P("cache"),
        P("cache"),
        P(("groups", "cache"), None, "tok", None, None),
        P("groups"),
        P("groups"),
        P("groups"),
        P("groups"),
    )
    return jax.shard_map(
        shards,
        mesh=mesh,
        in_specs=placed,
        out_specs=(
            P(("groups", "rep"), "tok", "cache"),
            P(("groups", "rep"), ("cache", "tok"), None, None),
        ),
        check_vma=False,
    )
```

time: 403 us -> 240 us (0.60); the launches traced: 397 us -> 239 us
  waiting for transfers between devices: 218 us -> 43.3 us
  Pallas kernels: 0 us -> 78 us
  local copies, waits for them, and re-layouts: 79.3 us -> 16.6 us
  blocking collectives: 0 us -> 28.8 us
  matrix products: 26 us -> 0 us
  starting transfers between devices: 18.6 us -> 39 us
  between operations: 15.8 us -> 1.71 us
  other arithmetic: 38.7 us -> 31.7 us
    all_gather x2 -> x0, waiting for transfers between devices: 96.1 us -> none  [the longest x1 81 us: shards(): lax.all_gather(c_in, 'tok', axis=1, tiled=True)]
    all_to_all x3 -> x0, waiting for transfers between devices: 85.9 us -> none  [the longest x1 83.7 us: shards(): lax.all_to_all(ssd, 'tok', split_axis=1, concat_axis=2, tiled=True)]
    pallas_call x0 -> x14, Pallas kernels: none -> 78 us  [the longest x8 37.1 us: out_chunk(): pl.pallas_call(functools.partial(out_body, ahead_of, init_of, unit_lanes,...]
    ppermute x0 -> x17, waiting for transfers between devices: none -> 43.3 us  [the longest x12 31.2 us: shards(): received[h] = lax.ppermute(pass_on(h), 'tok', pairs)]
    ppermute x0 -> x17, starting transfers between devices: none -> 39 us  [the longest x12 20.6 us: shards(): received[h] = lax.ppermute(pass_on(h), 'tok', pairs)]
    unnamed x4 -> x0, waiting for transfers between devices: 36.2 us -> none
    all_gather x0 -> x1, blocking collectives: none -> 28.8 us  [shards(): totals = lax.all_gather(total[:, 0], 'tok')]
    dot_general x4 -> x0, matrix products: 26 us -> none  [the longest x1 9.13 us: span_scan(): jnp.einsum('mkhij,mkjhp->mkihp', blend_factors, x_blocks, preferred_eleme...]
  transfers between devices with their start and end apart: 6 -> 17, of which waited for: 5 -> 6; matrix products, arithmetic and copies ran while one was open for 8% -> 17% of each run, Pallas kernels for 0% -> 33%
where the time goes in v1:
time: 240 us; the launch traced here: 239 us
  Pallas kernels  78 us (32%)
  waiting for transfers between devices  43.3 us (18%)
  starting transfers between devices  39 us (16%)
  other arithmetic  31.7 us (13%)
  blocking collectives  28.8 us (12%)
  local copies, waits for them, and re-layouts  16.6 us (7%)
    pallas_call x8, Pallas kernels, out_chunk(): pl.pallas_call(functools.partial(out_body, ahead_of, init_of, unit_lanes,...  37.1 us
    ppermute x12, waiting for transfers between devices, shards(): received[h] = lax.ppermute(pass_on(h), 'tok', pairs)  31.2 us
    all_gather x1, blocking collectives, shards(): totals = lax.all_gather(total[:, 0], 'tok')  28.8 us
    pallas_call x4, Pallas kernels, local_part(): pl.pallas_call(local_body, grid_spec=pltpu.PrefetchScalarGridSpec(num_sca...  22.5 us
    ppermute x12, starting transfers between devices, shards(): received[h] = lax.ppermute(pass_on(h), 'tok', pairs)  20.6 us
    ppermute x4, starting transfers between devices, shards(): arrived.append(lax.ppermute(sent, 'tok', backward))  16.8 us
    pallas_call x1, Pallas kernels, block_states(): pl.pallas_call(block_body, grid=(groups * parts, REQ_CHUNK), out_shape=ja...  14.7 us
    convert_element_type x4, other arithmetic, pass_on(): passed[h] = value.astype(BF16)  13.1 us
  transfers between devices with their start and end apart: 17, of which 6 were waited for; matrix products, arithmetic and copies ran while one was open for 17% of the time, Pallas kernels for 33%

profile of v1, /device:TPU:16, one launch (start us, length us, event | category | flops | bytes accessed | tf_op | source)
XLA Modules:
  0.0 239.2 jit_solution(16912997255632441441)
XLA Ops:
  0.7 1.8 fusion.42
  2.5 1.6 collective-permute-start.1
  6.5 3.7 %prep.1 = (f32[4,4,128,16]{3,2,1,0:T(8,128)}, f32[4,4,16,128]{3,2,1,0:T(8,128)}, f32[4,4,16,128]{3,2,1,0:T(8,128)}, f32[4,4,128,16]{3,2,1,0:T(8,128)}, f32[4,4,128,16]{3,2,1,0:T(8,128)}, /*index=5*/f32[4,1,64]{2,1,0:T(1,128)}) custom-call(s32[4]{0:T(128)} %compare_convert_fusion.valid_ref, bf16[4,128,64]{2,1,0:T(8,128)(2,1)} %copy.37.dt_ref, ...), custom_call_target="tpu_custom_call" | custom-call | flops 20000000 | bytes 4000000 | tf_op jit(solution)/shard_map/prep/pallas_call | solution.py:72
  10.2 14.7 %block_states.1 = bf16[8,2,128,1024]{3,2,1,0:T(8,128)(2,1)} custom-call(bf16[4,128,4096]{2,1,0:T(8,128)(2,1)} %x_ref.9, bf16[4,128,512]{2,1,0:T(8,128)(2,1)} %reshape.169.b_ref, f32[4,4,128,16]{3,2,1,0:T(8,128)} %get-tuple-element.13.weight_ref), custom_call_target="tpu_custom_call" | custom-call | flops 600000000 | bytes 12000000 | tf_op jit(solution)/shard_map/block_states/pallas_call | solution.py:102
  24.9 2.3 slice_bitcast_fusion
  28.6 28.8 %all-gather = f32[16,1,64]{2,1,0:T(1,128)S(1)} all-gather(f32[4,1,64]{2,1,0:T(1,128)S(1)} %copy-done.19), channel_id=2, replica_groups=mesh['groups'=2,'tok'=4,'cache'=2,'rep'=2] {'tok'}, dimensions={0}, use_global_device_ids=true | all-gather | bytes 5120 | tf_op jit(solution)/shard_map/all_gather | solution.py:314
  60.3 4.7 %collective-permute-start.13 = (bf16[4,128,1024]{2,1,0:T(8,128)(2,1)S(1)}, bf16[4,128,1024]{2,1,0:T(8,128)(2,1)S(1)}, u32[]{:S(2)}, u32[]{:S(2)}) collective-permute-start(bf16[4,128,1024]{2,1,0:T(8,128)(2,1)S(1)} %bitcast.167), channel_id=1, source_target_pairs={{4,0},{8,4},{12,8},{5,1},{9,5},{13,9},{6,2},{10,6},{14,10},{7,3},{... | collective-permute-start | bytes 3145736 | tf_op jit(solution)/shard_map/ppermute | solution.py:378
  66.0 3.3 %fusion.23 = (bf16[2,128,1024]{2,1,0:T(8,128)(2,1)}, bf16[2,128,1024]{2,1,0:T(8,128)(2,1)}) fusion(bf16[2,128,1024]{2,1,0:T(8,128)(2,1)S(1)} %collective-permute-done.7.refs_0_, bf16[2,2,128,1024]{3,2,1,0:T(8,128)(2,1)S(1)} %bitcast.168, s32[]{:T(128)S(6)} %select_n.312, f32[2,1024]{1,0:T(2,128)S(1)} %get-tuple-element.53, ...), kind=kLoop, calls=%fused_computation.39 | loop fusion | flops 4718592 | bytes 4227090 | tf_op jit(solution)/shard_map/convert_element_type | solution.py:363
  72.5 12.1 %collective-permute-done.13.refs_4_ = bf16[4,128,1024]{2,1,0:T(8,128)(2,1)S(1)} collective-permute-done((bf16[4,128,1024]{2,1,0:T(8,128)(2,1)S(1)}, bf16[4,128,1024]{2,1,0:T(8,128)(2,1)S(1)}, u32[]{:S(2)}, u32[]{:S(2)}) %collective-permute-start.13) | collective-permute-done | bytes 1048608 | tf_op jit(solution)/shard_map/ppermute | solution.py:378
  84.6 3.1 %fusion.6 = bf16[4,128,1024]{2,1,0:T(8,128)(2,1)} fusion(bf16[4,128,1024]{2,1,0:T(8,128)(2,1)S(1)} %collective-permute-done.13.refs_4_, bf16[4,4,128,1024]{3,2,1,0:T(8,128)(2,1)} %bitcast.182, s32[]{:T(128)S(6)} %select_n.333, f32[4,1024]{1,0:T(4,128)S(1)} %bitcast.207, pred[]{:T(512)S(6)} %le.19), kind=kLoop, calls=%fused_computation.13 | loop fusion | flops 3145728 | bytes 3162117 | tf_op jit(solution)/shard_map/jit(_where)/select_n | solution.py:377
  87.7 4.2 %collective-permute-start.14 = (bf16[4,128,1024]{2,1,0:T(8,128)(2,1)}, bf16[4,128,1024]{2,1,0:T(8,128)(2,1)S(1)}, u32[]{:S(2)}, u32[]{:S(2)}) collective-permute-start(bf16[4,128,1024]{2,1,0:T(8,128)(2,1)} %fusion.6), channel_id=1, source_target_pairs={{4,0},{8,4},{12,8},{5,1},{9,5},{13,9},{6,2},{10,6},{14,10},{7,3},{... | collective-permute-start | bytes 3145736 | tf_op jit(solution)/shard_map/ppermute | solution.py:378
  92.0 1.3 collective-permute-done.8.refs_1_.refs_0_
  93.3 3.3 %fusion.20 = (bf16[2,128,1024]{2,1,0:T(8,128)(2,1)}, bf16[2,128,1024]{2,1,0:T(8,128)(2,1)}) fusion(bf16[2,128,1024]{2,1,0:T(8,128)(2,1)} %collective-permute-done.8.refs_1_.refs_0_, bf16[2,2,128,1024]{3,2,1,0:T(8,128)(2,1)S(1)} %bitcast.169, s32[]{:T(128)S(6)} %select_n.316, f32[2,1024]{1,0:T(2,128)S(1)} %get-tuple-element.52, ...), kind=kLoop, calls=%fused_computation.35 | loop fusion | flops 4718592 | bytes 4227090 | tf_op jit(solution)/shard_map/convert_element_type | solution.py:363
  96.6 1.9 collective-permute-start.3
  98.5 1.9 collective-permute-start.9
  100.5 13.1 %collective-permute-done.3.refs_2_.refs_1_.refs_0_ = bf16[2,128,1024]{2,1,0:T(8,128)(2,1)S(1)} collective-permute-done((bf16[2,128,1024]{2,1,0:T(8,128)(2,1)}, bf16[2,128,1024]{2,1,0:T(8,128)(2,1)S(1)}, u32[]{:S(2)}, u32[]{:S(2)}) %collective-permute-start.3) | collective-permute-done | bytes 524320 | tf_op jit(solution)/shard_map/ppermute | solution.py:368
  113.6 5.9 %collective-permute-done.9.refs_2_.refs_1_.refs_0_ = bf16[2,128,1024]{2,1,0:T(8,128)(2,1)S(1)} collective-permute-done((bf16[2,128,1024]{2,1,0:T(8,128)(2,1)}, bf16[2,128,1024]{2,1,0:T(8,128)(2,1)S(1)}, u32[]{:S(2)}, u32[]{:S(2)}) %collective-permute-start.9) | collective-permute-done | bytes 524320 | tf_op jit(solution)/shard_map/ppermute | solution.py:368
  119.5 3.2 %fusion.17 = (bf16[2,128,1024]{2,1,0:T(8,128)(2,1)}, bf16[2,128,1024]{2,1,0:T(8,128)(2,1)}) fusion(bf16[2,128,1024]{2,1,0:T(8,128)(2,1)S(1)} %collective-permute-done.9.refs_2_.refs_1_.refs_0_, bf16[2,2,128,1024]{3,2,1,0:T(8,128)(2,1)S(1)} %bitcast.170, s32[]{:T(128)S(6)} %select_n.320, f32[2,1024]{1,0:T(2,128)S(1)} %get-tuple-element.51, ...), kind=kLoop, calls=%fused_computation.31 | loop fusion | flops 4718592 | bytes 4227090 | tf_op jit(solution)/shard_map/convert_element_type | solution.py:363
  122.7 2.2 collective-permute-start.10
  124.9 1.9 collective-permute-start.4
  126.8 3.1 %fusion.7 = bf16[4,128,1024]{2,1,0:T(8,128)(2,1)} fusion(bf16[4,128,1024]{2,1,0:T(8,128)(2,1)S(1)} %collective-permute-done.14.refs_5_, bf16[4,4,128,1024]{3,2,1,0:T(8,128)(2,1)} %bitcast.183, s32[]{:T(128)S(6)} %select_n.337, f32[4,1024]{1,0:T(4,128)S(1)} %bitcast.205, pred[]{:T(512)S(6)} %le.20), kind=kLoop, calls=%fused_computation.14 | loop fusion | flops 3145728 | bytes 3162117 | tf_op jit(solution)/shard_map/jit(_where)/select_n | solution.py:377
  129.9 3.9 %collective-permute-start.15 = (bf16[4,128,1024]{2,1,0:T(8,128)(2,1)}, bf16[4,128,1024]{2,1,0:T(8,128)(2,1)S(1)}, u32[]{:S(2)}, u32[]{:S(2)}) collective-permute-start(bf16[4,128,1024]{2,1,0:T(8,128)(2,1)} %fusion.7), channel_id=1, source_target_pairs={{4,0},{8,4},{12,8},{5,1},{9,5},{13,9},{6,2},{10,6},{14,10},{7,3},{... | collective-permute-start | bytes 3145736 | tf_op jit(solution)/shard_map/ppermute | solution.py:378
  133.8 5.3 %collective-permute-done.10.refs_2_.refs_1_.refs_0_ = bf16[2,128,1024]{2,1,0:T(8,128)(2,1)} collective-permute-done((bf16[2,128,1024]{2,1,0:T(8,128)(2,1)}, bf16[2,128,1024]{2,1,0:T(8,128)(2,1)}, u32[]{:S(2)}, u32[]{:S(2)}) %collective-permute-start.10) | collective-permute-done | bytes 524320 | tf_op jit(solution)/shard_map/ppermute | solution.py:368
  139.1 5.6 %collective-permute-done.4.refs_2_.refs_1_.refs_0_ = bf16[2,128,1024]{2,1,0:T(8,128)(2,1)} collective-permute-done((bf16[2,128,1024]{2,1,0:T(8,128)(2,1)}, bf16[2,128,1024]{2,1,0:T(8,128)(2,1)}, u32[]{:S(2)}, u32[]{:S(2)}) %collective-permute-start.4) | collective-permute-done | bytes 524320 | tf_op jit(solution)/shard_map/ppermute | solution.py:368
  144.7 3.3 %fusion.14 = (bf16[2,128,1024]{2,1,0:T(8,128)(2,1)}, bf16[2,128,1024]{2,1,0:T(8,128)(2,1)}) fusion(bf16[2,128,1024]{2,1,0:T(8,128)(2,1)} %collective-permute-done.10.refs_2_.refs_1_.refs_0_, bf16[2,2,128,1024]{3,2,1,0:T(8,128)(2,1)S(1)} %bitcast.171, s32[]{:T(128)S(6)} %select_n.324, f32[2,1024]{1,0:T(2,128)S(1)} %get-tuple-element.50, ...), kind=kLoop, calls=%fused_computation.26 | loop fusion | flops 4718592 | bytes 4227090 | tf_op jit(solution)/shard_map/convert_element_type | solution.py:363
  148.0 2.5 %collective-permute-start.11 = (bf16[2,128,1024]{2,1,0:T(8,128)(2,1)}, bf16[2,128,1024]{2,1,0:T(8,128)(2,1)S(1)}, u32[]{:S(2)}, u32[]{:S(2)}) collective-permute-start(bf16[2,128,1024]{2,1,0:T(8,128)(2,1)} %get-tuple-element.23), channel_id=1, source_target_pairs={{4,8},{8,12},{5,9},{9,13},{6,10},{10,14},{7,11},{11,15},{20,24},{2... | collective-permute-start | bytes 1572872 | tf_op jit(solution)/shard_map/ppermute | solution.py:368
  150.6 2.0 reshape.170.c_ref
  154.2 5.6 %local_part.7.local_ref = f32[4,128,1024]{2,1,0:T(8,128)} custom-call(s32[4]{0:T(128)} %compare_convert_fusion.valid_ref, bf16[4,128,4096]{2,1,0:T(8,128)(2,1)} %x_ref.9, bf16[4,128,512]{2,1,0:T(8,128)(2,1)} %reshape.169.b_ref, bf16[4,128,512]{2,1,0:T(8,128)(2,1)} %reshape.170.c_ref, f32[4,4,128,16]{3,2,1,0:T(8,128)} %get-tuple-element.8.cum_ref, ...), custom_call_target="tpu_custom_call" | custom-call | flops 1000000000 | bytes 10000000 | tf_op jit(solution)/shard_map/local_part/pallas_call | solution.py:150
  159.8 1.9 collective-permute-start.5
  161.8 3.1 %fusion.8 = bf16[4,128,1024]{2,1,0:T(8,128)(2,1)} fusion(bf16[4,128,1024]{2,1,0:T(8,128)(2,1)S(1)} %collective-permute-done.15.refs_6_, bf16[4,4,128,1024]{3,2,1,0:T(8,128)(2,1)} %bitcast.184, s32[]{:T(128)S(6)} %select_n.351, f32[4,1024]{1,0:T(4,128)S(1)} %bitcast.206, pred[]{:T(512)S(6)} %le.21), kind=kLoop, calls=%fused_computation.15 | loop fusion | flops 3145728 | bytes 3162117 | tf_op jit(solution)/shard_map/jit(_where)/select_n | solution.py:377
  164.9 3.9 %collective-permute-start.16 = (bf16[4,128,1024]{2,1,0:T(8,128)(2,1)}, bf16[4,128,1024]{2,1,0:T(8,128)(2,1)}, u32[]{:S(2)}, u32[]{:S(2)}) collective-permute-start(bf16[4,128,1024]{2,1,0:T(8,128)(2,1)} %fusion.8), channel_id=1, source_target_pairs={{4,0},{8,4},{12,8},{5,1},{9,5},{13,9},{6,2},{10,6},{14,10},{7,3},{... | collective-permute-start | bytes 3145736 | tf_op jit(solution)/shard_map/ppermute | solution.py:378
  168.8 3.0 %fusion.39 = (bf16[2,128,1024]{2,1,0:T(8,128)(2,1)}, bf16[2,128,1024]{2,1,0:T(8,128)(2,1)}) fusion(bf16[2,128,1024]{2,1,0:T(8,128)(2,1)} %get-tuple-element.25, bf16[2,128,1024]{2,1,0:T(8,128)(2,1)} %get-tuple-element.29, pred[]{:T(512)S(6)} %eq.54, pred[]{:T(512)S(6)} %eq.53, pred[]{:T(512)S(6)} %eq.52, bf16[2,2,128,1024]{3,2,1,0:T(8,128)(2,1)S(1)} %bitcast.172, ...), kind=kLoop, calls=%fused_computation.71 | loop fusion | flops 3145728 | bytes 3686412 | tf_op jit(solution)/shard_map/jit(_where)/select_n | solution.py:391
  171.9 2.9 %collective-permute-start.12 = (bf16[2,128,1024]{2,1,0:T(8,128)(2,1)}, bf16[2,128,1024]{2,1,0:T(8,128)(2,1)S(1)}, u32[]{:S(2)}, u32[]{:S(2)}) collective-permute-start(bf16[2,128,1024]{2,1,0:T(8,128)(2,1)} %get-tuple-element.20), channel_id=1, source_target_pairs={{8,12},{9,13},{10,14},{11,15},{24,28},{25,29},{26,30},{27,31}} | collective-permute-start | bytes 1572872 | tf_op jit(solution)/shard_map/ppermute | solution.py:368
  174.8 3.0 %fusion.40 = (bf16[2,128,1024]{2,1,0:T(8,128)(2,1)}, bf16[2,128,1024]{2,1,0:T(8,128)(2,1)}) fusion(bf16[2,128,1024]{2,1,0:T(8,128)(2,1)} %get-tuple-element.26, bf16[2,128,1024]{2,1,0:T(8,128)(2,1)} %get-tuple-element.30, pred[]{:T(512)S(6)} %eq.54, pred[]{:T(512)S(6)} %eq.53, pred[]{:T(512)S(6)} %eq.52, bf16[2,2,128,1024]{3,2,1,0:T(8,128)(2,1)S(1)} %bitcast.173, ...), kind=kLoop, calls=%fused_computation.72 | loop fusion | flops 3145728 | bytes 3686412 | tf_op jit(solution)/shard_map/jit(_where)/select_n | solution.py:391
  177.8 1.5 collective-permute-start.6
  179.3 5.6 %local_part.6.local_ref = f32[4,128,1024]{2,1,0:T(8,128)} custom-call(s32[4]{0:T(128)} %compare_convert_fusion.valid_ref, bf16[4,128,4096]{2,1,0:T(8,128)(2,1)} %x_ref.9, bf16[4,128,512]{2,1,0:T(8,128)(2,1)} %reshape.169.b_ref, bf16[4,128,512]{2,1,0:T(8,128)(2,1)} %reshape.170.c_ref, f32[4,4,128,16]{3,2,1,0:T(8,128)} %get-tuple-element.8.cum_ref, ...), custom_call_target="tpu_custom_call" | custom-call | flops 1000000000 | bytes 10000000 | tf_op jit(solution)/shard_map/local_part/pallas_call | solution.py:150
  184.9 5.6 %local_part.5.local_ref = f32[4,128,1024]{2,1,0:T(8,128)} custom-call(s32[4]{0:T(128)} %compare_convert_fusion.valid_ref, bf16[4,128,4096]{2,1,0:T(8,128)(2,1)} %x_ref.9, bf16[4,128,512]{2,1,0:T(8,128)(2,1)} %reshape.169.b_ref, bf16[4,128,512]{2,1,0:T(8,128)(2,1)} %reshape.170.c_ref, f32[4,4,128,16]{3,2,1,0:T(8,128)} %get-tuple-element.8.cum_ref, ...), custom_call_target="tpu_custom_call" | custom-call | flops 1000000000 | bytes 10000000 | tf_op jit(solution)/shard_map/local_part/pallas_call | solution.py:150
  190.5 5.7 %local_part.4.local_ref = f32[4,128,1024]{2,1,0:T(8,128)} custom-call(s32[4]{0:T(128)} %compare_convert_fusion.valid_ref, bf16[4,128,4096]{2,1,0:T(8,128)(2,1)} %x_ref.9, bf16[4,128,512]{2,1,0:T(8,128)(2,1)} %reshape.169.b_ref, bf16[4,128,512]{2,1,0:T(8,128)(2,1)} %reshape.170.c_ref, f32[4,4,128,16]{3,2,1,0:T(8,128)} %get-tuple-element.8.cum_ref, ...), custom_call_target="tpu_custom_call" | custom-call | flops 1000000000 | bytes 10000000 | tf_op jit(solution)/shard_map/local_part/pallas_call | solution.py:150
  196.8 4.3 %out_chunk.8.refs_5_ = bf16[4,128,4096]{2,1,0:T(8,128)(2,1)} custom-call(s32[5]{0:T(128)} %pad_add_fusion.scalars, f32[4,128,1024]{2,1,0:T(8,128)} %local_part.7.local_ref, bf16[4,128,512]{2,1,0:T(8,128)(2,1)} %reshape.170.c_ref, f32[4,4,128,16]{3,2,1,0:T(8,128)} %get-tuple-element.11.growth_ref, bf16[4,128,4096]{2,1,0:T(8,128)(2,1)} %z_ref.15, ...), custom_call_target="tpu_custom_call" | custom-call | flops 200000000 | bytes 4000000 | tf_op jit(solution)/shard_map/out_chunk/pallas_call | solution.py:256
  201.1 4.8 %out_chunk.9.refs_6_ = bf16[4,128,4096]{2,1,0:T(8,128)(2,1)} custom-call(s32[5]{0:T(128)} %pad_add_fusion.scalars, f32[4,128,1024]{2,1,0:T(8,128)} %local_part.7.local_ref, bf16[4,128,512]{2,1,0:T(8,128)(2,1)} %reshape.170.c_ref, f32[4,4,128,16]{3,2,1,0:T(8,128)} %get-tuple-element.11.growth_ref, ...), custom_call_target="tpu_custom_call", output_to_operand_aliasing={{}: (12, {})} | custom-call | flops 200000000 | bytes 4000000 | tf_op jit(solution)/shard_map/out_chunk/pallas_call | solution.py:256
  206.0 4.5 %out_chunk.10.refs_6_ = bf16[4,128,4096]{2,1,0:T(8,128)(2,1)} custom-call(s32[5]{0:T(128)} %pad_add_fusion.scalars, f32[4,128,1024]{2,1,0:T(8,128)} %local_part.6.local_ref, bf16[4,128,512]{2,1,0:T(8,128)(2,1)} %reshape.170.c_ref, f32[4,4,128,16]{3,2,1,0:T(8,128)} %get-tuple-element.11.growth_ref, ...), custom_call_target="tpu_custom_call", output_to_operand_aliasing={{}: (13, {})} | custom-call | flops 200000000 | bytes 4000000 | tf_op jit(solution)/shard_map/out_chunk/pallas_call | solution.py:256
  210.4 5.0 %out_chunk.11.refs_7_ = bf16[4,128,4096]{2,1,0:T(8,128)(2,1)} custom-call(s32[5]{0:T(128)} %pad_add_fusion.scalars, f32[4,128,1024]{2,1,0:T(8,128)} %local_part.6.local_ref, bf16[4,128,512]{2,1,0:T(8,128)(2,1)} %reshape.170.c_ref, f32[4,4,128,16]{3,2,1,0:T(8,128)} %get-tuple-element.11.growth_ref, ...), custom_call_target="tpu_custom_call", output_to_operand_aliasing={{}: (13, {})} | custom-call | flops 200000000 | bytes 4000000 | tf_op jit(solution)/shard_map/out_chunk/pallas_call | solution.py:256
  215.4 4.5 %out_chunk.12.refs_7_ = bf16[4,128,4096]{2,1,0:T(8,128)(2,1)} custom-call(s32[5]{0:T(128)} %pad_add_fusion.scalars, f32[4,128,1024]{2,1,0:T(8,128)} %local_part.5.local_ref, bf16[4,128,512]{2,1,0:T(8,128)(2,1)} %reshape.170.c_ref, f32[4,4,128,16]{3,2,1,0:T(8,128)} %get-tuple-element.11.growth_ref, ...), custom_call_target="tpu_custom_call", output_to_operand_aliasing={{}: (14, {})} | custom-call | flops 200000000 | bytes 4000000 | tf_op jit(solution)/shard_map/out_chunk/pallas_call | solution.py:256
  219.9 5.0 %out_chunk.13.refs_4_ = bf16[4,128,4096]{2,1,0:T(8,128)(2,1)} custom-call(s32[5]{0:T(128)} %pad_add_fusion.scalars, f32[4,128,1024]{2,1,0:T(8,128)} %local_part.5.local_ref, bf16[4,128,512]{2,1,0:T(8,128)(2,1)} %reshape.170.c_ref, f32[4,4,128,16]{3,2,1,0:T(8,128)} %get-tuple-element.11.growth_ref, ...), custom_call_target="tpu_custom_call", output_to_operand_aliasing={{}: (14, {})} | custom-call | flops 200000000 | bytes 4000000 | tf_op jit(solution)/shard_map/out_chunk/pallas_call | solution.py:256
  225.7 4.3 %out_chunk.14.refs_4_ = bf16[4,128,4096]{2,1,0:T(8,128)(2,1)} custom-call(s32[5]{0:T(128)} %pad_add_fusion.scalars, f32[4,128,1024]{2,1,0:T(8,128)} %local_part.4.local_ref, bf16[4,128,512]{2,1,0:T(8,128)(2,1)} %reshape.170.c_ref, f32[4,4,128,16]{3,2,1,0:T(8,128)} %get-tuple-element.11.growth_ref, ...), custom_call_target="tpu_custom_call", output_to_operand_aliasing={{}: (11, {})} | custom-call | flops 200000000 | bytes 4000000 | tf_op jit(solution)/shard_map/out_chunk/pallas_call | solution.py:256
  230.9 4.8 %out_chunk.15 = bf16[4,128,4096]{2,1,0:T(8,128)(2,1)} custom-call(s32[5]{0:T(128)} %pad_add_fusion.scalars, f32[4,128,1024]{2,1,0:T(8,128)} %local_part.4.local_ref, bf16[4,128,512]{2,1,0:T(8,128)(2,1)} %reshape.170.c_ref, f32[4,4,128,16]{3,2,1,0:T(8,128)} %get-tuple-element.11.growth_ref, ...), custom_call_target="tpu_custom_call", output_to_operand_aliasing={{}: (11, {})} | custom-call | flops 200000000 | bytes 4000000 | tf_op jit(solution)/shard_map/out_chunk/pallas_call | solution.py:256
  235.7 1.6 add_bitcast_fusion
  237.4 1.8 copy.42
  (109 shorter events, 14.3 us)
Async XLA Ops:
  0.6 56.9 %copy-start = (s32[4]{0:T(128)S(1)}, s32[4]{0:T(128)}, u32[]{:S(2)}) copy-start(s32[4]{0:T(128)} %param.25) | copy-start | bytes 52
  0.6 3.4 %copy-start.17 = (bf16[4,128,64]{1,2,0:T(8,128)(2,1)S(1)}, bf16[4,128,64]{1,2,0:T(8,128)(2,1)}, u32[]{:S(2)}) copy-start(bf16[4,128,64]{1,2,0:T(8,128)(2,1)} %param.18) | copy-start | bytes 196612
  0.7 4.2 %copy-start.16 = (bf16[4,128,4,128]{3,2,1,0:T(4,128)(2,1)S(1)}, bf16[4,128,4,128]{3,2,1,0:T(4,128)(2,1)}, u32[]{:S(2)}) copy-start(bf16[4,128,4,128]{3,2,1,0:T(4,128)(2,1)} %param.16) | copy-start | bytes 1572868
  0.7 5.2 %copy-start.21 = (s32[8]{0:T(128)S(1)}, s32[8]{0:T(128)}, u32[]{:S(2)}) copy-start(s32[8]{0:T(128)} %param.27) | copy-start | bytes 100
  2.5 56.3 %collective-permute-start.1 = (bf16[2,16,64,128]{3,2,1,0:T(8,128)(2,1)S(1)}, bf16[2,16,64,128]{3,2,1,0:T(8,128)(2,1)S(1)}, u32[]{:S(2)}, u32[]{:S(2)}) collective-permute-start(bf16[2,16,64,128]{3,2,1,0:T(8,128)(2,1)S(1)} %get-tuple-element.34), channel_id=1, source_target_pairs={{0,2},{2,0},{1,3},{3,1},{4,6},{6,4},{5,7},{7,5},{8,10},{10,8},{9,1... | collective-permute-start | bytes 1572872 | tf_op jit(solution)/shard_map/ppermute | solution.py:280
  24.9 3.7 %copy-start.19 = (f32[4,1,64]{2,1,0:T(1,128)S(1)}, f32[4,1,64]{2,1,0:T(1,128)}, u32[]{:S(2)}) copy-start(f32[4,1,64]{2,1,0:T(1,128)} %get-tuple-element.12) | copy-start | bytes 3076
  24.9 32.5 %copy-start.22 = (s32[8]{0:T(128)S(1)}, s32[8]{0:T(128)}, u32[]{:S(2)}) copy-start(s32[8]{0:T(128)} %param.24) | copy-start | bytes 100
  24.9 33.3 %copy-start.1 = (s32[4]{0:T(128)S(1)}, s32[4]{0:T(128)}, u32[]{:S(2)}) copy-start(s32[4]{0:T(128)} %param.26) | copy-start | bytes 52
  27.2 38.8 %collective-permute-start = (bf16[2,128,1024]{2,1,0:T(8,128)(2,1)}, bf16[2,128,1024]{2,1,0:T(8,128)(2,1)S(1)}, u32[]{:S(2)}, u32[]{:S(2)}) collective-permute-start(bf16[2,128,1024]{2,1,0:T(8,128)(2,1)} %get-tuple-element.32), channel_id=1, source_target_pairs={{0,4},{1,5},{2,6},{3,7},{16,20},{17,21},{18,22},{19,23}} | collective-permute-start | bytes 1572872 | tf_op jit(solution)/shard_map/ppermute | solution.py:368
  27.9 38.1 %collective-permute-start.7 = (bf16[2,128,1024]{2,1,0:T(8,128)(2,1)}, bf16[2,128,1024]{2,1,0:T(8,128)(2,1)S(1)}, u32[]{:S(2)}, u32[]{:S(2)}) collective-permute-start(bf16[2,128,1024]{2,1,0:T(8,128)(2,1)} %get-tuple-element.31), channel_id=1, source_target_pairs={{0,4},{1,5},{2,6},{3,7},{16,20},{17,21},{18,22},{19,23}} | collective-permute-start | bytes 1572872 | tf_op jit(solution)/shard_map/ppermute | solution.py:368
  60.2 114.5 %copy-start.2 = (bf16[4,1024,128]{1,2,0:T(8,128)(2,1)}, bf16[4,1024,128]{1,2,0:T(8,128)(2,1)S(1)}, u32[]{:S(2)}) copy-start(bf16[4,1024,128]{1,2,0:T(8,128)(2,1)S(1)} %copy.41) | copy-start | bytes 3145732
  60.3 24.4 %collective-permute-start.13 = (bf16[4,128,1024]{2,1,0:T(8,128)(2,1)S(1)}, bf16[4,128,1024]{2,1,0:T(8,128)(2,1)S(1)}, u32[]{:S(2)}, u32[]{:S(2)}) collective-permute-start(bf16[4,128,1024]{2,1,0:T(8,128)(2,1)S(1)} %bitcast.167), channel_id=1, source_target_pairs={{4,0},{8,4},{12,8},{5,1},{9,5},{13,9},{6,2},{10,6},{14,10},{7,3},{... | collective-permute-start | bytes 3145736 | tf_op jit(solution)/shard_map/ppermute | solution.py:378
  66.0 3.4 %copy-start.10 = (bf16[2,128,1024]{2,1,0:T(8,128)(2,1)}, bf16[2,128,1024]{2,1,0:T(8,128)(2,1)S(1)}, u32[]{:S(2)}) copy-start(bf16[2,128,1024]{2,1,0:T(8,128)(2,1)S(1)} %collective-permute-done.refs_0_) | copy-start | bytes 1572868
  66.0 3.3 %copy-start.11 = (bf16[2,128,1024]{2,1,0:T(8,128)(2,1)}, bf16[2,128,1024]{2,1,0:T(8,128)(2,1)S(1)}, u32[]{:S(2)}) copy-start(bf16[2,128,1024]{2,1,0:T(8,128)(2,1)S(1)} %collective-permute-done.7.refs_0_) | copy-start | bytes 1572868
  69.4 22.6 %collective-permute-start.2 = (bf16[2,128,1024]{2,1,0:T(8,128)(2,1)}, bf16[2,128,1024]{2,1,0:T(8,128)(2,1)}, u32[]{:S(2)}, u32[]{:S(2)}) collective-permute-start(bf16[2,128,1024]{2,1,0:T(8,128)(2,1)} %get-tuple-element.30), channel_id=1, source_target_pairs={{0,4},{4,8},{1,5},{5,9},{2,6},{6,10},{3,7},{7,11},{16,20},{20,24},... | collective-permute-start | bytes 1572872 | tf_op jit(solution)/shard_map/ppermute | solution.py:368
  70.7 22.6 %collective-permute-start.8 = (bf16[2,128,1024]{2,1,0:T(8,128)(2,1)}, bf16[2,128,1024]{2,1,0:T(8,128)(2,1)}, u32[]{:S(2)}, u32[]{:S(2)}) collective-permute-start(bf16[2,128,1024]{2,1,0:T(8,128)(2,1)} %get-tuple-element.29), channel_id=1, source_target_pairs={{0,4},{4,8},{1,5},{5,9},{2,6},{6,10},{3,7},{7,11},{16,20},{20,24},... | collective-permute-start | bytes 1572872 | tf_op jit(solution)/shard_map/ppermute | solution.py:368
  84.6 12.0 %copy-start.3 = (bf16[4,128,1024]{2,1,0:T(8,128)(2,1)}, bf16[4,128,1024]{2,1,0:T(8,128)(2,1)S(1)}, u32[]{:S(2)}) copy-start(bf16[4,128,1024]{2,1,0:T(8,128)(2,1)S(1)} %collective-permute-done.13.refs_4_) | copy-start | bytes 3145732
  87.7 39.1 %collective-permute-start.14 = (bf16[4,128,1024]{2,1,0:T(8,128)(2,1)}, bf16[4,128,1024]{2,1,0:T(8,128)(2,1)S(1)}, u32[]{:S(2)}, u32[]{:S(2)}) collective-permute-start(bf16[4,128,1024]{2,1,0:T(8,128)(2,1)} %fusion.6), channel_id=1, source_target_pairs={{4,0},{8,4},{12,8},{5,1},{9,5},{13,9},{6,2},{10,6},{14,10},{7,3},{... | collective-permute-start | bytes 3145736 | tf_op jit(solution)/shard_map/ppermute | solution.py:378
  96.6 17.0 %collective-permute-start.3 = (bf16[2,128,1024]{2,1,0:T(8,128)(2,1)}, bf16[2,128,1024]{2,1,0:T(8,128)(2,1)S(1)}, u32[]{:S(2)}, u32[]{:S(2)}) collective-permute-start(bf16[2,128,1024]{2,1,0:T(8,128)(2,1)} %get-tuple-element.28), channel_id=1, source_target_pairs={{0,4},{4,8},{8,12},{1,5},{5,9},{9,13},{2,6},{6,10},{10,14},{3,7},{... | collective-permute-start | bytes 1572872 | tf_op jit(solution)/shard_map/ppermute | solution.py:368
  98.5 21.0 %collective-permute-start.9 = (bf16[2,128,1024]{2,1,0:T(8,128)(2,1)}, bf16[2,128,1024]{2,1,0:T(8,128)(2,1)S(1)}, u32[]{:S(2)}, u32[]{:S(2)}) collective-permute-start(bf16[2,128,1024]{2,1,0:T(8,128)(2,1)} %get-tuple-element.27), channel_id=1, source_target_pairs={{0,4},{4,8},{8,12},{1,5},{5,9},{9,13},{2,6},{6,10},{10,14},{3,7},{... | collective-permute-start | bytes 1572872 | tf_op jit(solution)/shard_map/ppermute | solution.py:368
  113.6 9.1 %copy-start.6 = (bf16[2,128,1024]{2,1,0:T(8,128)(2,1)}, bf16[2,128,1024]{2,1,0:T(8,128)(2,1)S(1)}, u32[]{:S(2)}) copy-start(bf16[2,128,1024]{2,1,0:T(8,128)(2,1)S(1)} %collective-permute-done.3.refs_2_.refs_1_.refs_0_) | copy-start | bytes 1572868
  119.5 3.2 %copy-start.7 = (bf16[2,128,1024]{2,1,0:T(8,128)(2,1)}, bf16[2,128,1024]{2,1,0:T(8,128)(2,1)S(1)}, u32[]{:S(2)}) copy-start(bf16[2,128,1024]{2,1,0:T(8,128)(2,1)S(1)} %collective-permute-done.9.refs_2_.refs_1_.refs_0_) | copy-start | bytes 1572868
  122.7 16.5 %collective-permute-start.10 = (bf16[2,128,1024]{2,1,0:T(8,128)(2,1)}, bf16[2,128,1024]{2,1,0:T(8,128)(2,1)}, u32[]{:S(2)}, u32[]{:S(2)}) collective-permute-start(bf16[2,128,1024]{2,1,0:T(8,128)(2,1)} %get-tuple-element.25), channel_id=1, source_target_pairs={{0,4},{4,8},{8,12},{1,5},{5,9},{9,13},{2,6},{6,10},{10,14},{3,7},{... | collective-permute-start | bytes 1572872 | tf_op jit(solution)/shard_map/ppermute | solution.py:368
  124.9 19.9 %collective-permute-start.4 = (bf16[2,128,1024]{2,1,0:T(8,128)(2,1)}, bf16[2,128,1024]{2,1,0:T(8,128)(2,1)}, u32[]{:S(2)}, u32[]{:S(2)}) collective-permute-start(bf16[2,128,1024]{2,1,0:T(8,128)(2,1)} %get-tuple-element.26), channel_id=1, source_target_pairs={{0,4},{4,8},{8,12},{1,5},{5,9},{9,13},{2,6},{6,10},{10,14},{3,7},{... | collective-permute-start | bytes 1572872 | tf_op jit(solution)/shard_map/ppermute | solution.py:368
  126.8 21.2 %copy-start.4 = (bf16[4,128,1024]{2,1,0:T(8,128)(2,1)}, bf16[4,128,1024]{2,1,0:T(8,128)(2,1)S(1)}, u32[]{:S(2)}) copy-start(bf16[4,128,1024]{2,1,0:T(8,128)(2,1)S(1)} %collective-permute-done.14.refs_5_) | copy-start | bytes 3145732
  129.9 31.9 %collective-permute-start.15 = (bf16[4,128,1024]{2,1,0:T(8,128)(2,1)}, bf16[4,128,1024]{2,1,0:T(8,128)(2,1)S(1)}, u32[]{:S(2)}, u32[]{:S(2)}) collective-permute-start(bf16[4,128,1024]{2,1,0:T(8,128)(2,1)} %fusion.7), channel_id=1, source_target_pairs={{4,0},{8,4},{12,8},{5,1},{9,5},{13,9},{6,2},{10,6},{14,10},{7,3},{... | collective-permute-start | bytes 3145736 | tf_op jit(solution)/shard_map/ppermute | solution.py:378
  144.7 7.9 %copy-start.20 = (f32[64]{0:T(128)S(1)}, f32[64]{0:T(128)}, u32[]{:S(2)}) copy-start(f32[64]{0:T(128)} %param.21) | copy-start | bytes 772
  148.0 20.8 %collective-permute-start.11 = (bf16[2,128,1024]{2,1,0:T(8,128)(2,1)}, bf16[2,128,1024]{2,1,0:T(8,128)(2,1)S(1)}, u32[]{:S(2)}, u32[]{:S(2)}) collective-permute-start(bf16[2,128,1024]{2,1,0:T(8,128)(2,1)} %get-tuple-element.23), channel_id=1, source_target_pairs={{4,8},{8,12},{5,9},{9,13},{6,10},{10,14},{7,11},{11,15},{20,24},{2... | collective-permute-start | bytes 1572872 | tf_op jit(solution)/shard_map/ppermute | solution.py:368
  159.8 14.9 %collective-permute-start.5 = (bf16[2,128,1024]{2,1,0:T(8,128)(2,1)}, bf16[2,128,1024]{2,1,0:T(8,128)(2,1)S(1)}, u32[]{:S(2)}, u32[]{:S(2)}) collective-permute-start(bf16[2,128,1024]{2,1,0:T(8,128)(2,1)} %get-tuple-element.24), channel_id=1, source_target_pairs={{4,8},{8,12},{5,9},{9,13},{6,10},{10,14},{7,11},{11,15},{20,24},{2... | collective-permute-start | bytes 1572872 | tf_op jit(solution)/shard_map/ppermute | solution.py:368
  161.8 10.1 %copy-start.5 = (bf16[4,128,1024]{2,1,0:T(8,128)(2,1)}, bf16[4,128,1024]{2,1,0:T(8,128)(2,1)S(1)}, u32[]{:S(2)}) copy-start(bf16[4,128,1024]{2,1,0:T(8,128)(2,1)S(1)} %collective-permute-done.15.refs_6_) | copy-start | bytes 3145732
  164.9 70.8 %collective-permute-start.16 = (bf16[4,128,1024]{2,1,0:T(8,128)(2,1)}, bf16[4,128,1024]{2,1,0:T(8,128)(2,1)}, u32[]{:S(2)}, u32[]{:S(2)}) collective-permute-start(bf16[4,128,1024]{2,1,0:T(8,128)(2,1)} %fusion.8), channel_id=1, source_target_pairs={{4,0},{8,4},{12,8},{5,1},{9,5},{13,9},{6,2},{10,6},{14,10},{7,3},{... | collective-permute-start | bytes 3145736 | tf_op jit(solution)/shard_map/ppermute | solution.py:378
  168.8 9.0 %copy-start.8 = (bf16[2,128,1024]{2,1,0:T(8,128)(2,1)}, bf16[2,128,1024]{2,1,0:T(8,128)(2,1)S(1)}, u32[]{:S(2)}) copy-start(bf16[2,128,1024]{2,1,0:T(8,128)(2,1)S(1)} %collective-permute-done.11.refs_2_.refs_1_) | copy-start | bytes 1572868
  171.9 53.0 %collective-permute-start.12 = (bf16[2,128,1024]{2,1,0:T(8,128)(2,1)}, bf16[2,128,1024]{2,1,0:T(8,128)(2,1)S(1)}, u32[]{:S(2)}, u32[]{:S(2)}) collective-permute-start(bf16[2,128,1024]{2,1,0:T(8,128)(2,1)} %get-tuple-element.20), channel_id=1, source_target_pairs={{8,12},{9,13},{10,14},{11,15},{24,28},{25,29},{26,30},{27,31}} | collective-permute-start | bytes 1572872 | tf_op jit(solution)/shard_map/ppermute | solution.py:368
  174.8 10.1 %copy-start.9 = (bf16[2,128,1024]{2,1,0:T(8,128)(2,1)}, bf16[2,128,1024]{2,1,0:T(8,128)(2,1)S(1)}, u32[]{:S(2)}) copy-start(bf16[2,128,1024]{2,1,0:T(8,128)(2,1)S(1)} %collective-permute-done.5.refs_2_.refs_1_) | copy-start | bytes 1572868
  177.8 52.2 %collective-permute-start.6 = (bf16[2,128,1024]{2,1,0:T(8,128)(2,1)}, bf16[2,128,1024]{2,1,0:T(8,128)(2,1)S(1)}, u32[]{:S(2)}, u32[]{:S(2)}) collective-permute-start(bf16[2,128,1024]{2,1,0:T(8,128)(2,1)} %get-tuple-element.22), channel_id=1, source_target_pairs={{8,12},{9,13},{10,14},{11,15},{24,28},{25,29},{26,30},{27,31}} | collective-permute-start | bytes 1572872 | tf_op jit(solution)/shard_map/ppermute | solution.py:368
  190.5 5.7 %copy-start.18 = (s32[4]{0:T(128)S(1)}, s32[4]{0:T(128)}, u32[]{:S(2)}) copy-start(s32[4]{0:T(128)} %compare_convert_fusion.valid_ref) | copy-start | bytes 52
  224.9 0.8 copy-start.14
  230.0 5.7 %copy-start.12 = (bf16[2,128,1024]{2,1,0:T(8,128)(2,1)S(1)}, bf16[2,128,1024]{2,1,0:T(8,128)(2,1)}, u32[]{:S(2)}) copy-start(bf16[2,128,1024]{2,1,0:T(8,128)(2,1)} %get-tuple-element.19) | copy-start | bytes 1572868
  230.0 5.7 %copy-start.13 = (bf16[2,128,1024]{2,1,0:T(8,128)(2,1)S(1)}, bf16[2,128,1024]{2,1,0:T(8,128)(2,1)}, u32[]{:S(2)}) copy-start(bf16[2,128,1024]{2,1,0:T(8,128)(2,1)} %get-tuple-element.21) | copy-start | bytes 1572868
  230.0 0.8 copy-start.15

commit v2 on v0

v2 whole, which is shorter than its diff:
```python
import functools

import jax
import jax.numpy as jnp
from jax import lax
from jax.experimental import pallas as pl
from jax.experimental.pallas import tpu as pltpu
from jax.sharding import PartitionSpec as P

HEADS = 128
HEAD_DIM = 64
GROUPS = 8
STATE = 128
SPAN = 128
EPS = 1e-05

PER_GROUP = HEADS // GROUPS
GROUP_LANES = PER_GROUP * HEAD_DIM
PAIR_LANES = 2 * HEAD_DIM
PAIRS = PER_GROUP // 2
REQ_CHUNK = 2
HOP = 2
THROUGH, BEFORE, BEFORE_THROUGH, AFTER = range(4)

F32 = jnp.float32
BF16 = jnp.bfloat16
VMEM = pltpu.VMEM
SMEM = pltpu.SMEM


def pin(array):
    return pltpu.with_memory_space_constraint(array, VMEM)


def in_hbm(array):
    return pltpu.with_memory_space_constraint(array, pltpu.HBM)


def call(body, outs, ins, *, scalars=(), after=(), name, flops=1_000, nbytes=1_000, scratch=(), limit=12):
    n_scalars, n_ins, n_after = len(scalars), len(ins), len(after)

    def kernel(*refs):
        head = refs[: n_scalars + n_ins]
        body(*head, *refs[n_scalars + n_ins + n_after :])

    space = [pl.BlockSpec(memory_space=SMEM)] * n_scalars + [pl.BlockSpec(memory_space=VMEM)] * (n_ins + n_after)
    pinned = [pin(a) for a in (*ins, *after)]
    single = isinstance(outs[0][0], int)
    outs = (outs,) if single else tuple(outs)
    result = pl.pallas_call(
        kernel,
        out_shape=tuple(VMEM(shape, dtype) for shape, dtype in outs),
        in_specs=space,
        out_specs=(pl.BlockSpec(memory_space=VMEM),) * len(outs),
        scratch_shapes=list(scratch),
        compiler_params=pltpu.CompilerParams(vmem_limit_bytes=limit << 20),
        cost_estimate=pl.CostEstimate(flops=flops, bytes_accessed=nbytes, transcendentals=0),
        name=name,
    )(*scalars, *pinned)
    return result[0] if single else result


def low_half(rows):
    return lax.broadcasted_iota(jnp.int32, (rows, PAIR_LANES), 1) < HEAD_DIM


def spread_pair(values, q, low):
    return jnp.where(low, values[:, 2 * q : 2 * q + 1], values[:, 2 * q + 1 : 2 * q + 2])


def pair_lanes(q):
    return slice(q * PAIR_LANES, (q + 1) * PAIR_LANES)


def on_device(me, count, branch):
    for device in range(count):
        pl.when(me == device)(functools.partial(branch, device))


def softplus(raw):
    return jnp.maximum(raw, 0.0) + jnp.log1p(jnp.exp(-jnp.abs(raw)))


def front_body(
    order, ids, b_ref, c_ref, spans_hbm, dt_hbm, bias_hbm, alog_hbm, skip_hbm, gain_hbm, x_hbm, info, cum_ref, cum_t_ref,
    step_t_ref, weight_ref, growth_ref, x_ref, bias_ref, alog_ref, skip_ref, gain_ref, *rest
):
    outs, (dt_ref, spans, small_sems, x_sems) = rest[:-4], rest[-4:]
    requests, heads_here, span = dt_ref.shape
    pairs = (
        (spans_hbm, spans), (dt_hbm, dt_ref), (bias_hbm, bias_ref), (alog_hbm, alog_ref), (skip_hbm, skip_ref),
        (gain_hbm, gain_ref),
    )
    small = [pltpu.make_async_copy(source, target, small_sems.at[i]) for i, (source, target) in enumerate(pairs)]
    large = []
    for i, group in enumerate(order):
        lanes = pl.ds(group * GROUP_LANES, GROUP_LANES)
        large.append(pltpu.make_async_copy(x_hbm.at[:, :, lanes], x_ref.at[:, :, lanes], x_sems.at[i]))
    for copy in small + large:
        copy.start()
    for i in range(3):
        info[i] = ids[i]
    for copy in small:
        copy.wait()
    rows = lax.broadcasted_iota(jnp.int32, (span, span), 0)
    cols = lax.broadcasted_iota(jnp.int32, (span, span), 1)
    lower = (rows >= cols).astype(F32)
    rate = -jnp.exp(alog_ref[...])
    for r in range(requests):
        blocks = spans[ids[1] * requests + r]
        live = (ids[0] < blocks).astype(jnp.int32)
        info[3 + r] = live
        info[3 + requests + r] = blocks
        step = softplus(dt_ref[r].astype(F32).T + bias_ref[...]) * live.astype(F32)
        cum = jnp.dot(lower, rate * step, precision=lax.Precision.HIGHEST, preferred_element_type=F32)
        weight = jnp.exp(cum[span - 1 : span, :] - cum) * step
        growth = jnp.exp(cum)
        cum_t = cum.T
        step_t = step.T
        for g in range(heads_here // PER_GROUP):
            here = slice(g * PER_GROUP, (g + 1) * PER_GROUP)
            cum_ref[r, g] = cum[:, here]
            weight_ref[r, g] = weight[:, here]
            growth_ref[r, g] = growth[:, here]
            cum_t_ref[r, g] = cum_t[here, :]
            step_t_ref[r, g] = step_t[here, :]
    large[0].wait()
    block_body(order[0], x_ref, b_ref, weight_ref, *outs)
    for copy in large[1:]:
        copy.wait()


def decay_body(info, dt_ref, bias_ref, alog_ref, out_ref):
    requests = out_ref.shape[1]
    heads_here = dt_ref.shape[1]
    toks = dt_ref.shape[0] // requests
    width = out_ref.shape[-1]
    me = info[0]
    rate = -jnp.exp(alog_ref[...])

    def add(n, sums):
        t = me ^ n
        totals = []
        for r in range(requests):
            step = softplus(dt_ref[n * requests + r].astype(F32).T + bias_ref[...])
            live = (t < info[3 + requests + r]).astype(F32)
            totals.append(jnp.sum(step, axis=0, keepdims=True) * (rate * live))
        total = jnp.concatenate(totals, axis=0)
        return tuple(
            held + total * chosen.astype(F32) for held, chosen in zip(sums, (me == t, me > t, me < t))
        )

    blank = jnp.zeros((requests, heads_here), F32)
    through, before, after = lax.fori_loop(0, toks, add, (blank, blank, blank))
    factors = jnp.exp(jnp.concatenate([through, before, before + through, after], axis=0))
    owner = lax.broadcasted_iota(jnp.int32, (heads_here, width), 1) // HEAD_DIM
    head = lax.broadcasted_iota(jnp.int32, (heads_here, width), 0)
    lanes = jnp.dot(
        factors, (owner == head).astype(F32), precision=lax.Precision.HIGHEST, preferred_element_type=F32
    )
    for kind in range(4):
        for r in range(requests):
            row = kind * requests + r
            out_ref[kind, r] = lanes[row : row + 1]


def block_body(group, x_ref, b_ref, weight_ref, *outs):
    low = low_half(x_ref.shape[1])
    base = group * GROUP_LANES
    for part, out_ref in enumerate(outs):
        for i in range(REQ_CHUNK):
            r = part * REQ_CHUNK + i
            weight = weight_ref[r, group]
            scaled = []
            for q in range(PAIRS):
                here = slice(base + q * PAIR_LANES, base + (q + 1) * PAIR_LANES)
                scaled.append((x_ref[r, :, here].astype(F32) * spread_pair(weight, q, low)).astype(BF16))
            b_here = b_ref[r, :, group * STATE : (group + 1) * STATE]
            states = lax.dot_general(
                b_here, jnp.concatenate(scaled, axis=1), (((0,), (0,)), ((), ())), preferred_element_type=F32
            )
            out_ref[i] = states.astype(BF16)


def local_body(group, info, x_ref, b_ref, c_ref, cum_ref, cum_t_ref, step_t_ref, skip_ref, z_hbm, out_ref, z_ref, sem):
    requests, span = x_ref.shape[:2]
    z_copy = pltpu.make_async_copy(z_hbm.at[:, :, pl.ds(group * GROUP_LANES, GROUP_LANES)], z_ref, sem)
    z_copy.start()
    base = group * GROUP_LANES

    @pl.loop(0, requests)
    def _(r):
        @pl.when(info[3 + r] > 0)
        def _():
            rows = lax.broadcasted_iota(jnp.int32, (span, span), 0)
            cols = lax.broadcasted_iota(jnp.int32, (span, span), 1)
            causal = rows >= cols
            low = low_half(span)
            state = slice(group * STATE, (group + 1) * STATE)
            scores = lax.dot_general(
                c_ref[r, :, state], b_ref[r, :, state], (((1,), (1,)), ((), ())), preferred_element_type=F32
            )
            cum = cum_ref[r, group]
            cum_t = cum_t_ref[r, group]
            step_t = step_t_ref[r, group]

            def mix(h):
                apart = cum[:, h : h + 1] - cum_t[h : h + 1, :]
                decay = jnp.exp(jnp.where(causal, apart, -jnp.inf))
                return (scores * decay * step_t[h : h + 1, :]).astype(BF16)

            for q in range(PAIRS):
                here = slice(base + q * PAIR_LANES, base + (q + 1) * PAIR_LANES)
                x_pair = x_ref[r, :, here]
                nothing = jnp.zeros_like(x_pair)
                both = jnp.concatenate([jnp.where(low, x_pair, nothing), jnp.where(low, nothing, x_pair)], axis=0)
                blend = jnp.concatenate([mix(2 * q), mix(2 * q + 1)], axis=1)
                diagonal = jnp.dot(blend, both, preferred_element_type=F32)
                first = group * PER_GROUP + 2 * q
                skip = jnp.where(low[:1], skip_ref[:, first : first + 1], skip_ref[:, first + 1 : first + 2])
                out_ref[r, :, pair_lanes(q)] = diagonal + skip * x_pair.astype(F32)

    z_copy.wait()


def parents_body(requests, unit, info, parent, state_dev, state_slot, cache_hbm, *refs):
    pieces, (out_ref, rows, sems) = refs[:-3], refs[-3:]
    holders = len(pieces) + 1
    places = []
    for r in range(requests):
        kept = parent[info[1] * requests + r]
        places.append((lax.rem(info[2] - state_dev[kept] + holders, holders), state_slot[kept]))

    def own(r, do):
        shift, slot = places[r]

        @pl.when(shift == 0)
        def _():
            do(pltpu.make_async_copy(cache_hbm.at[slot, info[2]], rows.at[r], sems.at[r]))

    for r in range(requests):
        own(r, lambda copy: copy.start())
    for r in range(requests):
        shift, slot = places[r]
        for n, piece in enumerate(pieces):

            @pl.when(shift == n + 1)
            def _(r=r, slot=slot, piece=piece):
                out_ref[r] = piece[slot].T

        own(r, lambda copy: copy.wait())

        @pl.when(shift == 0)
        def _(r=r):
            out_ref[r] = rows[r].astype(BF16).T


def chain_lanes(group, device, unit):
    first = device * unit
    if first // GROUP_LANES != group:
        return None
    low = first % GROUP_LANES
    return slice(low, low + unit)


def shards(
    x_in, z_in, b_in, c_in, dt_in, dt_bias, a_log, skip_gain, norm_w, cache_states, parent, state_dev, state_slot, spans
):
    me = lax.axis_index("tok")
    toks = lax.axis_size("tok")
    holders = lax.axis_size("cache")
    requests, span, width = x_in.shape
    heads_here = dt_in.shape[2]
    groups = width // GROUP_LANES
    parts = requests // REQ_CHUNK
    chunks = groups * parts
    unit = width // toks
    order = [(i + 1) % groups for i in range(groups)]
    where = {group: i for i, group in enumerate(order)}
    assert span == SPAN and GROUP_LANES % unit == 0

    ids = jnp.stack([me, lax.axis_index("rep"), lax.axis_index("cache")]).astype(jnp.int32)


    slots_here = cache_states.shape[0]
    pieces = []
    for shift in range(1, holders):
        towards = lax.rem(lax.axis_index("cache") + shift, holders)
        piece = lax.dynamic_index_in_dim(cache_states, towards, 1, keepdims=False).astype(BF16)
        piece = lax.ppermute(piece, "cache", [(i, (i + shift) % holders) for i in range(holders)])
        pieces.append(pin(piece.reshape(slots_here, unit, STATE)))
    dt_t = dt_in.transpose(0, 2, 1)
    all_dt, step = dt_t, 1
    while step < toks:
        other = lax.ppermute(all_dt, "tok", [(k, k ^ step) for k in range(toks)])
        all_dt = jnp.concatenate([all_dt, other], axis=0)
        step *= 2

    b_flat = pin(b_in.reshape(requests, span, groups * STATE))
    c_flat = pin(c_in.reshape(requests, span, groups * STATE))
    columns = VMEM((requests, groups, span, PER_GROUP), F32)
    as_rows = VMEM((requests, groups, PER_GROUP, span), F32)
    chunk_type = ((REQ_CHUNK, STATE, GROUP_LANES), BF16)
    smem_spec, vmem_spec, any_spec, hbm_spec = (
        pl.BlockSpec(memory_space=space) for space in (SMEM, VMEM, pl.ANY, pltpu.HBM)
    )
    info, cum, cum_t, step_t, weight, growth, x_in, bias, rates, skip, gain, *found = pl.pallas_call(
        lambda *refs: front_body(order, *refs[:10], *refs[11:]),
        out_shape=(
            jax.ShapeDtypeStruct((3 + 2 * requests,), jnp.int32),
            columns, as_rows, as_rows, columns, columns, VMEM(x_in.shape, BF16),
            *(VMEM((1, heads_here), F32),) * 3, VMEM((1, width), F32), *(VMEM(*chunk_type),) * parts,
        ),
        in_specs=[smem_spec] + [vmem_spec] * 2 + [hbm_spec] * 7 + [vmem_spec],
        out_specs=(smem_spec,) + (vmem_spec,) * (10 + parts),
        scratch_shapes=[
            VMEM(dt_t.shape, BF16), SMEM(spans.shape, jnp.int32),
            pltpu.SemaphoreType.DMA((6,)), pltpu.SemaphoreType.DMA((groups,)),
        ],
        compiler_params=pltpu.CompilerParams(vmem_limit_bytes=12 << 20),
        cost_estimate=pl.CostEstimate(flops=1_000, bytes_accessed=1_000, transcendentals=0),
        name="front",
    )(
        ids,
        b_flat,
        c_flat,
        *map(in_hbm, (spans, dt_t, dt_bias[None], a_log[None], skip_gain[None], norm_w[None], x_in)),
        pin(all_dt),
    )
    states = {part: found[part] for part in range(parts)}
    previous = found[-1]

    for i in range(1, groups):
        found = call(
            functools.partial(block_body, order[i]),
            (chunk_type,) * parts,
            (x_in, b_flat, weight),
            after=(previous,),
            name="block_states",
        )
        for part in range(parts):
            states[i * parts + part] = found[part]
        previous = found[-1]

    initial = pl.pallas_call(
        lambda *refs: parents_body(requests, unit, *refs[: 5 + len(pieces)], *refs[6 + len(pieces) :]),
        out_shape=VMEM((requests, STATE, unit), BF16),
        in_specs=[smem_spec] * 4 + [hbm_spec] + [vmem_spec] * (len(pieces) + 1),
        out_specs=vmem_spec,
        scratch_shapes=[VMEM((requests, unit, STATE), F32), pltpu.SemaphoreType.DMA((requests,))],
        compiler_params=pltpu.CompilerParams(vmem_limit_bytes=12 << 20),
        cost_estimate=pl.CostEstimate(flops=1_000, bytes_accessed=1_000, transcendentals=0),
        name="parents",
    )(info, parent, state_dev, state_slot, in_hbm(cache_states.reshape(slots_here, holders, unit, STATE)), *pieces, pin(previous))
    decays = call(
        decay_body,
        ((4, requests, 1, width), F32),
        (all_dt, bias, rates),
        scalars=(info,),
        after=(initial,),
        name="decays",
    )

    def decay_of(decays_ref, kind, r, group, lanes=slice(0, GROUP_LANES)):
        return decays_ref[kind, r, :, group * GROUP_LANES + lanes.start : group * GROUP_LANES + lanes.stop]

    received, arrived = {}, []

    def pass_on(h, after):
        devices = [k for k in range(toks - 1) if 0 <= h - HOP * k < chunks]
        if devices == [0] and chain_lanes(order[h // parts], 0, unit) is None:
            return states[h]
        incoming = [received[h - HOP]] if any(devices) else []
        ins = [states[h - HOP * k] for k in devices] + incoming + [decays, initial]

        def body(ids_ref, *refs):
            state_refs, incoming_refs = refs[: len(devices)], refs[len(devices) : -3]
            decays_ref, initial_ref, out_ref = refs[-3:]

            def branch(n, device):
                c = h - HOP * device
                group, part = order[c // parts], c % parts
                lanes = chain_lanes(group, device, unit)
                for i in range(REQ_CHUNK):
                    r = part * REQ_CHUNK + i
                    value = state_refs[n][i].astype(F32)
                    if device:
                        value = value + decay_of(decays_ref, THROUGH, r, group) * incoming_refs[0][i].astype(F32)
                    out_ref[i] = value.astype(BF16)
                    if lanes is not None:
                        mine = decay_of(decays_ref, BEFORE_THROUGH, r, group, lanes) * initial_ref[r].astype(F32)
                        out_ref[i, :, lanes] = (value[:, lanes] + mine).astype(BF16)

            for n, device in enumerate(devices):
                pl.when(ids_ref[0] == device)(functools.partial(branch, n, device))

        return call(body, chunk_type, ins, scalars=(info,), after=after, name="pass_on")

    def send_up(h, after=()):
        sent = pass_on(h, after)
        pairs = [(k, k + 1) for k in range(toks - 1) if 0 <= h - HOP * k < chunks]
        received[h] = lax.ppermute(sent, "tok", pairs)
        return sent

    backward = [(k, k - 1) for k in range(1, toks)]

    def send_down(s, after=()):
        sent = initial
        if s:
            used = sorted(
                {where[(s - toks + k) * unit // GROUP_LANES] for k in range(1, toks) if s - toks + k >= 0}
            )
            wanted = [i * parts + part for i in used for part in range(parts)]

            def body(ids_ref, decays_ref, incoming_ref, *refs):
                state_refs, out_ref = refs[:-1], refs[-1]

                def branch(device):
                    target = s - toks + device
                    if target < 0:
                        out_ref[...] = incoming_ref[...]
                        return
                    first = target * unit
                    group, low = first // GROUP_LANES, first % GROUP_LANES
                    lanes = slice(low, low + unit)
                    for r in range(requests):
                        chunk = wanted.index(where[group] * parts + r // REQ_CHUNK)
                        state = state_refs[chunk][r % REQ_CHUNK, :, lanes].astype(F32)
                        later = decay_of(decays_ref, AFTER, r, group, lanes) * state
                        if device < toks - 1:
                            later = later + incoming_ref[r].astype(F32)
                        out_ref[r] = later.astype(BF16)

                on_device(ids_ref[0], toks, branch)

            sent = call(
                body,
                ((requests, STATE, unit), BF16),
                [decays, arrived[-1]] + [states[c] for c in wanted],
                scalars=(info,),
                after=after,
                name="pass_down",
            )
        arrived.append(lax.ppermute(sent, "tok", backward))
        return sent

    def local_sums(i, after):
        ins = (x_in, b_flat, c_flat, cum, cum_t, step_t, skip)
        n_ins, n_after = len(ins), len(after)
        return pl.pallas_call(
            lambda *refs: local_body(order[i], *refs[: 1 + n_ins], refs[1 + n_ins], *refs[2 + n_ins + n_after :]),
            out_shape=(VMEM((requests, span, GROUP_LANES), F32), VMEM((requests, span, GROUP_LANES), BF16)),
            in_specs=[smem_spec] + [vmem_spec] * n_ins + [hbm_spec] + [vmem_spec] * n_after,
            out_specs=(vmem_spec, vmem_spec),
            scratch_shapes=[pltpu.SemaphoreType.DMA],
            compiler_params=pltpu.CompilerParams(vmem_limit_bytes=12 << 20),
            cost_estimate=pl.CostEstimate(flops=1_000, bytes_accessed=1_000, transcendentals=0),
            name="local_sums",
        )(info, *(pin(a) for a in ins), in_hbm(z_in), *(pin(a) for a in after))

    def init_for(group):
        if unit == GROUP_LANES:
            inits = [initial] + arrived[:group]
            return inits, [group - k if k <= group else None for k in range(toks)]
        stacked = jnp.stack([initial] + arrived[: toks - 1])[lax.rem(jnp.arange(toks) - me + toks, toks)]
        full = stacked.transpose(1, 2, 0, 3).reshape(requests, STATE, width)
        return [full[:, :, group * GROUP_LANES : (group + 1) * GROUP_LANES]], [0] * toks

    def finish(i, these, y_so_far, after):
        group = order[i]
        inits, init_of = init_for(group)
        ahead = [received[i * parts + part + HOP * k] for part in these for k in range(toks - 1)]
        ins = [*local[i], c_flat, growth, gain, decays, *ahead, *inits]
        n_ahead, n_init = len(ahead), len(inits)
        had = y_so_far is not None
        count = len(these) * REQ_CHUNK

        def body(info_ref, *refs):
            local_ref, z_ref, c_ref, growth_ref, gain_ref, decays_ref = refs[:6]
            ahead_refs, init_refs = refs[6 : 6 + n_ahead], refs[6 + n_ahead : 6 + n_ahead + n_init]
            y_ref, token_ref, state_buf, y_buf, sems = refs[-5:]
            token_ref[...] = jnp.zeros_like(token_ref)

            def merge(device):
                for n, part in enumerate(these):
                    for j in range(REQ_CHUNK):
                        r = part * REQ_CHUNK + j
                        value = jnp.zeros((STATE, GROUP_LANES), F32)
                        if device:
                            value = ahead_refs[n * (toks - 1) + device - 1][j].astype(F32)
                        if init_of[device] is not None:
                            started = init_refs[init_of[device]][r].astype(F32) * decay_of(decays_ref, BEFORE, r, group)
                            if unit < GROUP_LANES:
                                lane = lax.broadcasted_iota(jnp.int32, (1, GROUP_LANES), 1) + group * GROUP_LANES
                                started = jnp.where(lane >= device * unit, started, 0.0)
                            value = value + started
                        state_buf[n * REQ_CHUNK + j] = value.astype(BF16)

            on_device(info_ref[0], toks, merge)
            copies = []
            for n in range(count):
                r = these[n // REQ_CHUNK] * REQ_CHUNK + n % REQ_CHUNK
                valid = info_ref[3 + r] > 0

                @pl.when(jnp.logical_not(valid))
                def _(n=n):
                    y_buf[n] = jnp.zeros_like(y_buf[n])

                @pl.when(valid)
                def _(n=n, r=r):
                    low = low_half(span)
                    c_here = c_ref[r, :, group * STATE : (group + 1) * STATE]
                    carried = jnp.dot(c_here, state_buf[n], preferred_element_type=F32)
                    grown = growth_ref[r, group]
                    gated = []
                    squares = jnp.zeros((span, PAIR_LANES), F32)
                    for q in range(PAIRS):
                        here = pair_lanes(q)
                        summed = local_ref[r, :, here] + carried[:, here] * spread_pair(grown, q, low)
                        gate = z_ref[r, :, here].astype(F32)
                        value = summed.astype(BF16).astype(F32) * (gate / (1.0 + jnp.exp(-gate)))
                        gated.append(value)
                        squares = squares + value * value
                    inverse = lax.rsqrt(jnp.sum(squares, axis=1, keepdims=True) * (1.0 / GROUP_LANES) + EPS)
                    for q in range(PAIRS):
                        gain = gain_ref[:, group * GROUP_LANES + q * PAIR_LANES : group * GROUP_LANES + (q + 1) * PAIR_LANES]
                        y_buf[n, :, pair_lanes(q)] = (gated[q] * inverse * gain).astype(BF16)

                copy = pltpu.make_async_copy(
                    y_buf.at[n],
                    y_ref.at[r, :, pl.ds(group * GROUP_LANES, GROUP_LANES)],
                    sems.at[n],
                )
                copy.start()
                copies.append(copy)
            for copy in copies:
                copy.wait()

        n_after = len(after)

        def kernel(*refs):
            body(*refs[: 1 + len(ins)], *refs[1 + len(ins) + n_after + had :])

        pinned = [pin(a) for a in (*ins, *after)]
        return pl.pallas_call(
            kernel,
            out_shape=(jax.ShapeDtypeStruct((requests, span, width), BF16), VMEM((8, PAIR_LANES), F32)),
            in_specs=[smem_spec] + [vmem_spec] * len(pinned) + [any_spec] * had,
            out_specs=(any_spec, vmem_spec),
            input_output_aliases={1 + len(pinned): 0} if had else {},
            scratch_shapes=[
                VMEM((count, STATE, GROUP_LANES), BF16),
                VMEM((count, span, GROUP_LANES), BF16),
                pltpu.SemaphoreType.DMA((count,)),
            ],
            compiler_params=pltpu.CompilerParams(vmem_limit_bytes=12 << 20),
            cost_estimate=pl.CostEstimate(flops=1_000, bytes_accessed=1_000, transcendentals=0),
            name="finish",
        )(info, *pinned, *([y_so_far] if had else []))

    def final_states(after):
        ahead = {}
        for k in range(1, toks):
            i = where[k * unit // GROUP_LANES]
            for part in range(parts):
                ahead[k, part] = received[i * parts + part + HOP * (k - 1)]
        keys = list(ahead)
        ins = [decays, initial, arrived[-1], *ahead.values(), *(states[c] for c in range(chunks))]
        n_after = len(after)

        def kernel(ids_ref, *refs):
            decays_ref, initial_ref, later_ref = refs[:3]
            ahead_refs = dict(zip(keys, refs[3 : 3 + len(keys)]))
            state_refs = refs[3 + len(keys) : 3 + len(keys) + chunks]
            final_ref, buf, sems = refs[-3:]

            def branch(device):
                first = device * unit
                group, low = first // GROUP_LANES, first % GROUP_LANES
                lanes = slice(low, low + unit)
                for r in range(requests):
                    part, j = r // REQ_CHUNK, r % REQ_CHUNK
                    value = state_refs[where[group] * parts + part][j, :, lanes].astype(F32)
                    value = value + decay_of(decays_ref, BEFORE_THROUGH, r, group, lanes) * initial_ref[r].astype(F32)
                    if device:
                        through = decay_of(decays_ref, THROUGH, r, group, lanes)
                        value = value + through * ahead_refs[device, part][j, :, lanes].astype(F32)
                    value = value * decay_of(decays_ref, AFTER, r, group, lanes)
                    if device < toks - 1:
                        value = value + later_ref[r].astype(F32)
                    buf[r] = value.T

            on_device(ids_ref[0], toks, branch)
            copies = [pltpu.make_async_copy(buf.at[r], final_ref.at[r], sems.at[r]) for r in range(requests)]
            for copy in copies:
                copy.start()
            for copy in copies:
                copy.wait()

        pinned = [pin(a) for a in (*ins, *after)]
        final = pl.pallas_call(
            kernel,
            out_shape=jax.ShapeDtypeStruct((requests, unit, STATE), F32),
            in_specs=[pl.BlockSpec(memory_space=SMEM)] + [pl.BlockSpec(memory_space=VMEM)] * len(pinned),
            out_specs=pl.BlockSpec(memory_space=pl.ANY),
            scratch_shapes=[VMEM((requests, unit, STATE), F32), pltpu.SemaphoreType.DMA((requests,))],
            compiler_params=pltpu.CompilerParams(vmem_limit_bytes=12 << 20),
            cost_estimate=pl.CostEstimate(flops=1_000, bytes_accessed=1_000, transcendentals=0),
            name="final_states",
        )(info, *pinned)
        return final.reshape(requests, unit // HEAD_DIM, HEAD_DIM, STATE)

    slots = chunks + HOP * (toks - 2)
    lag = HOP * (toks - 2) + parts
    for h in range(HOP):
        send_up(h)
    send_down(0)
    local = {0: local_sums(0, (decays,))}
    previous = local[0][0]
    pending = list(range(1, groups))
    downs = list(range(1, toks))
    y_out, done, final = None, 0, None
    for h in range(HOP, slots):
        previous = send_up(h, (previous,))
        if pending:
            i = pending.pop(0)
            local[i] = local_sums(i, (previous,))
            previous = local[i][0]
        elif done < groups - 1 and done * parts + lag + 1 <= h:
            y_out, previous = finish(done, list(range(parts)), y_out, (previous,))
            done += 1
        if downs and h >= round(HOP + 1 + 2.5 * (toks - 1 - len(downs))):
            previous = send_down(downs.pop(0), (previous,))
    for s in downs:
        previous = send_down(s, (previous,))
    while pending:
        i = pending.pop(0)
        local[i] = local_sums(i, (previous,))
        previous = local[i][0]
    while done < groups - 1:
        y_out, previous = finish(done, list(range(parts)), y_out, (previous,))
        done += 1
    for part in range(parts):
        if part == parts - 1:
            final = final_states((previous,))
        y_out, previous = finish(groups - 1, [part], y_out, (previous,))
    return (y_out, final)


def solution(mesh):
    placed = (
        P(("groups", "rep"), "tok", "cache"),
        P(("groups", "rep"), "tok", "cache"),
        P(("groups", "rep"), "tok", "cache", None),
        P(("groups", "rep"), "tok", "cache", None),
        P(("groups", "rep"), "tok", "cache"),
        P("cache"),
        P("cache"),
        P("cache"),
        P("cache"),
        P(("groups", "cache"), None, "tok", None, None),
        P("groups"),
        P("groups"),
        P("groups"),
        P("groups"),
    )
    return jax.shard_map(
        shards,
        mesh=mesh,
        in_specs=placed,
        out_specs=(
            P(("groups", "rep"), "tok", "cache"),
            P(("groups", "rep"), ("cache", "tok"), None, None),
        ),
        check_vma=False,
    )
```

time: 403 us -> 173 us (0.43); the launches traced: 397 us -> 171 us
  waiting for transfers between devices: 218 us -> 67.9 us
  local copies, waits for them, and re-layouts: 79.3 us -> 3.81 us
  Pallas kernels: 0 us -> 52.2 us
  other arithmetic: 38.7 us -> 1.8 us
  matrix products: 26 us -> 0 us
  starting transfers between devices: 18.6 us -> 44.4 us
  between operations: 15.8 us -> 1.27 us
    all_gather x2 -> x0, waiting for transfers between devices: 96.1 us -> none  [the longest x1 81 us: shards(): lax.all_gather(c_in, 'tok', axis=1, tiled=True)]
    all_to_all x3 -> x0, waiting for transfers between devices: 85.9 us -> none  [the longest x1 83.7 us: shards(): lax.all_to_all(ssd, 'tok', split_axis=1, concat_axis=2, tiled=True)]
    ppermute x0 -> x19, waiting for transfers between devices: none -> 67.9 us  [the longest x12 51.4 us: send_up(): received[h] = lax.ppermute(sent, 'tok', pairs)]
    pallas_call x0 -> x29, Pallas kernels: none -> 52.2 us  [the longest x17 16.4 us: call(): pl.pallas_call(kernel, out_shape=tuple((VMEM(shape, dtype) for shape, dty...]
    ppermute x0 -> x19, starting transfers between devices: none -> 44.4 us  [the longest x12 20.6 us: send_up(): received[h] = lax.ppermute(sent, 'tok', pairs)]
    unnamed x4 -> x0, waiting for transfers between devices: 36.2 us -> none
    unnamed x47 -> x6, local copies, waits for them, and re-layouts: 26.5 us -> 0.02 us
    dot_general x4 -> x0, matrix products: 26 us -> none  [the longest x1 9.13 us: span_scan(): jnp.einsum('mkhij,mkjhp->mkihp', blend_factors, x_blocks, preferred_eleme...]
  transfers between devices with their start and end apart: 6 -> 19, of which waited for: 5 -> 13; matrix products, arithmetic and copies ran while one was open for 8% -> 2% of each run, Pallas kernels for 0% -> 28%
where the time goes in v2:
time: 173 us; the launch traced here: 171 us
  waiting for transfers between devices  67.9 us (39%)
  Pallas kernels  52.2 us (30%)
  starting transfers between devices  44.4 us (26%)
  local copies, waits for them, and re-layouts  3.81 us (2%)
  other arithmetic  1.8 us (1%)
    ppermute x12, waiting for transfers between devices, send_up(): received[h] = lax.ppermute(sent, 'tok', pairs)  51.4 us
    ppermute x12, starting transfers between devices, send_up(): received[h] = lax.ppermute(sent, 'tok', pairs)  20.6 us
    ppermute x4, starting transfers between devices, send_down(): arrived.append(lax.ppermute(sent, 'tok', backward))  20.2 us
    pallas_call x17, Pallas kernels, call(): pl.pallas_call(kernel, out_shape=tuple((VMEM(shape, dtype) for shape, dty...  16.4 us
    pallas_call x5, Pallas kernels, finish(): pl.pallas_call(kernel, out_shape=(jax.ShapeDtypeStruct((requests, span, w...  15.1 us
    ppermute x4, waiting for transfers between devices, send_down(): arrived.append(lax.ppermute(sent, 'tok', backward))  10.6 us
    pallas_call x4, Pallas kernels, local_sums(): pl.pallas_call(lambda *refs: local_body(order[i], *refs[:1 + n_ins], refs...  9.48 us
    pallas_call x1, Pallas kernels, shards(): pl.pallas_call(lambda *refs: front_body(order, *refs[:10], *refs[11:]), o...  6.41 us
  transfers between devices with their start and end apart: 19, of which 13 were waited for; matrix products, arithmetic and copies ran while one was open for 2% of the time, Pallas kernels for 28%

profile of v2, /device:TPU:16, one launch (start us, length us, event | category | flops | bytes accessed | tf_op | source)
XLA Modules:
  0.0 171.4 jit_solution(14362933681778866351)
XLA Ops:
  0.6 1.3 fusion
  2.0 1.6 collective-permute-start.3
  3.5 1.6 collective-permute-start
  5.1 2.9 %collective-permute-done = bf16[4,64,128]{2,1,0:T(8,128)(2,1)S(1)} collective-permute-done((bf16[4,64,128]{2,1,0:T(8,128)(2,1)}, bf16[4,64,128]{2,1,0:T(8,128)(2,1)S(1)}, u32[]{:S(2)}, u32[]{:S(2)}) %collective-permute-start) | collective-permute-done | bytes 65568 | tf_op jit(solution)/shard_map/ppermute | solution.py:295
  9.2 1.2 reshape.21.refs_2_.refs_3_
  10.5 1.2 reshape.20.refs_1_.refs_2_
  11.8 3.1 %collective-permute-done.1 = bf16[8,64,128]{2,1,0:T(8,128)(2,1)S(1)} collective-permute-done((bf16[8,64,128]{2,1,0:T(8,128)(2,1)S(1)}, bf16[8,64,128]{2,1,0:T(8,128)(2,1)S(1)}, u32[]{:S(2)}, u32[]{:S(2)}) %collective-permute-start.1) | collective-permute-done | bytes 131104 | tf_op jit(solution)/shard_map/ppermute | solution.py:295
  15.7 6.4 %front.1 = (s32[11]{0:T(128)S(1)}, f32[4,4,128,16]{3,2,1,0:T(8,128)S(1)}, f32[4,4,16,128]{3,2,1,0:T(8,128)S(1)}, f32[4,4,16,128]{3,2,1,0:T(8,128)S(1)}, f32[4,4,...) custom-call(s32[3]{0:T(128)S(1)} %pad_add_fusion.refs_0_, ...), custom_call_target="tpu_custom_call" | custom-call | flops 1000 | bytes 1000 | tf_op jit(solution)/shard_map/front/pallas_call | solution.py:307
  22.2 1.6 block_states.3
  23.8 1.6 block_states.4
  25.4 1.6 block_states.5
  27.1 2.1 %parents.1.refs_4_.refs_5_.refs_6_.refs_13_.refs_10_.refs_1_ = bf16[4,128,1024]{2,1,0:T(8,128)(2,1)S(1)} custom-call(s32[11]{0:T(128)S(1)} %get-tuple-element.38.refs_0_.ids_ref, s32[8]{0:T(128)S(1)} %copy-done, s32[4]{0:T(128)S(1)} %copy-done.1, s32[4]{0:T(128)S(1)} %copy-done.2, f32[2,2,1024,128]{3,2,1,0:T(8,128)} %bitcast.14, ...), custom_call_target="tpu_custom_call" | custom-call | flops 1000 | bytes 1000 | tf_op jit(solution)/shard_map/parents/pallas_call | solution.py:345
  29.2 3.3 %collective-permute-start.5 = (bf16[4,128,1024]{2,1,0:T(8,128)(2,1)S(1)}, bf16[4,128,1024]{2,1,0:T(8,128)(2,1)S(1)}, u32[]{:S(2)}, u32[]{:S(2)}) collective-permute-start(bf16[4,128,1024]{2,1,0:T(8,128)(2,1)S(1)} %parents.1.refs_4_.refs_5_.refs_6_.refs_13_.refs_10_.refs_1_), channel_id=1, source_target_pairs={{4,0},{8,4},{12,8},{5,1},{9,5},{13,9},{6,2},{10,6},{14,10},{7,3},{... | collective-permute-start | bytes 3145736 | tf_op jit(solution)/shard_map/ppermute | solution.py:444
  33.9 2.0 %decays.1.refs_9_.refs_4_.refs_1_.refs_5_.refs_6_.refs_3_.refs_0_ = f32[4,4,1,4096]{3,2,1,0:T(1,128)S(1)} custom-call(s32[11]{0:T(128)S(1)} %get-tuple-element.38.refs_0_.ids_ref, bf16[16,64,128]{2,1,0:T(8,128)(2,1)S(1)} %pad_maximum_fusion.refs_10_.refs_1_, f32[1,64]{1,0:T(1,128)S(1)} %get-tuple-element.50.refs_2_, f32[1,64]{1,0:T(1,128)S(1)} %get-tuple-element.51.refs_3_, ...), custom_call_target="tpu_custom_call" | custom-call | flops 1000 | bytes 1000 | tf_op jit(solution)/shard_map/decays/pallas_call | solution.py:50
  36.0 2.4 %local_sums.4 = (f32[4,128,1024]{2,1,0:T(8,128)S(1)}, bf16[4,128,1024]{2,1,0:T(8,128)(2,1)S(1)}) custom-call(s32[11]{0:T(128)S(1)} %get-tuple-element.38.refs_0_.ids_ref, bf16[4,128,4096]{2,1,0:T(8,128)(2,1)S(1)} %get-tuple-element.39.refs_0_.refs_1_, bf16[4,128,512]{2,1,0:T(8,128)(2,1)S(1)} %reshape.20.refs_1_.refs_2_, ...), custom_call_target="tpu_custom_call" | custom-call | flops 1000 | bytes 1000 | tf_op jit(solution)/shard_map/local_sums/pallas_call | solution.py:450
  38.9 2.4 %local_sums.5 = (f32[4,128,1024]{2,1,0:T(8,128)S(1)}, bf16[4,128,1024]{2,1,0:T(8,128)(2,1)S(1)}) custom-call(s32[11]{0:T(128)S(1)} %get-tuple-element.38.refs_0_.ids_ref, bf16[4,128,4096]{2,1,0:T(8,128)(2,1)S(1)} %get-tuple-element.39.refs_0_.refs_1_, bf16[4,128,512]{2,1,0:T(8,128)(2,1)S(1)} %reshape.20.refs_1_.refs_2_, ...), custom_call_target="tpu_custom_call" | custom-call | flops 1000 | bytes 1000 | tf_op jit(solution)/shard_map/local_sums/pallas_call | solution.py:450
  41.9 1.3 collective-permute-start.4
  43.2 2.4 %local_sums.6 = (f32[4,128,1024]{2,1,0:T(8,128)S(1)}, bf16[4,128,1024]{2,1,0:T(8,128)(2,1)S(1)}) custom-call(s32[11]{0:T(128)S(1)} %get-tuple-element.38.refs_0_.ids_ref, bf16[4,128,4096]{2,1,0:T(8,128)(2,1)S(1)} %get-tuple-element.39.refs_0_.refs_1_, bf16[4,128,512]{2,1,0:T(8,128)(2,1)S(1)} %reshape.20.refs_1_.refs_2_, ...), custom_call_target="tpu_custom_call" | custom-call | flops 1000 | bytes 1000 | tf_op jit(solution)/shard_map/local_sums/pallas_call | solution.py:450
  45.5 10.6 %collective-permute-done.5.refs_2_.refs_14_ = bf16[4,128,1024]{2,1,0:T(8,128)(2,1)S(1)} collective-permute-done((bf16[4,128,1024]{2,1,0:T(8,128)(2,1)S(1)}, bf16[4,128,1024]{2,1,0:T(8,128)(2,1)S(1)}, u32[]{:S(2)}, u32[]{:S(2)}) %collective-permute-start.5) | collective-permute-done | bytes 1048608 | tf_op jit(solution)/shard_map/ppermute | solution.py:444
  56.9 9.4 %collective-permute-start.9 = (bf16[4,128,1024]{2,1,0:T(8,128)(2,1)S(1)}, bf16[4,128,1024]{2,1,0:T(8,128)(2,1)S(1)}, u32[]{:S(2)}, u32[]{:S(2)}) collective-permute-start(bf16[4,128,1024]{2,1,0:T(8,128)(2,1)S(1)} %pass_down.3.refs_7_), channel_id=1, source_target_pairs={{4,0},{8,4},{12,8},{5,1},{9,5},{13,9},{6,2},{10,6},{14,10},{7,3},{... | collective-permute-start | bytes 3145736 | tf_op jit(solution)/shard_map/ppermute | solution.py:444
  66.4 1.3 collective-permute-start.7
  67.7 4.4 %collective-permute-done.4.refs_4_.refs_8_.refs_7_ = bf16[2,128,1024]{2,1,0:T(8,128)(2,1)S(1)} collective-permute-done((bf16[2,128,1024]{2,1,0:T(8,128)(2,1)S(1)}, bf16[2,128,1024]{2,1,0:T(8,128)(2,1)S(1)}, u32[]{:S(2)}, u32[]{:S(2)}) %collective-permute-start.4) | collective-permute-done | bytes 524320 | tf_op jit(solution)/shard_map/ppermute | solution.py:402
  72.8 1.9 %collective-permute-start.10 = (bf16[2,128,1024]{2,1,0:T(8,128)(2,1)S(1)}, bf16[2,128,1024]{2,1,0:T(8,128)(2,1)S(1)}, u32[]{:S(2)}, u32[]{:S(2)}) collective-permute-start(bf16[2,128,1024]{2,1,0:T(8,128)(2,1)S(1)} %pass_on.12.refs_9_), channel_id=1, source_target_pairs={{0,4},{4,8},{8,12},{1,5},{5,9},{9,13},{2,6},{6,10},{10,14},{3,7},{... | collective-permute-start | bytes 1572872 | tf_op jit(solution)/shard_map/ppermute | solution.py:402
  74.7 2.4 %local_sums.7 = (f32[4,128,1024]{2,1,0:T(8,128)S(1)}, bf16[4,128,1024]{2,1,0:T(8,128)(2,1)S(1)}) custom-call(s32[11]{0:T(128)S(1)} %get-tuple-element.38.refs_0_.ids_ref, bf16[4,128,4096]{2,1,0:T(8,128)(2,1)S(1)} %get-tuple-element.39.refs_0_.refs_1_, bf16[4,128,512]{2,1,0:T(8,128)(2,1)S(1)} %reshape.20.refs_1_.refs_2_, ...), custom_call_target="tpu_custom_call" | custom-call | flops 1000 | bytes 1000 | tf_op jit(solution)/shard_map/local_sums/pallas_call | solution.py:450
  77.1 6.6 %collective-permute-done.7.refs_4_.refs_11_.refs_10_ = bf16[2,128,1024]{2,1,0:T(8,128)(2,1)S(1)} collective-permute-done((bf16[2,128,1024]{2,1,0:T(8,128)(2,1)S(1)}, bf16[2,128,1024]{2,1,0:T(8,128)(2,1)S(1)}, u32[]{:S(2)}, u32[]{:S(2)}) %collective-permute-start.7) | collective-permute-done | bytes 524320 | tf_op jit(solution)/shard_map/ppermute | solution.py:402
  84.4 1.9 %collective-permute-start.8 = (bf16[2,128,1024]{2,1,0:T(8,128)(2,1)S(1)}, bf16[2,128,1024]{2,1,0:T(8,128)(2,1)S(1)}, u32[]{:S(2)}, u32[]{:S(2)}) collective-permute-start(bf16[2,128,1024]{2,1,0:T(8,128)(2,1)S(1)} %pass_on.13.refs_7_), channel_id=1, source_target_pairs={{0,4},{4,8},{8,12},{1,5},{5,9},{9,13},{2,6},{6,10},{10,14},{3,7},{... | collective-permute-start | bytes 1572872 | tf_op jit(solution)/shard_map/ppermute | solution.py:402
  86.4 8.6 %collective-permute-done.10.refs_4_.refs_9_.refs_8_.refs_7_.refs_5_ = bf16[2,128,1024]{2,1,0:T(8,128)(2,1)S(1)} collective-permute-done((bf16[2,128,1024]{2,1,0:T(8,128)(2,1)S(1)}, bf16[2,128,1024]{2,1,0:T(8,128)(2,1)S(1)}, u32[]{:S(2)}, u32[]{:S(2)}) %collective-permute-start.10) | collective-permute-done | bytes 524320 | tf_op jit(solution)/shard_map/ppermute | solution.py:402
  96.7 3.6 %collective-permute-start.12 = (bf16[4,128,1024]{2,1,0:T(8,128)(2,1)S(1)}, bf16[4,128,1024]{2,1,0:T(8,128)(2,1)S(1)}, u32[]{:S(2)}, u32[]{:S(2)}) collective-permute-start(bf16[4,128,1024]{2,1,0:T(8,128)(2,1)S(1)} %pass_down.4.refs_7_), channel_id=1, source_target_pairs={{4,0},{8,4},{12,8},{5,1},{9,5},{13,9},{6,2},{10,6},{14,10},{7,3},{... | collective-permute-start | bytes 3145736 | tf_op jit(solution)/shard_map/ppermute | solution.py:444
  100.3 2.3 %collective-permute-start.13 = (bf16[2,128,1024]{2,1,0:T(8,128)(2,1)S(1)}, bf16[2,128,1024]{2,1,0:T(8,128)(2,1)S(1)}, u32[]{:S(2)}, u32[]{:S(2)}) collective-permute-start(bf16[2,128,1024]{2,1,0:T(8,128)(2,1)S(1)} %pass_on.14.refs_7_), channel_id=1, source_target_pairs={{0,4},{4,8},{8,12},{1,5},{5,9},{9,13},{2,6},{6,10},{10,14},{3,7},{... | collective-permute-start | bytes 1572872 | tf_op jit(solution)/shard_map/ppermute | solution.py:402
  102.6 3.6 %collective-permute-done.8.refs_4_.refs_12_.refs_11_.refs_10_.refs_6_ = bf16[2,128,1024]{2,1,0:T(8,128)(2,1)S(1)} collective-permute-done((bf16[2,128,1024]{2,1,0:T(8,128)(2,1)S(1)}, bf16[2,128,1024]{2,1,0:T(8,128)(2,1)S(1)}, u32[]{:S(2)}, u32[]{:S(2)}) %collective-permute-start.8) | collective-permute-done | bytes 524320 | tf_op jit(solution)/shard_map/ppermute | solution.py:402
  107.0 1.9 %collective-permute-start.11 = (bf16[2,128,1024]{2,1,0:T(8,128)(2,1)S(1)}, bf16[2,128,1024]{2,1,0:T(8,128)(2,1)S(1)}, u32[]{:S(2)}, u32[]{:S(2)}) collective-permute-start(bf16[2,128,1024]{2,1,0:T(8,128)(2,1)S(1)} %pass_on.15.refs_15_), channel_id=1, source_target_pairs={{0,4},{4,8},{8,12},{1,5},{5,9},{9,13},{2,6},{6,10},{10,14},{3,7},{... | collective-permute-start | bytes 1572872 | tf_op jit(solution)/shard_map/ppermute | solution.py:402
  109.0 3.1 %finish.5 = (bf16[4,128,4096]{2,1,0:T(8,128)(2,1)}, f32[8,128]{1,0:T(8,128)S(1)}) custom-call(s32[11]{0:T(128)S(1)} %get-tuple-element.38.refs_0_.ids_ref, f32[4,128,1024]{2,1,0:T(8,128)S(1)} %get-tuple-element.54.refs_6_.refs_1_, bf16[4,128,1024]{2,1,0:T(8,128)(2,1)S(1)} %get-tuple-element.62.refs_2_, bf16[4,128,512]{2,1,0:T(8,128)(2,1)S(1)} %reshape.21.refs_2_.refs_3_, ...), custom_call_target="tpu_custom_call" | custom-call | flops 1000 | bytes 1000 | tf_op jit(solution)/shard_map/finish/pallas_call | solution.py:545
  112.1 5.3 %collective-permute-done.13.refs_3_.refs_9_.refs_8_.refs_7_ = bf16[2,128,1024]{2,1,0:T(8,128)(2,1)S(1)} collective-permute-done((bf16[2,128,1024]{2,1,0:T(8,128)(2,1)S(1)}, bf16[2,128,1024]{2,1,0:T(8,128)(2,1)S(1)}, u32[]{:S(2)}, u32[]{:S(2)}) %collective-permute-start.13) | collective-permute-done | bytes 524320 | tf_op jit(solution)/shard_map/ppermute | solution.py:402
  118.1 1.9 %collective-permute-start.15 = (bf16[2,128,1024]{2,1,0:T(8,128)(2,1)S(1)}, bf16[2,128,1024]{2,1,0:T(8,128)(2,1)S(1)}, u32[]{:S(2)}, u32[]{:S(2)}) collective-permute-start(bf16[2,128,1024]{2,1,0:T(8,128)(2,1)S(1)} %pass_on.16.refs_9_), channel_id=1, source_target_pairs={{4,8},{8,12},{5,9},{9,13},{6,10},{10,14},{7,11},{11,15},{20,24},{2... | collective-permute-start | bytes 1572872 | tf_op jit(solution)/shard_map/ppermute | solution.py:402
  121.0 7.7 %collective-permute-done.11.refs_3_.refs_12_.refs_11_.refs_7_ = bf16[2,128,1024]{2,1,0:T(8,128)(2,1)S(1)} collective-permute-done((bf16[2,128,1024]{2,1,0:T(8,128)(2,1)S(1)}, bf16[2,128,1024]{2,1,0:T(8,128)(2,1)S(1)}, u32[]{:S(2)}, u32[]{:S(2)}) %collective-permute-start.11) | collective-permute-done | bytes 524320 | tf_op jit(solution)/shard_map/ppermute | solution.py:402
  129.4 1.9 %collective-permute-start.14 = (bf16[2,128,1024]{2,1,0:T(8,128)(2,1)S(1)}, bf16[2,128,1024]{2,1,0:T(8,128)(2,1)S(1)}, u32[]{:S(2)}, u32[]{:S(2)}) collective-permute-start(bf16[2,128,1024]{2,1,0:T(8,128)(2,1)S(1)} %pass_on.17.refs_16_), channel_id=1, source_target_pairs={{4,8},{8,12},{5,9},{9,13},{6,10},{10,14},{7,11},{11,15},{20,24},{2... | collective-permute-start | bytes 1572872 | tf_op jit(solution)/shard_map/ppermute | solution.py:402
  131.3 4.0 %collective-permute-start.18 = (bf16[4,128,1024]{2,1,0:T(8,128)(2,1)S(1)}, bf16[4,128,1024]{2,1,0:T(8,128)(2,1)S(1)}, u32[]{:S(2)}, u32[]{:S(2)}) collective-permute-start(bf16[4,128,1024]{2,1,0:T(8,128)(2,1)S(1)} %pass_down.5.refs_6_), channel_id=1, source_target_pairs={{4,0},{8,4},{12,8},{5,1},{9,5},{13,9},{6,2},{10,6},{14,10},{7,3},{... | collective-permute-start | bytes 3145736 | tf_op jit(solution)/shard_map/ppermute | solution.py:444
  135.3 3.6 %finish.6 = (bf16[4,128,4096]{2,1,0:T(8,128)(2,1)}, f32[8,128]{1,0:T(8,128)S(1)}) custom-call(s32[11]{0:T(128)S(1)} %get-tuple-element.38.refs_0_.ids_ref, f32[4,128,1024]{2,1,0:T(8,128)S(1)} %get-tuple-element.56.refs_6_.refs_1_, bf16[4,128,1024]{2,1,0:T(8,128)(2,1)S(1)} %get-tuple-element.64.refs_2_, ...), custom_call_target="tpu_custom_call", output_to_operand_aliasing={{0}: (17, {})} | custom-call | flops 1000 | bytes 1000 | tf_op jit(solution)/shard_map/finish/pallas_call | solution.py:545
  138.9 1.0 collective-permute-done.15.refs_2_.refs_9_.refs_8_.refs_7_
  140.6 1.3 collective-permute-start.17
  141.9 6.7 %collective-permute-done.14.refs_2_.refs_12_.refs_8_ = bf16[2,128,1024]{2,1,0:T(8,128)(2,1)S(1)} collective-permute-done((bf16[2,128,1024]{2,1,0:T(8,128)(2,1)S(1)}, bf16[2,128,1024]{2,1,0:T(8,128)(2,1)S(1)}, u32[]{:S(2)}, u32[]{:S(2)}) %collective-permute-start.14) | collective-permute-done | bytes 524320 | tf_op jit(solution)/shard_map/ppermute | solution.py:402
  149.4 3.4 %collective-permute-start.16 = (bf16[2,128,1024]{2,1,0:T(8,128)(2,1)S(1)}, bf16[2,128,1024]{2,1,0:T(8,128)(2,1)S(1)}, u32[]{:S(2)}, u32[]{:S(2)}) collective-permute-start(bf16[2,128,1024]{2,1,0:T(8,128)(2,1)S(1)} %pass_on.19.refs_17_), channel_id=1, source_target_pairs={{8,12},{9,13},{10,14},{11,15},{24,28},{25,29},{26,30},{27,31}} | collective-permute-start | bytes 1572872 | tf_op jit(solution)/shard_map/ppermute | solution.py:402
  152.8 3.4 %finish.7 = (bf16[4,128,4096]{2,1,0:T(8,128)(2,1)}, f32[8,128]{1,0:T(8,128)S(1)}) custom-call(s32[11]{0:T(128)S(1)} %get-tuple-element.38.refs_0_.ids_ref, f32[4,128,1024]{2,1,0:T(8,128)S(1)} %get-tuple-element.57.refs_5_.refs_1_, bf16[4,128,1024]{2,1,0:T(8,128)(2,1)S(1)} %get-tuple-element.67.refs_2_, ...), custom_call_target="tpu_custom_call", output_to_operand_aliasing={{0}: (18, {})} | custom-call | flops 1000 | bytes 1000 | tf_op jit(solution)/shard_map/finish/pallas_call | solution.py:545
  156.1 2.9 %collective-permute-done.17.refs_9_ = bf16[2,128,1024]{2,1,0:T(8,128)(2,1)S(1)} collective-permute-done((bf16[2,128,1024]{2,1,0:T(8,128)(2,1)S(1)}, bf16[2,128,1024]{2,1,0:T(8,128)(2,1)S(1)}, u32[]{:S(2)}, u32[]{:S(2)}) %collective-permute-start.17) | collective-permute-done | bytes 524320 | tf_op jit(solution)/shard_map/ppermute | solution.py:402
  159.0 1.9 %finish.8 = (bf16[4,128,4096]{2,1,0:T(8,128)(2,1)}, f32[8,128]{1,0:T(8,128)S(1)}) custom-call(s32[11]{0:T(128)S(1)} %get-tuple-element.38.refs_0_.ids_ref, f32[4,128,1024]{2,1,0:T(8,128)S(1)} %get-tuple-element.58.refs_7_.refs_1_, bf16[4,128,1024]{2,1,0:T(8,128)(2,1)S(1)} %get-tuple-element.59.refs_2_, ...), custom_call_target="tpu_custom_call", output_to_operand_aliasing={{0}: (12, {})} | custom-call | flops 1000 | bytes 1000 | tf_op jit(solution)/shard_map/finish/pallas_call | solution.py:545
  160.9 4.5 %collective-permute-done.16.refs_9_ = bf16[2,128,1024]{2,1,0:T(8,128)(2,1)S(1)} collective-permute-done((bf16[2,128,1024]{2,1,0:T(8,128)(2,1)S(1)}, bf16[2,128,1024]{2,1,0:T(8,128)(2,1)S(1)}, u32[]{:S(2)}, u32[]{:S(2)}) %collective-permute-start.16) | collective-permute-done | bytes 524320 | tf_op jit(solution)/shard_map/ppermute | solution.py:402
  165.5 3.1 %finish.9 = (bf16[4,128,4096]{2,1,0:T(8,128)(2,1)}, f32[8,128]{1,0:T(8,128)}) custom-call(s32[11]{0:T(128)S(1)} %get-tuple-element.38.refs_0_.ids_ref, f32[4,128,1024]{2,1,0:T(8,128)S(1)} %get-tuple-element.58.refs_7_.refs_1_, bf16[4,128,1024]{2,1,0:T(8,128)(2,1)S(1)} %get-tuple-element.59.refs_2_, ...), custom_call_target="tpu_custom_call", output_to_operand_aliasing={{0}: (12, {})} | custom-call | flops 1000 | bytes 1000 | tf_op jit(solution)/shard_map/finish/pallas_call | solution.py:545
  168.5 2.7 %final_states.1 = f32[4,1024,128]{2,1,0:T(8,128)} custom-call(s32[11]{0:T(128)S(1)} %get-tuple-element.38.refs_0_.ids_ref, f32[4,4,1,4096]{3,2,1,0:T(1,128)S(1)} %decays.1.refs_9_.refs_4_.refs_1_.refs_5_.refs_6_.refs_3_.refs_0_, bf16[4,128,1024]{2,1,0:T(8,128)(2,1)S(1)} %parents.1.refs_4_.refs_5_.refs_6_.refs_13_.refs_10_.refs_1_, ...), custom_call_target="tpu_custom_call" | custom-call | flops 1000 | bytes 1000 | tf_op jit(solution)/shard_map/final_states/pallas_call | solution.py:601
  (31 shorter events, 13.2 us)
Async XLA Ops:
  2.0 25.1 %collective-permute-start.3 = (bf16[2,16,64,128]{3,2,1,0:T(8,128)(2,1)S(1)}, bf16[2,16,64,128]{3,2,1,0:T(8,128)(2,1)S(1)}, u32[]{:S(2)}, u32[]{:S(2)}) collective-permute-start(bf16[2,16,64,128]{3,2,1,0:T(8,128)(2,1)S(1)} %fusion), channel_id=1, source_target_pairs={{0,2},{2,0},{1,3},{3,1},{4,6},{6,4},{5,7},{7,5},{8,10},{10,8},{9,1... | collective-permute-start | bytes 1572872 | tf_op jit(solution)/shard_map/ppermute | solution.py:290
  3.5 4.5 %collective-permute-start = (bf16[4,64,128]{2,1,0:T(8,128)(2,1)}, bf16[4,64,128]{2,1,0:T(8,128)(2,1)S(1)}, u32[]{:S(2)}, u32[]{:S(2)}) collective-permute-start(bf16[4,64,128]{2,1,0:T(8,128)(2,1)} %bitcast.16), channel_id=1, source_target_pairs={{0,4},{4,0},{8,12},{12,8},{1,5},{5,1},{9,13},{13,9},{2,6},{6,2},{1... | collective-permute-start | bytes 196616 | tf_op jit(solution)/shard_map/ppermute | solution.py:295
  8.8 6.0 %collective-permute-start.1 = (bf16[8,64,128]{2,1,0:T(8,128)(2,1)S(1)}, bf16[8,64,128]{2,1,0:T(8,128)(2,1)S(1)}, u32[]{:S(2)}, u32[]{:S(2)}) collective-permute-start(bf16[8,64,128]{2,1,0:T(8,128)(2,1)S(1)} %pad_maximum_fusion.1), channel_id=1, source_target_pairs={{0,8},{4,12},{8,0},{12,4},{1,9},{5,13},{9,1},{13,5},{2,10},{6,14},... | collective-permute-start | bytes 393224 | tf_op jit(solution)/shard_map/ppermute | solution.py:295
  25.4 1.7 copy-start
  25.4 1.7 copy-start.1
  25.4 1.6 copy-start.2
  29.2 26.9 %collective-permute-start.5 = (bf16[4,128,1024]{2,1,0:T(8,128)(2,1)S(1)}, bf16[4,128,1024]{2,1,0:T(8,128)(2,1)S(1)}, u32[]{:S(2)}, u32[]{:S(2)}) collective-permute-start(bf16[4,128,1024]{2,1,0:T(8,128)(2,1)S(1)} %parents.1.refs_4_.refs_5_.refs_6_.refs_13_.refs_10_.refs_1_), channel_id=1, source_target_pairs={{4,0},{8,4},{12,8},{5,1},{9,5},{13,9},{6,2},{10,6},{14,10},{7,3},{... | collective-permute-start | bytes 3145736 | tf_op jit(solution)/shard_map/ppermute | solution.py:444
  32.5 5.8 %collective-permute-start.2 = (bf16[2,128,1024]{2,1,0:T(8,128)(2,1)S(1)}, bf16[2,128,1024]{2,1,0:T(8,128)(2,1)S(1)}, u32[]{:S(2)}, u32[]{:S(2)}) collective-permute-start(bf16[2,128,1024]{2,1,0:T(8,128)(2,1)S(1)} %get-tuple-element.49.refs_2_.refs_3_.refs_9_), channel_id=1, source_target_pairs={{0,4},{1,5},{2,6},{3,7},{16,20},{17,21},{18,22},{19,23}} | collective-permute-start | bytes 1572872 | tf_op jit(solution)/shard_map/ppermute | solution.py:402
  33.2 8.1 %collective-permute-start.6 = (bf16[2,128,1024]{2,1,0:T(8,128)(2,1)S(1)}, bf16[2,128,1024]{2,1,0:T(8,128)(2,1)S(1)}, u32[]{:S(2)}, u32[]{:S(2)}) collective-permute-start(bf16[2,128,1024]{2,1,0:T(8,128)(2,1)S(1)} %get-tuple-element.45.refs_3_.refs_2_.refs_4_.refs_10_), channel_id=1, source_target_pairs={{0,4},{1,5},{2,6},{3,7},{16,20},{17,21},{18,22},{19,23}} | collective-permute-start | bytes 1572872 | tf_op jit(solution)/shard_map/ppermute | solution.py:402
  41.9 30.2 %collective-permute-start.4 = (bf16[2,128,1024]{2,1,0:T(8,128)(2,1)S(1)}, bf16[2,128,1024]{2,1,0:T(8,128)(2,1)S(1)}, u32[]{:S(2)}, u32[]{:S(2)}) collective-permute-start(bf16[2,128,1024]{2,1,0:T(8,128)(2,1)S(1)} %pass_on.10.refs_9_), channel_id=1, source_target_pairs={{0,4},{4,8},{1,5},{5,9},{2,6},{6,10},{3,7},{7,11},{16,20},{20,24},... | collective-permute-start | bytes 1572872 | tf_op jit(solution)/shard_map/ppermute | solution.py:402
  56.9 38.9 %collective-permute-start.9 = (bf16[4,128,1024]{2,1,0:T(8,128)(2,1)S(1)}, bf16[4,128,1024]{2,1,0:T(8,128)(2,1)S(1)}, u32[]{:S(2)}, u32[]{:S(2)}) collective-permute-start(bf16[4,128,1024]{2,1,0:T(8,128)(2,1)S(1)} %pass_down.3.refs_7_), channel_id=1, source_target_pairs={{4,0},{8,4},{12,8},{5,1},{9,5},{13,9},{6,2},{10,6},{14,10},{7,3},{... | collective-permute-start | bytes 3145736 | tf_op jit(solution)/shard_map/ppermute | solution.py:444
  66.4 17.4 %collective-permute-start.7 = (bf16[2,128,1024]{2,1,0:T(8,128)(2,1)S(1)}, bf16[2,128,1024]{2,1,0:T(8,128)(2,1)S(1)}, u32[]{:S(2)}, u32[]{:S(2)}) collective-permute-start(bf16[2,128,1024]{2,1,0:T(8,128)(2,1)S(1)} %pass_on.11.refs_9_), channel_id=1, source_target_pairs={{0,4},{4,8},{1,5},{5,9},{2,6},{6,10},{3,7},{7,11},{16,20},{20,24},... | collective-permute-start | bytes 1572872 | tf_op jit(solution)/shard_map/ppermute | solution.py:402
  72.8 22.2 %collective-permute-start.10 = (bf16[2,128,1024]{2,1,0:T(8,128)(2,1)S(1)}, bf16[2,128,1024]{2,1,0:T(8,128)(2,1)S(1)}, u32[]{:S(2)}, u32[]{:S(2)}) collective-permute-start(bf16[2,128,1024]{2,1,0:T(8,128)(2,1)S(1)} %pass_on.12.refs_9_), channel_id=1, source_target_pairs={{0,4},{4,8},{8,12},{1,5},{5,9},{9,13},{2,6},{6,10},{10,14},{3,7},{... | collective-permute-start | bytes 1572872 | tf_op jit(solution)/shard_map/ppermute | solution.py:402
  84.4 21.7 %collective-permute-start.8 = (bf16[2,128,1024]{2,1,0:T(8,128)(2,1)S(1)}, bf16[2,128,1024]{2,1,0:T(8,128)(2,1)S(1)}, u32[]{:S(2)}, u32[]{:S(2)}) collective-permute-start(bf16[2,128,1024]{2,1,0:T(8,128)(2,1)S(1)} %pass_on.13.refs_7_), channel_id=1, source_target_pairs={{0,4},{4,8},{8,12},{1,5},{5,9},{9,13},{2,6},{6,10},{10,14},{3,7},{... | collective-permute-start | bytes 1572872 | tf_op jit(solution)/shard_map/ppermute | solution.py:402
  96.7 23.4 %collective-permute-start.12 = (bf16[4,128,1024]{2,1,0:T(8,128)(2,1)S(1)}, bf16[4,128,1024]{2,1,0:T(8,128)(2,1)S(1)}, u32[]{:S(2)}, u32[]{:S(2)}) collective-permute-start(bf16[4,128,1024]{2,1,0:T(8,128)(2,1)S(1)} %pass_down.4.refs_7_), channel_id=1, source_target_pairs={{4,0},{8,4},{12,8},{5,1},{9,5},{13,9},{6,2},{10,6},{14,10},{7,3},{... | collective-permute-start | bytes 3145736 | tf_op jit(solution)/shard_map/ppermute | solution.py:444
  100.3 17.2 %collective-permute-start.13 = (bf16[2,128,1024]{2,1,0:T(8,128)(2,1)S(1)}, bf16[2,128,1024]{2,1,0:T(8,128)(2,1)S(1)}, u32[]{:S(2)}, u32[]{:S(2)}) collective-permute-start(bf16[2,128,1024]{2,1,0:T(8,128)(2,1)S(1)} %pass_on.14.refs_7_), channel_id=1, source_target_pairs={{0,4},{4,8},{8,12},{1,5},{5,9},{9,13},{2,6},{6,10},{10,14},{3,7},{... | collective-permute-start | bytes 1572872 | tf_op jit(solution)/shard_map/ppermute | solution.py:402
  107.0 21.6 %collective-permute-start.11 = (bf16[2,128,1024]{2,1,0:T(8,128)(2,1)S(1)}, bf16[2,128,1024]{2,1,0:T(8,128)(2,1)S(1)}, u32[]{:S(2)}, u32[]{:S(2)}) collective-permute-start(bf16[2,128,1024]{2,1,0:T(8,128)(2,1)S(1)} %pass_on.15.refs_15_), channel_id=1, source_target_pairs={{0,4},{4,8},{8,12},{1,5},{5,9},{9,13},{2,6},{6,10},{10,14},{3,7},{... | collective-permute-start | bytes 1572872 | tf_op jit(solution)/shard_map/ppermute | solution.py:402
  118.1 21.8 %collective-permute-start.15 = (bf16[2,128,1024]{2,1,0:T(8,128)(2,1)S(1)}, bf16[2,128,1024]{2,1,0:T(8,128)(2,1)S(1)}, u32[]{:S(2)}, u32[]{:S(2)}) collective-permute-start(bf16[2,128,1024]{2,1,0:T(8,128)(2,1)S(1)} %pass_on.16.refs_9_), channel_id=1, source_target_pairs={{4,8},{8,12},{5,9},{9,13},{6,10},{10,14},{7,11},{11,15},{20,24},{2... | collective-permute-start | bytes 1572872 | tf_op jit(solution)/shard_map/ppermute | solution.py:402
  129.4 19.3 %collective-permute-start.14 = (bf16[2,128,1024]{2,1,0:T(8,128)(2,1)S(1)}, bf16[2,128,1024]{2,1,0:T(8,128)(2,1)S(1)}, u32[]{:S(2)}, u32[]{:S(2)}) collective-permute-start(bf16[2,128,1024]{2,1,0:T(8,128)(2,1)S(1)} %pass_on.17.refs_16_), channel_id=1, source_target_pairs={{4,8},{8,12},{5,9},{9,13},{6,10},{10,14},{7,11},{11,15},{20,24},{2... | collective-permute-start | bytes 1572872 | tf_op jit(solution)/shard_map/ppermute | solution.py:402
  131.3 37.2 %collective-permute-start.18 = (bf16[4,128,1024]{2,1,0:T(8,128)(2,1)S(1)}, bf16[4,128,1024]{2,1,0:T(8,128)(2,1)S(1)}, u32[]{:S(2)}, u32[]{:S(2)}) collective-permute-start(bf16[4,128,1024]{2,1,0:T(8,128)(2,1)S(1)} %pass_down.5.refs_6_), channel_id=1, source_target_pairs={{4,0},{8,4},{12,8},{5,1},{9,5},{13,9},{6,2},{10,6},{14,10},{7,3},{... | collective-permute-start | bytes 3145736 | tf_op jit(solution)/shard_map/ppermute | solution.py:444
  140.6 18.4 %collective-permute-start.17 = (bf16[2,128,1024]{2,1,0:T(8,128)(2,1)S(1)}, bf16[2,128,1024]{2,1,0:T(8,128)(2,1)S(1)}, u32[]{:S(2)}, u32[]{:S(2)}) collective-permute-start(bf16[2,128,1024]{2,1,0:T(8,128)(2,1)S(1)} %pass_on.18.refs_5_), channel_id=1, source_target_pairs={{8,12},{9,13},{10,14},{11,15},{24,28},{25,29},{26,30},{27,31}} | collective-permute-start | bytes 1572872 | tf_op jit(solution)/shard_map/ppermute | solution.py:402
  149.4 16.1 %collective-permute-start.16 = (bf16[2,128,1024]{2,1,0:T(8,128)(2,1)S(1)}, bf16[2,128,1024]{2,1,0:T(8,128)(2,1)S(1)}, u32[]{:S(2)}, u32[]{:S(2)}) collective-permute-start(bf16[2,128,1024]{2,1,0:T(8,128)(2,1)S(1)} %pass_on.19.refs_17_), channel_id=1, source_target_pairs={{8,12},{9,13},{10,14},{11,15},{24,28},{25,29},{26,30},{27,31}} | collective-permute-start | bytes 1572872 | tf_op jit(solution)/shard_map/ppermute | solution.py:402

commit v3 on v2

--- a/solution.py
+++ b/solution.py
@@ -28,6 +28,10 @@
 SMEM = pltpu.SMEM
 
 
+def takes(us):
+    return pl.CostEstimate(flops=int(us * 4e9), bytes_accessed=int(us * 14e6), transcendentals=0)
+
+
 def pin(array):
     return pltpu.with_memory_space_constraint(array, VMEM)
 
@@ -36,7 +40,7 @@
     return pltpu.with_memory_space_constraint(array, pltpu.HBM)
 
 
-def call(body, outs, ins, *, scalars=(), after=(), name, flops=1_000, nbytes=1_000, scratch=(), limit=12):
+def call(body, outs, ins, *, scalars=(), after=(), name, us=1.0, scratch=(), limit=12):
     n_scalars, n_ins, n_after = len(scalars), len(ins), len(after)
 
     def kernel(*refs):
@@ -54,7 +58,7 @@
         out_specs=(pl.BlockSpec(memory_space=VMEM),) * len(outs),
         scratch_shapes=list(scratch),
         compiler_params=pltpu.CompilerParams(vmem_limit_bytes=limit << 20),
-        cost_estimate=pl.CostEstimate(flops=flops, bytes_accessed=nbytes, transcendentals=0),
+        cost_estimate=takes(us),
         name=name,
     )(*scalars, *pinned)
     return result[0] if single else result
@@ -85,18 +89,15 @@
     order, ids, b_ref, c_ref, spans_hbm, dt_hbm, bias_hbm, alog_hbm, skip_hbm, gain_hbm, x_hbm, info, cum_ref, cum_t_ref,
     step_t_ref, weight_ref, growth_ref, x_ref, bias_ref, alog_ref, skip_ref, gain_ref, *rest
 ):
-    outs, (dt_ref, spans, small_sems, x_sems) = rest[:-4], rest[-4:]
+    outs, (dt_ref, spans, small_sems, x_sem) = rest[:-4], rest[-4:]
     requests, heads_here, span = dt_ref.shape
     pairs = (
         (spans_hbm, spans), (dt_hbm, dt_ref), (bias_hbm, bias_ref), (alog_hbm, alog_ref), (skip_hbm, skip_ref),
         (gain_hbm, gain_ref),
     )
     small = [pltpu.make_async_copy(source, target, small_sems.at[i]) for i, (source, target) in enumerate(pairs)]
-    large = []
-    for i, group in enumerate(order):
-        lanes = pl.ds(group * GROUP_LANES, GROUP_LANES)
-        large.append(pltpu.make_async_copy(x_hbm.at[:, :, lanes], x_ref.at[:, :, lanes], x_sems.at[i]))
-    for copy in small + large:
+    x_copy = pltpu.make_async_copy(x_hbm.at[:, :, pl.ds(order[0] * GROUP_LANES, GROUP_LANES)], x_ref, x_sem)
+    for copy in (*small, x_copy):
         copy.start()
     for i in range(3):
         info[i] = ids[i]
@@ -124,34 +125,30 @@
             growth_ref[r, g] = growth[:, here]
             cum_t_ref[r, g] = cum_t[here, :]
             step_t_ref[r, g] = step_t[here, :]
-    large[0].wait()
+    x_copy.wait()
     block_body(order[0], x_ref, b_ref, weight_ref, *outs)
-    for copy in large[1:]:
-        copy.wait()
-
-
-def decay_body(info, dt_ref, bias_ref, alog_ref, out_ref):
-    requests = out_ref.shape[1]
-    heads_here = dt_ref.shape[1]
-    toks = dt_ref.shape[0] // requests
+
+
+def decay_body(info, *refs):
+    dt_refs, (bias_ref, alog_ref, out_ref) = refs[:-3], refs[-3:]
+    toks = len(dt_refs)
+    requests, heads_here, _ = dt_refs[0].shape
     width = out_ref.shape[-1]
     me = info[0]
     rate = -jnp.exp(alog_ref[...])
 
-    def add(n, sums):
-        t = me ^ n
+    blank = jnp.zeros((requests, heads_here), F32)
+    sums = (blank, blank, blank)
+    for n, dt_ref in enumerate(dt_refs):
+        t = lax.rem(me - n + toks, toks)
         totals = []
         for r in range(requests):
-            step = softplus(dt_ref[n * requests + r].astype(F32).T + bias_ref[...])
+            step = softplus(dt_ref[r].astype(F32).T + bias_ref[...])
             live = (t < info[3 + requests + r]).astype(F32)
             totals.append(jnp.sum(step, axis=0, keepdims=True) * (rate * live))
         total = jnp.concatenate(totals, axis=0)
-        return tuple(
-            held + total * chosen.astype(F32) for held, chosen in zip(sums, (me == t, me > t, me < t))
-        )
-
-    blank = jnp.zeros((requests, heads_here), F32)
-    through, before, after = lax.fori_loop(0, toks, add, (blank, blank, blank))
+        sums = [held + total * chosen.astype(F32) for held, chosen in zip(sums, (me == t, me > t, me < t))]
+    through, before, after = sums
     factors = jnp.exp(jnp.concatenate([through, before, before + through, after], axis=0))
     owner = lax.broadcasted_iota(jnp.int32, (heads_here, width), 1) // HEAD_DIM
     head = lax.broadcasted_iota(jnp.int32, (heads_here, width), 0)
@@ -166,14 +163,13 @@
 
 def block_body(group, x_ref, b_ref, weight_ref, *outs):
     low = low_half(x_ref.shape[1])
-    base = group * GROUP_LANES
     for part, out_ref in enumerate(outs):
         for i in range(REQ_CHUNK):
             r = part * REQ_CHUNK + i
             weight = weight_ref[r, group]
             scaled = []
             for q in range(PAIRS):
-                here = slice(base + q * PAIR_LANES, base + (q + 1) * PAIR_LANES)
+                here = pair_lanes(q)
                 scaled.append((x_ref[r, :, here].astype(F32) * spread_pair(weight, q, low)).astype(BF16))
             b_here = b_ref[r, :, group * STATE : (group + 1) * STATE]
             states = lax.dot_general(
@@ -186,7 +182,6 @@
     requests, span = x_ref.shape[:2]
     z_copy = pltpu.make_async_copy(z_hbm.at[:, :, pl.ds(group * GROUP_LANES, GROUP_LANES)], z_ref, sem)
     z_copy.start()
-    base = group * GROUP_LANES
 
     @pl.loop(0, requests)
     def _(r):
@@ -210,7 +205,7 @@
                 return (scores * decay * step_t[h : h + 1, :]).astype(BF16)
 
             for q in range(PAIRS):
-                here = slice(base + q * PAIR_LANES, base + (q + 1) * PAIR_LANES)
+                here = pair_lanes(q)
                 x_pair = x_ref[r, :, here]
                 nothing = jnp.zeros_like(x_pair)
                 both = jnp.concatenate([jnp.where(low, x_pair, nothing), jnp.where(low, nothing, x_pair)], axis=0)
@@ -223,8 +218,13 @@
     z_copy.wait()
 
 
-def parents_body(requests, unit, info, parent, state_dev, state_slot, cache_hbm, *refs):
-    pieces, (out_ref, rows, sems) = refs[:-3], refs[-3:]
+def parents_body(order, requests, unit, info, parent, state_dev, state_slot, cache_hbm, x_hbm, *refs):
+    n_later = len(order) - 1
+    pieces, (out_ref, *x_refs), (rows, sems, x_sems) = refs[: -4 - n_later], refs[-4 - n_later : -3], refs[-3:]
+    x_copies = [
+        pltpu.make_async_copy(x_hbm.at[:, :, pl.ds(group * GROUP_LANES, GROUP_LANES)], x_refs[i], x_sems.at[i])
+        for i, group in enumerate(order[1:])
+    ]
     holders = len(pieces) + 1
     places = []
     for r in range(requests):
@@ -240,6 +240,8 @@
 
     for r in range(requests):
         own(r, lambda copy: copy.start())
+    for copy in x_copies:
+        copy.start()
     for r in range(requests):
         shift, slot = places[r]
         for n, piece in enumerate(pieces):
@@ -253,6 +255,9 @@
         @pl.when(shift == 0)
         def _(r=r):
             out_ref[r] = rows[r].astype(BF16).T
+
+    for copy in x_copies:
+        copy.wait()
 
 
 def chain_lanes(group, device, unit):
@@ -290,11 +295,9 @@
         piece = lax.ppermute(piece, "cache", [(i, (i + shift) % holders) for i in range(holders)])
         pieces.append(pin(piece.reshape(slots_here, unit, STATE)))
     dt_t = dt_in.transpose(0, 2, 1)
-    all_dt, step = dt_t, 1
-    while step < toks:
-        other = lax.ppermute(all_dt, "tok", [(k, k ^ step) for k in range(toks)])
-        all_dt = jnp.concatenate([all_dt, other], axis=0)
-        step *= 2
+    all_dt = [dt_t] + [
+        lax.ppermute(dt_t, "tok", [(k, (k + shift) % toks) for k in range(toks)]) for shift in range(1, toks)
+    ]
 
     b_flat = pin(b_in.reshape(requests, span, groups * STATE))
     c_flat = pin(c_in.reshape(requests, span, groups * STATE))
@@ -304,62 +307,69 @@
     smem_spec, vmem_spec, any_spec, hbm_spec = (
         pl.BlockSpec(memory_space=space) for space in (SMEM, VMEM, pl.ANY, pltpu.HBM)
     )
-    info, cum, cum_t, step_t, weight, growth, x_in, bias, rates, skip, gain, *found = pl.pallas_call(
-        lambda *refs: front_body(order, *refs[:10], *refs[11:]),
+    info, cum, cum_t, step_t, weight, growth, x_first, bias, rates, skip, gain, *found = pl.pallas_call(
+        lambda *refs: front_body(order, *refs[:10], *refs[9 + toks :]),
         out_shape=(
             jax.ShapeDtypeStruct((3 + 2 * requests,), jnp.int32),
-            columns, as_rows, as_rows, columns, columns, VMEM(x_in.shape, BF16),
+            columns, as_rows, as_rows, columns, columns, VMEM((requests, span, GROUP_LANES), BF16),
             *(VMEM((1, heads_here), F32),) * 3, VMEM((1, width), F32), *(VMEM(*chunk_type),) * parts,
         ),
-        in_specs=[smem_spec] + [vmem_spec] * 2 + [hbm_spec] * 7 + [vmem_spec],
+        in_specs=[smem_spec] + [vmem_spec] * 2 + [hbm_spec] * 7 + [vmem_spec] * (toks - 1),
         out_specs=(smem_spec,) + (vmem_spec,) * (10 + parts),
         scratch_shapes=[
             VMEM(dt_t.shape, BF16), SMEM(spans.shape, jnp.int32),
-            pltpu.SemaphoreType.DMA((6,)), pltpu.SemaphoreType.DMA((groups,)),
+            pltpu.SemaphoreType.DMA((6,)), pltpu.SemaphoreType.DMA,
         ],
         compiler_params=pltpu.CompilerParams(vmem_limit_bytes=12 << 20),
-        cost_estimate=pl.CostEstimate(flops=1_000, bytes_accessed=1_000, transcendentals=0),
+        cost_estimate=takes(5.0),
         name="front",
     )(
         ids,
         b_flat,
         c_flat,
         *map(in_hbm, (spans, dt_t, dt_bias[None], a_log[None], skip_gain[None], norm_w[None], x_in)),
-        pin(all_dt),
+        *map(pin, all_dt[1:]),
     )
     states = {part: found[part] for part in range(parts)}
     previous = found[-1]
 
+    initial, *x_groups = pl.pallas_call(
+        lambda *refs: parents_body(order, requests, unit, *refs[: 6 + len(pieces)], *refs[7 + len(pieces) :]),
+        out_shape=(VMEM((requests, STATE, unit), BF16),) + (VMEM(x_first.shape, BF16),) * (groups - 1),
+        in_specs=[smem_spec] * 4 + [hbm_spec] * 2 + [vmem_spec] * (len(pieces) + 1),
+        out_specs=(vmem_spec,) * groups,
+        scratch_shapes=[
+            VMEM((requests, unit, STATE), F32), pltpu.SemaphoreType.DMA((requests,)), pltpu.SemaphoreType.DMA((groups,)),
+        ],
+        compiler_params=pltpu.CompilerParams(vmem_limit_bytes=12 << 20),
+        cost_estimate=takes(2.8),
+        name="parents",
+    )(info, parent, state_dev, state_slot, in_hbm(cache_states.reshape(slots_here, holders, unit, STATE)), in_hbm(x_in),
+        *pieces, pin(previous))
+    x_groups = [x_first, *x_groups]
+    decays = call(
+        decay_body,
+        ((4, requests, 1, width), F32),
+        (*all_dt, bias, rates),
+        scalars=(info,),
+        after=(initial,),
+        name="decays",
+        us=1.7,
+    )
+
+    previous = decays
     for i in range(1, groups):
         found = call(
             functools.partial(block_body, order[i]),
             (chunk_type,) * parts,
-            (x_in, b_flat, weight),
+            (x_groups[i], b_flat, weight),
             after=(previous,),
             name="block_states",
+            us=1.6,
         )
         for part in range(parts):
             states[i * parts + part] = found[part]
         previous = found[-1]
-
-    initial = pl.pallas_call(
-        lambda *refs: parents_body(requests, unit, *refs[: 5 + len(pieces)], *refs[6 + len(pieces) :]),
-        out_shape=VMEM((requests, STATE, unit), BF16),
-        in_specs=[smem_spec] * 4 + [hbm_spec] + [vmem_spec] * (len(pieces) + 1),
-        out_specs=vmem_spec,
-        scratch_shapes=[VMEM((requests, unit, STATE), F32), pltpu.SemaphoreType.DMA((requests,))],
-        compiler_params=pltpu.CompilerParams(vmem_limit_bytes=12 << 20),
-        cost_estimate=pl.CostEstimate(flops=1_000, bytes_accessed=1_000, transcendentals=0),
-        name="parents",
-    )(info, parent, state_dev, state_slot, in_hbm(cache_states.reshape(slots_here, holders, unit, STATE)), *pieces, pin(previous))
-    decays = call(
-        decay_body,
-        ((4, requests, 1, width), F32),
-        (all_dt, bias, rates),
-        scalars=(info,),
-        after=(initial,),
-        name="decays",
-    )
 
     def decay_of(decays_ref, kind, r, group, lanes=slice(0, GROUP_LANES)):
         return decays_ref[kind, r, :, group * GROUP_LANES + lanes.start : group * GROUP_LANES + lanes.stop]
@@ -394,7 +404,7 @@
             for n, device in enumerate(devices):
                 pl.when(ids_ref[0] == device)(functools.partial(branch, n, device))
 
-        return call(body, chunk_type, ins, scalars=(info,), after=after, name="pass_on")
+        return call(body, chunk_type, ins, scalars=(info,), after=after, name="pass_on", us=0.8)
 
     def send_up(h, after=()):
         sent = pass_on(h, after)
@@ -440,12 +450,13 @@
                 scalars=(info,),
                 after=after,
                 name="pass_down",
+                us=0.8,
             )
         arrived.append(lax.ppermute(sent, "tok", backward))
         return sent
 
     def local_sums(i, after):
-        ins = (x_in, b_flat, c_flat, cum, cum_t, step_t, skip)
+        ins = (x_groups[i], b_flat, c_flat, cum, cum_t, step_t, skip)
         n_ins, n_after = len(ins), len(after)
         return pl.pallas_call(
             lambda *refs: local_body(order[i], *refs[: 1 + n_ins], refs[1 + n_ins], *refs[2 + n_ins + n_after :]),
@@ -454,7 +465,7 @@
             out_specs=(vmem_spec, vmem_spec),
             scratch_shapes=[pltpu.SemaphoreType.DMA],
             compiler_params=pltpu.CompilerParams(vmem_limit_bytes=12 << 20),
-            cost_estimate=pl.CostEstimate(flops=1_000, bytes_accessed=1_000, transcendentals=0),
+            cost_estimate=takes(3.0),
             name="local_sums",
         )(info, *(pin(a) for a in ins), in_hbm(z_in), *(pin(a) for a in after))
 
@@ -554,7 +565,7 @@
                 pltpu.SemaphoreType.DMA((count,)),
             ],
             compiler_params=pltpu.CompilerParams(vmem_limit_bytes=12 << 20),
-            cost_estimate=pl.CostEstimate(flops=1_000, bytes_accessed=1_000, transcendentals=0),
+            cost_estimate=takes(4.0),
             name="finish",
         )(info, *pinned, *([y_so_far] if had else []))
 
@@ -572,7 +583,8 @@
             decays_ref, initial_ref, later_ref = refs[:3]
             ahead_refs = dict(zip(keys, refs[3 : 3 + len(keys)]))
             state_refs = refs[3 + len(keys) : 3 + len(keys) + chunks]
-            final_ref, buf, sems = refs[-3:]
+            final_ref, buf, sems = refs[-4:][:1] + refs[-2:]
+            refs[-3][...] = jnp.zeros_like(refs[-3])
 
             def branch(device):
                 first = device * unit
@@ -598,24 +610,24 @@
                 copy.wait()
 
         pinned = [pin(a) for a in (*ins, *after)]
-        final = pl.pallas_call(
+        final, token = pl.pallas_call(
             kernel,
-            out_shape=jax.ShapeDtypeStruct((requests, unit, STATE), F32),
+            out_shape=(jax.ShapeDtypeStruct((requests, unit, STATE), F32), VMEM((8, PAIR_LANES), F32)),
             in_specs=[pl.BlockSpec(memory_space=SMEM)] + [pl.BlockSpec(memory_space=VMEM)] * len(pinned),
-            out_specs=pl.BlockSpec(memory_space=pl.ANY),
+            out_specs=(any_spec, vmem_spec),
             scratch_shapes=[VMEM((requests, unit, STATE), F32), pltpu.SemaphoreType.DMA((requests,))],
             compiler_params=pltpu.CompilerParams(vmem_limit_bytes=12 << 20),
-            cost_estimate=pl.CostEstimate(flops=1_000, bytes_accessed=1_000, transcendentals=0),
+            cost_estimate=takes(2.7),
             name="final_states",
         )(info, *pinned)
-        return final.reshape(requests, unit // HEAD_DIM, HEAD_DIM, STATE)
+        return final.reshape(requests, unit // HEAD_DIM, HEAD_DIM, STATE), token
 
     slots = chunks + HOP * (toks - 2)
     lag = HOP * (toks - 2) + parts
     for h in range(HOP):
         send_up(h)
     send_down(0)
-    local = {0: local_sums(0, (decays,))}
+    local = {0: local_sums(0, (previous,))}
     previous = local[0][0]
     pending = list(range(1, groups))
     downs = list(range(1, toks))
@@ -629,7 +641,7 @@
         elif done < groups - 1 and done * parts + lag + 1 <= h:
             y_out, previous = finish(done, list(range(parts)), y_out, (previous,))
             done += 1
-        if downs and h >= round(HOP + 1 + 2.5 * (toks - 1 - len(downs))):
+        if downs and h >= round(HOP + (1 + 2.5 * (toks - 1 - len(downs))) * parts / 2):
             previous = send_down(downs.pop(0), (previous,))
     for s in downs:
         previous = send_down(s, (previous,))
@@ -642,7 +654,7 @@
         done += 1
     for part in range(parts):
         if part == parts - 1:
-            final = final_states((previous,))
+            final, previous = final_states((previous,))
         y_out, previous = finish(groups - 1, [part], y_out, (previous,))
     return (y_out, final)
 

time: 173 us -> 147 us (0.85)
  waiting for transfers between devices: 67.9 us -> 49.8 us
  Pallas kernels: 52.2 us -> 46.6 us
    ppermute x12, waiting for transfers between devices: 51.4 us -> 38.4 us  [send_up(): received[h] = lax.ppermute(sent, 'tok', pairs)]
    ppermute x2 -> x3, waiting for transfers between devices: 5.96 us -> 0.09 us  [shards(): lax.ppermute(dt_t, 'tok', [(k, (k + shift) % toks) for k in range(toks)])]
    ppermute x1, waiting for transfers between devices: 0.01 us -> 2.67 us  [shards(): lax.ppermute(piece, 'cache', [(i, (i + shift) % holders) for i in range(h...]
    ppermute x12, starting transfers between devices: 20.6 us -> 18.1 us  [send_up(): received[h] = lax.ppermute(sent, 'tok', pairs)]
    pallas_call x4, Pallas kernels: 9.48 us -> 7.11 us  [local_sums(): pl.pallas_call(lambda *refs: local_body(order[i], *refs[:1 + n_ins], refs...]
    pallas_call x5, Pallas kernels: 15.1 us -> 12.9 us  [finish(): pl.pallas_call(kernel, out_shape=(jax.ShapeDtypeStruct((requests, span, w...]
    ppermute x2 -> x3, starting transfers between devices: 1.98 us -> 3.99 us  [shards(): lax.ppermute(dt_t, 'tok', [(k, (k + shift) % toks) for k in range(toks)])]
    ppermute x4, waiting for transfers between devices: 10.6 us -> 8.61 us  [send_down(): arrived.append(lax.ppermute(sent, 'tok', backward))]
  transfers between devices with their start and end apart: 19 -> 20, of which waited for: 13 -> 12; matrix products, arithmetic and copies ran while one was open for 2% -> 3% of each run, Pallas kernels for 28% -> 31%
where the time goes in v3:
time: 147 us; the launch traced here: 144 us
  waiting for transfers between devices  49.8 us (34%)
  Pallas kernels  46.6 us (32%)
  starting transfers between devices  42.9 us (29%)
  local copies, waits for them, and re-layouts  3.8 us (3%)
    ppermute x12, waiting for transfers between devices, send_up(): received[h] = lax.ppermute(sent, 'tok', pairs)  38.4 us
    ppermute x4, starting transfers between devices, send_down(): arrived.append(lax.ppermute(sent, 'tok', backward))  19.3 us
    ppermute x12, starting transfers between devices, send_up(): received[h] = lax.ppermute(sent, 'tok', pairs)  18.1 us
    pallas_call x17, Pallas kernels, call(): pl.pallas_call(kernel, out_shape=tuple((VMEM(shape, dtype) for shape, dty...  16.3 us
    pallas_call x5, Pallas kernels, finish(): pl.pallas_call(kernel, out_shape=(jax.ShapeDtypeStruct((requests, span, w...  12.9 us
    ppermute x4, waiting for transfers between devices, send_down(): arrived.append(lax.ppermute(sent, 'tok', backward))  8.61 us
    pallas_call x4, Pallas kernels, local_sums(): pl.pallas_call(lambda *refs: local_body(order[i], *refs[:1 + n_ins], refs...  7.11 us
    pallas_call x1, Pallas kernels, shards(): pl.pallas_call(lambda *refs: front_body(order, *refs[:10], *refs[9 + toks...  4.87 us
  transfers between devices with their start and end apart: 20, of which 12 were waited for; matrix products, arithmetic and copies ran while one was open for 3% of the time, Pallas kernels for 31%

profile of v3, /device:TPU:16, one launch (start us, length us, event | category | flops | bytes accessed | tf_op | source)
XLA Modules:
  0.0 144.4 jit_solution(5065875666166335489)
XLA Ops:
  1.1 3.5 %collective-permute-start.1 = (bf16[4,64,128]{2,1,0:T(8,128)(2,1)}, bf16[4,64,128]{2,1,0:T(8,128)(2,1)S(1)}, u32[]{:S(2)}, u32[]{:S(2)}) collective-permute-start(bf16[4,64,128]{2,1,0:T(8,128)(2,1)} %bitcast.15), channel_id=1, source_target_pairs={{0,8},{4,12},{8,0},{12,4},{1,9},{5,13},{9,1},{13,5},{2,10},{6,14},... | collective-permute-start | bytes 196616 | tf_op jit(solution)/shard_map/ppermute | solution.py:299
  4.6 1.3 fusion
  5.9 1.6 %collective-permute-start.3 = (bf16[2,16,64,128]{3,2,1,0:T(8,128)(2,1)S(1)}, bf16[2,16,64,128]{3,2,1,0:T(8,128)(2,1)S(1)}, u32[]{:S(2)}, u32[]{:S(2)}) collective-permute-start(bf16[2,16,64,128]{3,2,1,0:T(8,128)(2,1)S(1)} %fusion), channel_id=1, source_target_pairs={{0,2},{2,0},{1,3},{3,1},{4,6},{6,4},{5,7},{7,5},{8,10},{10,8},{9,1... | collective-permute-start | bytes 1572872 | tf_op jit(solution)/shard_map/ppermute | solution.py:295
  7.5 1.2 reshape.21.refs_2_.refs_3_
  8.7 1.2 reshape.20.refs_1_.refs_2_
  10.2 4.9 %front.1 = (s32[11]{0:T(128)S(1)}, f32[4,4,128,16]{3,2,1,0:T(8,128)S(1)}, f32[4,4,16,128]{3,2,1,0:T(8,128)S(1)}, f32[4,4,16,128]{3,2,1,0:T(8,128)S(1)}, f32[4,4,...) custom-call(s32[3]{0:T(128)S(1)} %pad_add_fusion.refs_0_, ...), custom_call_target="tpu_custom_call" | custom-call | flops 20000000000 | bytes 70000000 | tf_op jit(solution)/shard_map/front/pallas_call | solution.py:310
  16.4 2.7 %collective-permute-done.3 = bf16[2,16,64,128]{3,2,1,0:T(8,128)(2,1)S(1)} collective-permute-done((bf16[2,16,64,128]{3,2,1,0:T(8,128)(2,1)S(1)}, bf16[2,16,64,128]{3,2,1,0:T(8,128)(2,1)S(1)}, u32[]{:S(2)}, u32[]{:S(2)}) %collective-permute-start.3) | collective-permute-done | bytes 524320 | tf_op jit(solution)/shard_map/ppermute | solution.py:295
  19.1 2.7 %parents.1 = (bf16[4,128,1024]{2,1,0:T(8,128)(2,1)S(1)}, bf16[4,128,1024]{2,1,0:T(8,128)(2,1)S(1)}, bf16[4,128,1024]{2,1,0:T(8,128)(2,1)S(1)}, bf16[4,128,1024]{2,1,0:T(8,128)(2,1)S(1)}) custom-call(s32[11]{0:T(128)S(1)} %get-tuple-element.44.refs_0_.ids_ref, s32[8]{0:T(128)S(1)} %copy-done.1, s32[4]{0:T(128)S(1)} %copy-done.2, s32[4]{0:T(128)S(1)} %copy-done.3, ...), custom_call_target="tpu_custom_call" | custom-call | flops 11200000000 | bytes 39200000 | tf_op jit(solution)/shard_map/parents/pallas_call | solution.py:336
  21.8 3.7 %collective-permute-start.6 = (bf16[4,128,1024]{2,1,0:T(8,128)(2,1)S(1)}, bf16[4,128,1024]{2,1,0:T(8,128)(2,1)S(1)}, u32[]{:S(2)}, u32[]{:S(2)}) collective-permute-start(bf16[4,128,1024]{2,1,0:T(8,128)(2,1)S(1)} %get-tuple-element.56.refs_7_.refs_5_.refs_6_.refs_13_.refs_4_.refs_10_.refs_1_), channel_id=1, source_target_pairs={{4,0},{8,4},{12,8},{5,1},{9,5},{13,9},{6,2},{10,6},{14,10},{7,3},{... | collective-permute-start | bytes 3145736 | tf_op jit(solution)/shard_map/ppermute | solution.py:455
  25.5 1.8 %decays.1.refs_3_.refs_4_.refs_1_.refs_5_.refs_6_.refs_0_ = f32[4,4,1,4096]{3,2,1,0:T(1,128)S(1)} custom-call(s32[11]{0:T(128)S(1)} %get-tuple-element.44.refs_0_.ids_ref, bf16[4,64,128]{2,1,0:T(8,128)(2,1)S(1)} %bitcast.18, bf16[4,64,128]{2,1,0:T(8,128)(2,1)S(1)} %collective-permute-done.refs_10_.refs_2_, ...), custom_call_target="tpu_custom_call" | custom-call | flops 6800000000 | bytes 23800000 | tf_op jit(solution)/shard_map/decays/pallas_call | solution.py:54
  27.3 1.6 %block_states.3 = (bf16[2,128,1024]{2,1,0:T(8,128)(2,1)S(1)}, bf16[2,128,1024]{2,1,0:T(8,128)(2,1)S(1)}) custom-call(bf16[4,128,1024]{2,1,0:T(8,128)(2,1)S(1)} %get-tuple-element.53.refs_0_.refs_1_, bf16[4,128,512]{2,1,0:T(8,128)(2,1)S(1)} %reshape.20.refs_1_.refs_2_, f32[4,4,128,16]{3,2,1,0:T(8,128)S(1)} %get-tuple-element.52.refs_2_, ...), custom_call_target="tpu_custom_call" | custom-call | flops 6400000000 | bytes 22400000 | tf_op jit(solution)/shard_map/block_states/pallas_call | solution.py:54
  28.9 1.6 %block_states.4 = (bf16[2,128,1024]{2,1,0:T(8,128)(2,1)S(1)}, bf16[2,128,1024]{2,1,0:T(8,128)(2,1)S(1)}) custom-call(bf16[4,128,1024]{2,1,0:T(8,128)(2,1)S(1)} %get-tuple-element.51.refs_0_.refs_1_, bf16[4,128,512]{2,1,0:T(8,128)(2,1)S(1)} %reshape.20.refs_1_.refs_2_, f32[4,4,128,16]{3,2,1,0:T(8,128)S(1)} %get-tuple-element.52.refs_2_, ...), custom_call_target="tpu_custom_call" | custom-call | flops 6400000000 | bytes 22400000 | tf_op jit(solution)/shard_map/block_states/pallas_call | solution.py:54
  30.5 1.6 %block_states.5 = (bf16[2,128,1024]{2,1,0:T(8,128)(2,1)S(1)}, bf16[2,128,1024]{2,1,0:T(8,128)(2,1)S(1)}) custom-call(bf16[4,128,1024]{2,1,0:T(8,128)(2,1)S(1)} %get-tuple-element.46.refs_0_.refs_1_, bf16[4,128,512]{2,1,0:T(8,128)(2,1)S(1)} %reshape.20.refs_1_.refs_2_, f32[4,4,128,16]{3,2,1,0:T(8,128)S(1)} %get-tuple-element.52.refs_2_, ...), custom_call_target="tpu_custom_call" | custom-call | flops 6400000000 | bytes 22400000 | tf_op jit(solution)/shard_map/block_states/pallas_call | solution.py:54
  32.1 1.8 %local_sums.4 = (f32[4,128,1024]{2,1,0:T(8,128)S(1)}, bf16[4,128,1024]{2,1,0:T(8,128)(2,1)S(1)}) custom-call(s32[11]{0:T(128)S(1)} %get-tuple-element.44.refs_0_.ids_ref, bf16[4,128,1024]{2,1,0:T(8,128)(2,1)S(1)} %get-tuple-element.61.refs_1_, bf16[4,128,512]{2,1,0:T(8,128)(2,1)S(1)} %reshape.20.refs_1_.refs_2_, ...), custom_call_target="tpu_custom_call" | custom-call | flops 12000000000 | bytes 42000000 | tf_op jit(solution)/shard_map/local_sums/pallas_call | solution.py:461
  34.5 1.3 collective-permute-start.5
  35.8 1.8 %local_sums.5 = (f32[4,128,1024]{2,1,0:T(8,128)S(1)}, bf16[4,128,1024]{2,1,0:T(8,128)(2,1)S(1)}) custom-call(s32[11]{0:T(128)S(1)} %get-tuple-element.44.refs_0_.ids_ref, bf16[4,128,1024]{2,1,0:T(8,128)(2,1)S(1)} %get-tuple-element.53.refs_0_.refs_1_, bf16[4,128,512]{2,1,0:T(8,128)(2,1)S(1)} %reshape.20.refs_1_.refs_2_, ...), custom_call_target="tpu_custom_call" | custom-call | flops 12000000000 | bytes 42000000 | tf_op jit(solution)/shard_map/local_sums/pallas_call | solution.py:461
  38.3 1.3 collective-permute-start.8
  39.6 1.8 %local_sums.6 = (f32[4,128,1024]{2,1,0:T(8,128)S(1)}, bf16[4,128,1024]{2,1,0:T(8,128)(2,1)S(1)}) custom-call(s32[11]{0:T(128)S(1)} %get-tuple-element.44.refs_0_.ids_ref, bf16[4,128,1024]{2,1,0:T(8,128)(2,1)S(1)} %get-tuple-element.51.refs_0_.refs_1_, bf16[4,128,512]{2,1,0:T(8,128)(2,1)S(1)} %reshape.20.refs_1_.refs_2_, ...), custom_call_target="tpu_custom_call" | custom-call | flops 12000000000 | bytes 42000000 | tf_op jit(solution)/shard_map/local_sums/pallas_call | solution.py:461
  41.4 5.8 %collective-permute-done.6.refs_2_.refs_14_ = bf16[4,128,1024]{2,1,0:T(8,128)(2,1)S(1)} collective-permute-done((bf16[4,128,1024]{2,1,0:T(8,128)(2,1)S(1)}, bf16[4,128,1024]{2,1,0:T(8,128)(2,1)S(1)}, u32[]{:S(2)}, u32[]{:S(2)}) %collective-permute-start.6) | collective-permute-done | bytes 1048608 | tf_op jit(solution)/shard_map/ppermute | solution.py:455
  47.8 5.0 %collective-permute-start.10 = (bf16[4,128,1024]{2,1,0:T(8,128)(2,1)S(1)}, bf16[4,128,1024]{2,1,0:T(8,128)(2,1)S(1)}, u32[]{:S(2)}, u32[]{:S(2)}) collective-permute-start(bf16[4,128,1024]{2,1,0:T(8,128)(2,1)S(1)} %pass_down.3.refs_7_), channel_id=1, source_target_pairs={{4,0},{8,4},{12,8},{5,1},{9,5},{13,9},{6,2},{10,6},{14,10},{7,3},{... | collective-permute-start | bytes 3145736 | tf_op jit(solution)/shard_map/ppermute | solution.py:455
  53.6 1.9 %collective-permute-start.11 = (bf16[2,128,1024]{2,1,0:T(8,128)(2,1)S(1)}, bf16[2,128,1024]{2,1,0:T(8,128)(2,1)S(1)}, u32[]{:S(2)}, u32[]{:S(2)}) collective-permute-start(bf16[2,128,1024]{2,1,0:T(8,128)(2,1)S(1)} %pass_on.12.refs_9_), channel_id=1, source_target_pairs={{0,4},{4,8},{8,12},{1,5},{5,9},{9,13},{2,6},{6,10},{10,14},{3,7},{... | collective-permute-start | bytes 1572872 | tf_op jit(solution)/shard_map/ppermute | solution.py:412
  55.6 1.8 %local_sums.7 = (f32[4,128,1024]{2,1,0:T(8,128)S(1)}, bf16[4,128,1024]{2,1,0:T(8,128)(2,1)S(1)}) custom-call(s32[11]{0:T(128)S(1)} %get-tuple-element.44.refs_0_.ids_ref, bf16[4,128,1024]{2,1,0:T(8,128)(2,1)S(1)} %get-tuple-element.46.refs_0_.refs_1_, bf16[4,128,512]{2,1,0:T(8,128)(2,1)S(1)} %reshape.20.refs_1_.refs_2_, ...), custom_call_target="tpu_custom_call" | custom-call | flops 12000000000 | bytes 42000000 | tf_op jit(solution)/shard_map/local_sums/pallas_call | solution.py:461
  57.3 5.5 %collective-permute-done.8.refs_4_.refs_11_.refs_10_ = bf16[2,128,1024]{2,1,0:T(8,128)(2,1)S(1)} collective-permute-done((bf16[2,128,1024]{2,1,0:T(8,128)(2,1)S(1)}, bf16[2,128,1024]{2,1,0:T(8,128)(2,1)S(1)}, u32[]{:S(2)}, u32[]{:S(2)}) %collective-permute-start.8) | collective-permute-done | bytes 524320 | tf_op jit(solution)/shard_map/ppermute | solution.py:412
  63.6 1.9 %collective-permute-start.9 = (bf16[2,128,1024]{2,1,0:T(8,128)(2,1)S(1)}, bf16[2,128,1024]{2,1,0:T(8,128)(2,1)S(1)}, u32[]{:S(2)}, u32[]{:S(2)}) collective-permute-start(bf16[2,128,1024]{2,1,0:T(8,128)(2,1)S(1)} %pass_on.13.refs_7_), channel_id=1, source_target_pairs={{0,4},{4,8},{8,12},{1,5},{5,9},{9,13},{2,6},{6,10},{10,14},{3,7},{... | collective-permute-start | bytes 1572872 | tf_op jit(solution)/shard_map/ppermute | solution.py:412
  65.5 8.6 %collective-permute-done.11.refs_4_.refs_9_.refs_8_.refs_7_.refs_5_ = bf16[2,128,1024]{2,1,0:T(8,128)(2,1)S(1)} collective-permute-done((bf16[2,128,1024]{2,1,0:T(8,128)(2,1)S(1)}, bf16[2,128,1024]{2,1,0:T(8,128)(2,1)S(1)}, u32[]{:S(2)}, u32[]{:S(2)}) %collective-permute-start.11) | collective-permute-done | bytes 524320 | tf_op jit(solution)/shard_map/ppermute | solution.py:412
  74.1 0.9 pass_on.14.refs_7_
  74.9 1.9 %collective-permute-start.14 = (bf16[2,128,1024]{2,1,0:T(8,128)(2,1)S(1)}, bf16[2,128,1024]{2,1,0:T(8,128)(2,1)S(1)}, u32[]{:S(2)}, u32[]{:S(2)}) collective-permute-start(bf16[2,128,1024]{2,1,0:T(8,128)(2,1)S(1)} %pass_on.14.refs_7_), channel_id=1, source_target_pairs={{0,4},{4,8},{8,12},{1,5},{5,9},{9,13},{2,6},{6,10},{10,14},{3,7},{... | collective-permute-start | bytes 1572872 | tf_op jit(solution)/shard_map/ppermute | solution.py:412
  76.9 0.9 pass_down.4.refs_7_
  77.8 6.2 %collective-permute-start.13 = (bf16[4,128,1024]{2,1,0:T(8,128)(2,1)S(1)}, bf16[4,128,1024]{2,1,0:T(8,128)(2,1)S(1)}, u32[]{:S(2)}, u32[]{:S(2)}) collective-permute-start(bf16[4,128,1024]{2,1,0:T(8,128)(2,1)S(1)} %pass_down.4.refs_7_), channel_id=1, source_target_pairs={{4,0},{8,4},{12,8},{5,1},{9,5},{13,9},{6,2},{10,6},{14,10},{7,3},{... | collective-permute-start | bytes 3145736 | tf_op jit(solution)/shard_map/ppermute | solution.py:455
  84.0 1.3 collective-permute-done.9.refs_4_.refs_12_.refs_11_.refs_10_.refs_6_
  86.1 1.9 %collective-permute-start.12 = (bf16[2,128,1024]{2,1,0:T(8,128)(2,1)S(1)}, bf16[2,128,1024]{2,1,0:T(8,128)(2,1)S(1)}, u32[]{:S(2)}, u32[]{:S(2)}) collective-permute-start(bf16[2,128,1024]{2,1,0:T(8,128)(2,1)S(1)} %pass_on.15.refs_15_), channel_id=1, source_target_pairs={{0,4},{4,8},{8,12},{1,5},{5,9},{9,13},{2,6},{6,10},{10,14},{3,7},{... | collective-permute-start | bytes 1572872 | tf_op jit(solution)/shard_map/ppermute | solution.py:412
  88.1 2.6 %finish.5 = (bf16[4,128,4096]{2,1,0:T(8,128)(2,1)}, f32[8,128]{1,0:T(8,128)S(1)}) custom-call(s32[11]{0:T(128)S(1)} %get-tuple-element.44.refs_0_.ids_ref, f32[4,128,1024]{2,1,0:T(8,128)S(1)} %get-tuple-element.64.refs_6_.refs_1_, bf16[4,128,1024]{2,1,0:T(8,128)(2,1)S(1)} %get-tuple-element.72.refs_2_, bf16[4,128,512]{2,1,0:T(8,128)(2,1)S(1)} %reshape.21.refs_2_.refs_3_, ...), custom_call_target="tpu_custom_call" | custom-call | flops 16000000000 | bytes 56000000 | tf_op jit(solution)/shard_map/finish/pallas_call | solution.py:556
  90.6 5.9 %collective-permute-done.14.refs_3_.refs_9_.refs_8_.refs_7_ = bf16[2,128,1024]{2,1,0:T(8,128)(2,1)S(1)} collective-permute-done((bf16[2,128,1024]{2,1,0:T(8,128)(2,1)S(1)}, bf16[2,128,1024]{2,1,0:T(8,128)(2,1)S(1)}, u32[]{:S(2)}, u32[]{:S(2)}) %collective-permute-start.14) | collective-permute-done | bytes 524320 | tf_op jit(solution)/shard_map/ppermute | solution.py:412
  97.3 1.9 %collective-permute-start.16 = (bf16[2,128,1024]{2,1,0:T(8,128)(2,1)S(1)}, bf16[2,128,1024]{2,1,0:T(8,128)(2,1)S(1)}, u32[]{:S(2)}, u32[]{:S(2)}) collective-permute-start(bf16[2,128,1024]{2,1,0:T(8,128)(2,1)S(1)} %pass_on.16.refs_9_), channel_id=1, source_target_pairs={{4,8},{8,12},{5,9},{9,13},{6,10},{10,14},{7,11},{11,15},{20,24},{2... | collective-permute-start | bytes 1572872 | tf_op jit(solution)/shard_map/ppermute | solution.py:412
  99.2 2.8 %collective-permute-done.13.refs_2_.refs_16_ = bf16[4,128,1024]{2,1,0:T(8,128)(2,1)S(1)} collective-permute-done((bf16[4,128,1024]{2,1,0:T(8,128)(2,1)S(1)}, bf16[4,128,1024]{2,1,0:T(8,128)(2,1)S(1)}, u32[]{:S(2)}, u32[]{:S(2)}) %collective-permute-start.13) | collective-permute-done | bytes 1048608 | tf_op jit(solution)/shard_map/ppermute | solution.py:455
  102.0 0.9 pass_down.5.refs_6_
  102.9 4.4 %collective-permute-start.18 = (bf16[4,128,1024]{2,1,0:T(8,128)(2,1)S(1)}, bf16[4,128,1024]{2,1,0:T(8,128)(2,1)S(1)}, u32[]{:S(2)}, u32[]{:S(2)}) collective-permute-start(bf16[4,128,1024]{2,1,0:T(8,128)(2,1)S(1)} %pass_down.5.refs_6_), channel_id=1, source_target_pairs={{4,0},{8,4},{12,8},{5,1},{9,5},{13,9},{6,2},{10,6},{14,10},{7,3},{... | collective-permute-start | bytes 3145736 | tf_op jit(solution)/shard_map/ppermute | solution.py:455
  108.5 1.9 %collective-permute-start.15 = (bf16[2,128,1024]{2,1,0:T(8,128)(2,1)S(1)}, bf16[2,128,1024]{2,1,0:T(8,128)(2,1)S(1)}, u32[]{:S(2)}, u32[]{:S(2)}) collective-permute-start(bf16[2,128,1024]{2,1,0:T(8,128)(2,1)S(1)} %pass_on.17.refs_16_), channel_id=1, source_target_pairs={{4,8},{8,12},{5,9},{9,13},{6,10},{10,14},{7,11},{11,15},{20,24},{2... | collective-permute-start | bytes 1572872 | tf_op jit(solution)/shard_map/ppermute | solution.py:412
  110.4 3.0 %finish.6 = (bf16[4,128,4096]{2,1,0:T(8,128)(2,1)}, f32[8,128]{1,0:T(8,128)S(1)}) custom-call(s32[11]{0:T(128)S(1)} %get-tuple-element.44.refs_0_.ids_ref, f32[4,128,1024]{2,1,0:T(8,128)S(1)} %get-tuple-element.66.refs_6_.refs_1_, bf16[4,128,1024]{2,1,0:T(8,128)(2,1)S(1)} %get-tuple-element.74.refs_2_, ...), custom_call_target="tpu_custom_call", output_to_operand_aliasing={{0}: (17, {})} | custom-call | flops 16000000000 | bytes 56000000 | tf_op jit(solution)/shard_map/finish/pallas_call | solution.py:556
  113.4 5.6 %collective-permute-done.16.refs_2_.refs_9_.refs_8_.refs_7_ = bf16[2,128,1024]{2,1,0:T(8,128)(2,1)S(1)} collective-permute-done((bf16[2,128,1024]{2,1,0:T(8,128)(2,1)S(1)}, bf16[2,128,1024]{2,1,0:T(8,128)(2,1)S(1)}, u32[]{:S(2)}, u32[]{:S(2)}) %collective-permute-start.16) | collective-permute-done | bytes 524320 | tf_op jit(solution)/shard_map/ppermute | solution.py:412
  119.7 1.3 collective-permute-start.19
  121.0 7.3 %collective-permute-done.15.refs_2_.refs_12_.refs_8_ = bf16[2,128,1024]{2,1,0:T(8,128)(2,1)S(1)} collective-permute-done((bf16[2,128,1024]{2,1,0:T(8,128)(2,1)S(1)}, bf16[2,128,1024]{2,1,0:T(8,128)(2,1)S(1)}, u32[]{:S(2)}, u32[]{:S(2)}) %collective-permute-start.15) | collective-permute-done | bytes 524320 | tf_op jit(solution)/shard_map/ppermute | solution.py:412
  129.0 1.3 collective-permute-start.17
  130.3 2.8 %finish.7 = (bf16[4,128,4096]{2,1,0:T(8,128)(2,1)}, f32[8,128]{1,0:T(8,128)S(1)}) custom-call(s32[11]{0:T(128)S(1)} %get-tuple-element.44.refs_0_.ids_ref, f32[4,128,1024]{2,1,0:T(8,128)S(1)} %get-tuple-element.67.refs_5_.refs_1_, bf16[4,128,1024]{2,1,0:T(8,128)(2,1)S(1)} %get-tuple-element.77.refs_2_, ...), custom_call_target="tpu_custom_call", output_to_operand_aliasing={{0}: (18, {})} | custom-call | flops 16000000000 | bytes 56000000 | tf_op jit(solution)/shard_map/finish/pallas_call | solution.py:556
  133.2 2.0 %finish.8 = (bf16[4,128,4096]{2,1,0:T(8,128)(2,1)}, f32[8,128]{1,0:T(8,128)S(1)}) custom-call(s32[11]{0:T(128)S(1)} %get-tuple-element.44.refs_0_.ids_ref, f32[4,128,1024]{2,1,0:T(8,128)S(1)} %get-tuple-element.68.refs_7_.refs_1_, bf16[4,128,1024]{2,1,0:T(8,128)(2,1)S(1)} %get-tuple-element.69.refs_2_, ...), custom_call_target="tpu_custom_call", output_to_operand_aliasing={{0}: (12, {})} | custom-call | flops 16000000000 | bytes 56000000 | tf_op jit(solution)/shard_map/finish/pallas_call | solution.py:556
  135.2 2.7 %final_states.1 = (f32[4,1024,128]{2,1,0:T(8,128)}, f32[8,128]{1,0:T(8,128)S(1)}) custom-call(s32[11]{0:T(128)S(1)} %get-tuple-element.44.refs_0_.ids_ref, f32[4,4,1,4096]{3,2,1,0:T(1,128)S(1)} %decays.1.refs_3_.refs_4_.refs_1_.refs_5_.refs_6_.refs_0_, bf16[4,128,1024]{2,1,0:T(8,128)(2,1)S(1)} %get-tuple-element.56.refs_7_.refs_5_.refs_6_.refs_13_.refs_4_.refs_10_.refs_1_, ...), custom_call_target="tpu_custom_call" | custom-call | flops 10800000000 | bytes 37800000 | tf_op jit(solution)/shard_map/final_states/pallas_call | solution.py:613
  137.9 3.8 %collective-permute-done.17.refs_9_ = bf16[2,128,1024]{2,1,0:T(8,128)(2,1)S(1)} collective-permute-done((bf16[2,128,1024]{2,1,0:T(8,128)(2,1)S(1)}, bf16[2,128,1024]{2,1,0:T(8,128)(2,1)S(1)}, u32[]{:S(2)}, u32[]{:S(2)}) %collective-permute-start.17) | collective-permute-done | bytes 524320 | tf_op jit(solution)/shard_map/ppermute | solution.py:412
  141.7 2.5 %finish.9 = (bf16[4,128,4096]{2,1,0:T(8,128)(2,1)}, f32[8,128]{1,0:T(8,128)}) custom-call(s32[11]{0:T(128)S(1)} %get-tuple-element.44.refs_0_.ids_ref, f32[4,128,1024]{2,1,0:T(8,128)S(1)} %get-tuple-element.68.refs_7_.refs_1_, bf16[4,128,1024]{2,1,0:T(8,128)(2,1)S(1)} %get-tuple-element.69.refs_2_, ...), custom_call_target="tpu_custom_call", output_to_operand_aliasing={{0}: (12, {})} | custom-call | flops 16000000000 | bytes 56000000 | tf_op jit(solution)/shard_map/finish/pallas_call | solution.py:556
  (33 shorter events, 9.6 us)
Async XLA Ops:
  0.6 9.4 %collective-permute-start.2 = (bf16[4,64,128]{2,1,0:T(8,128)(2,1)}, bf16[4,64,128]{2,1,0:T(8,128)(2,1)S(1)}, u32[]{:S(2)}, u32[]{:S(2)}) collective-permute-start(bf16[4,64,128]{2,1,0:T(8,128)(2,1)} %bitcast.14), channel_id=1, source_target_pairs={{0,12},{4,0},{8,4},{12,8},{1,13},{5,1},{9,5},{13,9},{2,14},{6,2},{... | collective-permute-start | bytes 196616 | tf_op jit(solution)/shard_map/ppermute | solution.py:299
  1.1 8.9 %collective-permute-start.1 = (bf16[4,64,128]{2,1,0:T(8,128)(2,1)}, bf16[4,64,128]{2,1,0:T(8,128)(2,1)S(1)}, u32[]{:S(2)}, u32[]{:S(2)}) collective-permute-start(bf16[4,64,128]{2,1,0:T(8,128)(2,1)} %bitcast.15), channel_id=1, source_target_pairs={{0,8},{4,12},{8,0},{12,4},{1,9},{5,13},{9,1},{13,5},{2,10},{6,14},... | collective-permute-start | bytes 196616 | tf_op jit(solution)/shard_map/ppermute | solution.py:299
  4.6 5.5 %collective-permute-start = (bf16[4,64,128]{2,1,0:T(8,128)(2,1)}, bf16[4,64,128]{2,1,0:T(8,128)(2,1)S(1)}, u32[]{:S(2)}, u32[]{:S(2)}) collective-permute-start(bf16[4,64,128]{2,1,0:T(8,128)(2,1)} %bitcast.16), channel_id=1, source_target_pairs={{0,4},{4,8},{8,12},{12,0},{1,5},{5,9},{9,13},{13,1},{2,6},{6,10},{... | collective-permute-start | bytes 196616 | tf_op jit(solution)/shard_map/ppermute | solution.py:299
  5.9 13.2 %collective-permute-start.3 = (bf16[2,16,64,128]{3,2,1,0:T(8,128)(2,1)S(1)}, bf16[2,16,64,128]{3,2,1,0:T(8,128)(2,1)S(1)}, u32[]{:S(2)}, u32[]{:S(2)}) collective-permute-start(bf16[2,16,64,128]{3,2,1,0:T(8,128)(2,1)S(1)} %fusion), channel_id=1, source_target_pairs={{0,2},{2,0},{1,3},{3,1},{4,6},{6,4},{5,7},{7,5},{8,10},{10,8},{9,1... | collective-permute-start | bytes 1572872 | tf_op jit(solution)/shard_map/ppermute | solution.py:295
  10.1 9.0 %copy-start.1 = (s32[8]{0:T(128)S(1)}, s32[8]{0:T(128)}, u32[]{:S(2)}) copy-start(s32[8]{0:T(128)} %refs_1_.1) | copy-start | bytes 100
  10.1 9.0 %copy-start.2 = (s32[4]{0:T(128)S(1)}, s32[4]{0:T(128)}, u32[]{:S(2)}) copy-start(s32[4]{0:T(128)} %refs_2_.1) | copy-start | bytes 52
  10.2 9.0 %copy-start.3 = (s32[4]{0:T(128)S(1)}, s32[4]{0:T(128)}, u32[]{:S(2)}) copy-start(s32[4]{0:T(128)} %refs_3_.3) | copy-start | bytes 52
  15.0 18.9 %collective-permute-start.4 = (bf16[2,128,1024]{2,1,0:T(8,128)(2,1)S(1)}, bf16[2,128,1024]{2,1,0:T(8,128)(2,1)S(1)}, u32[]{:S(2)}, u32[]{:S(2)}) collective-permute-start(bf16[2,128,1024]{2,1,0:T(8,128)(2,1)S(1)} %get-tuple-element.60.refs_2_.refs_3_.refs_9_), channel_id=1, source_target_pairs={{0,4},{1,5},{2,6},{3,7},{16,20},{17,21},{18,22},{19,23}} | collective-permute-start | bytes 1572872 | tf_op jit(solution)/shard_map/ppermute | solution.py:412
  15.7 21.8 %collective-permute-start.7 = (bf16[2,128,1024]{2,1,0:T(8,128)(2,1)S(1)}, bf16[2,128,1024]{2,1,0:T(8,128)(2,1)S(1)}, u32[]{:S(2)}, u32[]{:S(2)}) collective-permute-start(bf16[2,128,1024]{2,1,0:T(8,128)(2,1)S(1)} %get-tuple-element.45.refs_7_.refs_2_.refs_3_.refs_4_.refs_10_), channel_id=1, source_target_pairs={{0,4},{1,5},{2,6},{3,7},{16,20},{17,21},{18,22},{19,23}} | collective-permute-start | bytes 1572872 | tf_op jit(solution)/shard_map/ppermute | solution.py:412
  19.1 6.4 %copy-start = (bf16[4,128,64]{1,2,0:T(8,128)(2,1)S(1)}, bf16[4,128,64]{1,2,0:T(8,128)(2,1)}, u32[]{:S(2)}) copy-start(bf16[4,128,64]{1,2,0:T(8,128)(2,1)} %param.18) | copy-start | bytes 196612
  21.8 25.4 %collective-permute-start.6 = (bf16[4,128,1024]{2,1,0:T(8,128)(2,1)S(1)}, bf16[4,128,1024]{2,1,0:T(8,128)(2,1)S(1)}, u32[]{:S(2)}, u32[]{:S(2)}) collective-permute-start(bf16[4,128,1024]{2,1,0:T(8,128)(2,1)S(1)} %get-tuple-element.56.refs_7_.refs_5_.refs_6_.refs_13_.refs_4_.refs_10_.refs_1_), channel_id=1, source_target_pairs={{4,0},{8,4},{12,8},{5,1},{9,5},{13,9},{6,2},{10,6},{14,10},{7,3},{... | collective-permute-start | bytes 3145736 | tf_op jit(solution)/shard_map/ppermute | solution.py:455
  34.5 18.4 %collective-permute-start.5 = (bf16[2,128,1024]{2,1,0:T(8,128)(2,1)S(1)}, bf16[2,128,1024]{2,1,0:T(8,128)(2,1)S(1)}, u32[]{:S(2)}, u32[]{:S(2)}) collective-permute-start(bf16[2,128,1024]{2,1,0:T(8,128)(2,1)S(1)} %pass_on.10.refs_9_), channel_id=1, source_target_pairs={{0,4},{4,8},{1,5},{5,9},{2,6},{6,10},{3,7},{7,11},{16,20},{20,24},... | collective-permute-start | bytes 1572872 | tf_op jit(solution)/shard_map/ppermute | solution.py:412
  38.3 24.5 %collective-permute-start.8 = (bf16[2,128,1024]{2,1,0:T(8,128)(2,1)S(1)}, bf16[2,128,1024]{2,1,0:T(8,128)(2,1)S(1)}, u32[]{:S(2)}, u32[]{:S(2)}) collective-permute-start(bf16[2,128,1024]{2,1,0:T(8,128)(2,1)S(1)} %pass_on.11.refs_9_), channel_id=1, source_target_pairs={{0,4},{4,8},{1,5},{5,9},{2,6},{6,10},{3,7},{7,11},{16,20},{20,24},... | collective-permute-start | bytes 1572872 | tf_op jit(solution)/shard_map/ppermute | solution.py:412
  47.8 29.0 %collective-permute-start.10 = (bf16[4,128,1024]{2,1,0:T(8,128)(2,1)S(1)}, bf16[4,128,1024]{2,1,0:T(8,128)(2,1)S(1)}, u32[]{:S(2)}, u32[]{:S(2)}) collective-permute-start(bf16[4,128,1024]{2,1,0:T(8,128)(2,1)S(1)} %pass_down.3.refs_7_), channel_id=1, source_target_pairs={{4,0},{8,4},{12,8},{5,1},{9,5},{13,9},{6,2},{10,6},{14,10},{7,3},{... | collective-permute-start | bytes 3145736 | tf_op jit(solution)/shard_map/ppermute | solution.py:455
  53.6 20.4 %collective-permute-start.11 = (bf16[2,128,1024]{2,1,0:T(8,128)(2,1)S(1)}, bf16[2,128,1024]{2,1,0:T(8,128)(2,1)S(1)}, u32[]{:S(2)}, u32[]{:S(2)}) collective-permute-start(bf16[2,128,1024]{2,1,0:T(8,128)(2,1)S(1)} %pass_on.12.refs_9_), channel_id=1, source_target_pairs={{0,4},{4,8},{8,12},{1,5},{5,9},{9,13},{2,6},{6,10},{10,14},{3,7},{... | collective-permute-start | bytes 1572872 | tf_op jit(solution)/shard_map/ppermute | solution.py:412
  63.6 21.7 %collective-permute-start.9 = (bf16[2,128,1024]{2,1,0:T(8,128)(2,1)S(1)}, bf16[2,128,1024]{2,1,0:T(8,128)(2,1)S(1)}, u32[]{:S(2)}, u32[]{:S(2)}) collective-permute-start(bf16[2,128,1024]{2,1,0:T(8,128)(2,1)S(1)} %pass_on.13.refs_7_), channel_id=1, source_target_pairs={{0,4},{4,8},{8,12},{1,5},{5,9},{9,13},{2,6},{6,10},{10,14},{3,7},{... | collective-permute-start | bytes 1572872 | tf_op jit(solution)/shard_map/ppermute | solution.py:412
  74.9 21.6 %collective-permute-start.14 = (bf16[2,128,1024]{2,1,0:T(8,128)(2,1)S(1)}, bf16[2,128,1024]{2,1,0:T(8,128)(2,1)S(1)}, u32[]{:S(2)}, u32[]{:S(2)}) collective-permute-start(bf16[2,128,1024]{2,1,0:T(8,128)(2,1)S(1)} %pass_on.14.refs_7_), channel_id=1, source_target_pairs={{0,4},{4,8},{8,12},{1,5},{5,9},{9,13},{2,6},{6,10},{10,14},{3,7},{... | collective-permute-start | bytes 1572872 | tf_op jit(solution)/shard_map/ppermute | solution.py:412
  77.8 24.2 %collective-permute-start.13 = (bf16[4,128,1024]{2,1,0:T(8,128)(2,1)S(1)}, bf16[4,128,1024]{2,1,0:T(8,128)(2,1)S(1)}, u32[]{:S(2)}, u32[]{:S(2)}) collective-permute-start(bf16[4,128,1024]{2,1,0:T(8,128)(2,1)S(1)} %pass_down.4.refs_7_), channel_id=1, source_target_pairs={{4,0},{8,4},{12,8},{5,1},{9,5},{13,9},{6,2},{10,6},{14,10},{7,3},{... | collective-permute-start | bytes 3145736 | tf_op jit(solution)/shard_map/ppermute | solution.py:455
  86.1 21.6 %collective-permute-start.12 = (bf16[2,128,1024]{2,1,0:T(8,128)(2,1)S(1)}, bf16[2,128,1024]{2,1,0:T(8,128)(2,1)S(1)}, u32[]{:S(2)}, u32[]{:S(2)}) collective-permute-start(bf16[2,128,1024]{2,1,0:T(8,128)(2,1)S(1)} %pass_on.15.refs_15_), channel_id=1, source_target_pairs={{0,4},{4,8},{8,12},{1,5},{5,9},{9,13},{2,6},{6,10},{10,14},{3,7},{... | collective-permute-start | bytes 1572872 | tf_op jit(solution)/shard_map/ppermute | solution.py:412
  97.3 21.7 %collective-permute-start.16 = (bf16[2,128,1024]{2,1,0:T(8,128)(2,1)S(1)}, bf16[2,128,1024]{2,1,0:T(8,128)(2,1)S(1)}, u32[]{:S(2)}, u32[]{:S(2)}) collective-permute-start(bf16[2,128,1024]{2,1,0:T(8,128)(2,1)S(1)} %pass_on.16.refs_9_), channel_id=1, source_target_pairs={{4,8},{8,12},{5,9},{9,13},{6,10},{10,14},{7,11},{11,15},{20,24},{2... | collective-permute-start | bytes 1572872 | tf_op jit(solution)/shard_map/ppermute | solution.py:412
  102.9 32.3 %collective-permute-start.18 = (bf16[4,128,1024]{2,1,0:T(8,128)(2,1)S(1)}, bf16[4,128,1024]{2,1,0:T(8,128)(2,1)S(1)}, u32[]{:S(2)}, u32[]{:S(2)}) collective-permute-start(bf16[4,128,1024]{2,1,0:T(8,128)(2,1)S(1)} %pass_down.5.refs_6_), channel_id=1, source_target_pairs={{4,0},{8,4},{12,8},{5,1},{9,5},{13,9},{6,2},{10,6},{14,10},{7,3},{... | collective-permute-start | bytes 3145736 | tf_op jit(solution)/shard_map/ppermute | solution.py:455
  108.5 19.8 %collective-permute-start.15 = (bf16[2,128,1024]{2,1,0:T(8,128)(2,1)S(1)}, bf16[2,128,1024]{2,1,0:T(8,128)(2,1)S(1)}, u32[]{:S(2)}, u32[]{:S(2)}) collective-permute-start(bf16[2,128,1024]{2,1,0:T(8,128)(2,1)S(1)} %pass_on.17.refs_16_), channel_id=1, source_target_pairs={{4,8},{8,12},{5,9},{9,13},{6,10},{10,14},{7,11},{11,15},{20,24},{2... | collective-permute-start | bytes 1572872 | tf_op jit(solution)/shard_map/ppermute | solution.py:412
  119.7 13.5 %collective-permute-start.19 = (bf16[2,128,1024]{2,1,0:T(8,128)(2,1)S(1)}, bf16[2,128,1024]{2,1,0:T(8,128)(2,1)S(1)}, u32[]{:S(2)}, u32[]{:S(2)}) collective-permute-start(bf16[2,128,1024]{2,1,0:T(8,128)(2,1)S(1)} %pass_on.18.refs_5_), channel_id=1, source_target_pairs={{8,12},{9,13},{10,14},{11,15},{24,28},{25,29},{26,30},{27,31}} | collective-permute-start | bytes 1572872 | tf_op jit(solution)/shard_map/ppermute | solution.py:412
  129.0 12.7 %collective-permute-start.17 = (bf16[2,128,1024]{2,1,0:T(8,128)(2,1)S(1)}, bf16[2,128,1024]{2,1,0:T(8,128)(2,1)S(1)}, u32[]{:S(2)}, u32[]{:S(2)}) collective-permute-start(bf16[2,128,1024]{2,1,0:T(8,128)(2,1)S(1)} %pass_on.19.refs_17_), channel_id=1, source_target_pairs={{8,12},{9,13},{10,14},{11,15},{24,28},{25,29},{26,30},{27,31}} | collective-permute-start | bytes 1572872 | tf_op jit(solution)/shard_map/ppermute | solution.py:412

commit v4 on v3

--- a/solution.py
+++ b/solution.py
@@ -86,14 +86,14 @@
 
 
 def front_body(
-    order, ids, b_ref, c_ref, spans_hbm, dt_hbm, bias_hbm, alog_hbm, skip_hbm, gain_hbm, x_hbm, info, cum_ref, cum_t_ref,
-    step_t_ref, weight_ref, growth_ref, x_ref, bias_ref, alog_ref, skip_ref, gain_ref, *rest
+    order, ids, spans_hbm, b_hbm, dt_hbm, bias_hbm, alog_hbm, skip_hbm, gain_hbm, x_hbm, info, cum_ref, cum_t_ref,
+    step_t_ref, weight_ref, growth_ref, x_ref, b_ref, dt_ref, bias_ref, alog_ref, skip_ref, gain_ref, *rest
 ):
-    outs, (dt_ref, spans, small_sems, x_sem) = rest[:-4], rest[-4:]
+    outs, (raw_b, spans, small_sems, x_sem) = rest[:-4], rest[-4:]
     requests, heads_here, span = dt_ref.shape
     pairs = (
         (spans_hbm, spans), (dt_hbm, dt_ref), (bias_hbm, bias_ref), (alog_hbm, alog_ref), (skip_hbm, skip_ref),
-        (gain_hbm, gain_ref),
+        (gain_hbm, gain_ref), (b_hbm, raw_b),
     )
     small = [pltpu.make_async_copy(source, target, small_sems.at[i]) for i, (source, target) in enumerate(pairs)]
     x_copy = pltpu.make_async_copy(x_hbm.at[:, :, pl.ds(order[0] * GROUP_LANES, GROUP_LANES)], x_ref, x_sem)
@@ -125,6 +125,8 @@
             growth_ref[r, g] = growth[:, here]
             cum_t_ref[r, g] = cum_t[here, :]
             step_t_ref[r, g] = step_t[here, :]
+    for r in range(requests):
+        b_ref[r] = raw_b[r].reshape(b_ref.shape[1:])
     x_copy.wait()
     block_body(order[0], x_ref, b_ref, weight_ref, *outs)
 
@@ -218,13 +220,8 @@
     z_copy.wait()
 
 
-def parents_body(order, requests, unit, info, parent, state_dev, state_slot, cache_hbm, x_hbm, *refs):
-    n_later = len(order) - 1
-    pieces, (out_ref, *x_refs), (rows, sems, x_sems) = refs[: -4 - n_later], refs[-4 - n_later : -3], refs[-3:]
-    x_copies = [
-        pltpu.make_async_copy(x_hbm.at[:, :, pl.ds(group * GROUP_LANES, GROUP_LANES)], x_refs[i], x_sems.at[i])
-        for i, group in enumerate(order[1:])
-    ]
+def parents_body(requests, info, parent, state_dev, state_slot, cache_hbm, *refs):
+    pieces, (out_ref, rows, sems) = refs[:-3], refs[-3:]
     holders = len(pieces) + 1
     places = []
     for r in range(requests):
@@ -240,8 +237,6 @@
 
     for r in range(requests):
         own(r, lambda copy: copy.start())
-    for copy in x_copies:
-        copy.start()
     for r in range(requests):
         shift, slot = places[r]
         for n, piece in enumerate(pieces):
@@ -255,9 +250,6 @@
         @pl.when(shift == 0)
         def _(r=r):
             out_ref[r] = rows[r].astype(BF16).T
-
-    for copy in x_copies:
-        copy.wait()
 
 
 def chain_lanes(group, device, unit):
@@ -280,96 +272,102 @@
     parts = requests // REQ_CHUNK
     chunks = groups * parts
     unit = width // toks
-    order = [(i + 1) % groups for i in range(groups)]
+    order = [(i + 2) % groups for i in range(groups)]
     where = {group: i for i, group in enumerate(order)}
     assert span == SPAN and GROUP_LANES % unit == 0
 
     ids = jnp.stack([me, lax.axis_index("rep"), lax.axis_index("cache")]).astype(jnp.int32)
 
 
-    slots_here = cache_states.shape[0]
-    pieces = []
-    for shift in range(1, holders):
-        towards = lax.rem(lax.axis_index("cache") + shift, holders)
-        piece = lax.dynamic_index_in_dim(cache_states, towards, 1, keepdims=False).astype(BF16)
-        piece = lax.ppermute(piece, "cache", [(i, (i + shift) % holders) for i in range(holders)])
-        pieces.append(pin(piece.reshape(slots_here, unit, STATE)))
     dt_t = dt_in.transpose(0, 2, 1)
-    all_dt = [dt_t] + [
-        lax.ppermute(dt_t, "tok", [(k, (k + shift) % toks) for k in range(toks)]) for shift in range(1, toks)
-    ]
-
-    b_flat = pin(b_in.reshape(requests, span, groups * STATE))
-    c_flat = pin(c_in.reshape(requests, span, groups * STATE))
+    flat = VMEM((requests, span, groups * STATE), BF16)
     columns = VMEM((requests, groups, span, PER_GROUP), F32)
     as_rows = VMEM((requests, groups, PER_GROUP, span), F32)
     chunk_type = ((REQ_CHUNK, STATE, GROUP_LANES), BF16)
     smem_spec, vmem_spec, any_spec, hbm_spec = (
         pl.BlockSpec(memory_space=space) for space in (SMEM, VMEM, pl.ANY, pltpu.HBM)
     )
-    info, cum, cum_t, step_t, weight, growth, x_first, bias, rates, skip, gain, *found = pl.pallas_call(
-        lambda *refs: front_body(order, *refs[:10], *refs[9 + toks :]),
+    info, cum, cum_t, step_t, weight, growth, x_first, b_flat, dt_here, bias, rates, skip, gain, *found = pl.pallas_call(
+        functools.partial(front_body, order),
         out_shape=(
             jax.ShapeDtypeStruct((3 + 2 * requests,), jnp.int32),
-            columns, as_rows, as_rows, columns, columns, VMEM((requests, span, GROUP_LANES), BF16),
+            columns, as_rows, as_rows, columns, columns, VMEM((requests, span, GROUP_LANES), BF16), flat, VMEM(dt_t.shape, BF16),
             *(VMEM((1, heads_here), F32),) * 3, VMEM((1, width), F32), *(VMEM(*chunk_type),) * parts,
         ),
-        in_specs=[smem_spec] + [vmem_spec] * 2 + [hbm_spec] * 7 + [vmem_spec] * (toks - 1),
-        out_specs=(smem_spec,) + (vmem_spec,) * (10 + parts),
+        in_specs=[smem_spec] + [hbm_spec] * 8,
+        out_specs=(smem_spec,) + (vmem_spec,) * (12 + parts),
         scratch_shapes=[
-            VMEM(dt_t.shape, BF16), SMEM(spans.shape, jnp.int32),
-            pltpu.SemaphoreType.DMA((6,)), pltpu.SemaphoreType.DMA,
+            VMEM(b_in.shape, BF16), SMEM(spans.shape, jnp.int32),
+            pltpu.SemaphoreType.DMA((7,)), pltpu.SemaphoreType.DMA,
         ],
         compiler_params=pltpu.CompilerParams(vmem_limit_bytes=12 << 20),
         cost_estimate=takes(5.0),
         name="front",
     )(
         ids,
-        b_flat,
-        c_flat,
-        *map(in_hbm, (spans, dt_t, dt_bias[None], a_log[None], skip_gain[None], norm_w[None], x_in)),
-        *map(pin, all_dt[1:]),
+        *map(in_hbm, (spans, b_in, dt_t, dt_bias[None], a_log[None], skip_gain[None], norm_w[None], x_in)),
     )
     states = {part: found[part] for part in range(parts)}
     previous = found[-1]
 
-    initial, *x_groups = pl.pallas_call(
-        lambda *refs: parents_body(order, requests, unit, *refs[: 6 + len(pieces)], *refs[7 + len(pieces) :]),
-        out_shape=(VMEM((requests, STATE, unit), BF16),) + (VMEM(x_first.shape, BF16),) * (groups - 1),
-        in_specs=[smem_spec] * 4 + [hbm_spec] * 2 + [vmem_spec] * (len(pieces) + 1),
-        out_specs=(vmem_spec,) * groups,
+    slots_here = cache_states.shape[0]
+    cache_rows = in_hbm(cache_states.reshape(slots_here, holders, unit, STATE))
+
+    def load_body(info_ref, cache_hbm, x_hbm, c_hbm, _, *refs):
+        piece_refs, c_ref, x_refs = refs[: holders - 1], refs[holders - 1], refs[holders : holders + groups - 1]
+        rows_ref, raw_c, sems = refs[-3:]
+        copies = []
+        for n in range(holders - 1):
+            towards = lax.rem(info_ref[2] + n + 1, holders)
+            copies.append(pltpu.make_async_copy(cache_hbm.at[:, towards], rows_ref.at[n], sems.at[n]))
+        copies.append(pltpu.make_async_copy(c_hbm, raw_c, sems.at[holders - 1]))
+        for n, group in enumerate(order[1:]):
+            lanes = pl.ds(group * GROUP_LANES, GROUP_LANES)
+            copies.append(pltpu.make_async_copy(x_hbm.at[:, :, lanes], x_refs[n], sems.at[holders + n]))
+        for copy in copies:
+            copy.start()
+        for n in range(holders - 1):
+            copies[n].wait()
+            piece_refs[n][...] = rows_ref[n].astype(BF16)
+        copies[holders - 1].wait()
+        for r in range(requests):
+            c_ref[r] = raw_c[r].reshape(c_ref.shape[1:])
+        for copy in copies[holders:]:
+            copy.wait()
+
+    piece_type = (slots_here, unit, STATE)
+    loaded = pl.pallas_call(
+        load_body,
+        out_shape=(VMEM(piece_type, BF16),) * (holders - 1) + (flat,) + (VMEM(x_first.shape, BF16),) * (groups - 1),
+        in_specs=[smem_spec] + [hbm_spec] * 3 + [vmem_spec],
+        out_specs=(vmem_spec,) * (holders + groups - 1),
         scratch_shapes=[
-            VMEM((requests, unit, STATE), F32), pltpu.SemaphoreType.DMA((requests,)), pltpu.SemaphoreType.DMA((groups,)),
+            VMEM((holders - 1, *piece_type), F32), VMEM(c_in.shape, BF16), pltpu.SemaphoreType.DMA((holders + groups,)),
         ],
         compiler_params=pltpu.CompilerParams(vmem_limit_bytes=12 << 20),
-        cost_estimate=takes(2.8),
-        name="parents",
-    )(info, parent, state_dev, state_slot, in_hbm(cache_states.reshape(slots_here, holders, unit, STATE)), in_hbm(x_in),
-        *pieces, pin(previous))
-    x_groups = [x_first, *x_groups]
-    decays = call(
-        decay_body,
-        ((4, requests, 1, width), F32),
-        (*all_dt, bias, rates),
-        scalars=(info,),
-        after=(initial,),
-        name="decays",
-        us=1.7,
-    )
-
-    previous = decays
-    for i in range(1, groups):
+        cost_estimate=takes(3.0),
+        name="loads",
+    )(info, cache_rows, in_hbm(x_in), in_hbm(c_in), pin(previous))
+    all_dt = [dt_here] + [
+        lax.ppermute(dt_here, "tok", [(k, (k + shift) % toks) for k in range(toks)]) for shift in range(1, toks)
+    ]
+    pieces = [
+        pin(lax.ppermute(loaded[n], "cache", [(i, (i + n + 1) % holders) for i in range(holders)]))
+        for n in range(holders - 1)
+    ]
+    c_flat, x_groups = loaded[holders - 1], [x_first, *loaded[holders:]]
+    def find_states(i, after):
         found = call(
             functools.partial(block_body, order[i]),
             (chunk_type,) * parts,
             (x_groups[i], b_flat, weight),
-            after=(previous,),
+            after=after,
             name="block_states",
-            us=1.6,
+            us=0.4,
         )
         for part in range(parts):
             states[i * parts + part] = found[part]
-        previous = found[-1]
+        return found[-1]
 
     def decay_of(decays_ref, kind, r, group, lanes=slice(0, GROUP_LANES)):
         return decays_ref[kind, r, :, group * GROUP_LANES + lanes.start : group * GROUP_LANES + lanes.stop]
@@ -381,23 +379,30 @@
         if devices == [0] and chain_lanes(order[h // parts], 0, unit) is None:
             return states[h]
         incoming = [received[h - HOP]] if any(devices) else []
-        ins = [states[h - HOP * k] for k in devices] + incoming + [decays, initial]
+        merging = any(chain_lanes(order[(h - HOP * k) // parts], k, unit) is not None for k in devices)
+        ins = [states[h - HOP * k] for k in devices] + incoming + [growth] + (started[::-1] if merging else [])
 
         def body(ids_ref, *refs):
-            state_refs, incoming_refs = refs[: len(devices)], refs[len(devices) : -3]
-            decays_ref, initial_ref, out_ref = refs[-3:]
+            out_ref = refs[-1]
+            state_refs, refs = refs[: len(devices)], refs[len(devices) : -1]
+            incoming_ref, refs = (refs[0], refs[1:]) if incoming else (None, refs)
+            growth_ref = refs[0]
 
             def branch(n, device):
                 c = h - HOP * device
                 group, part = order[c // parts], c % parts
                 lanes = chain_lanes(group, device, unit)
+                low = low_half(1)
                 for i in range(REQ_CHUNK):
                     r = part * REQ_CHUNK + i
                     value = state_refs[n][i].astype(F32)
                     if device:
-                        value = value + decay_of(decays_ref, THROUGH, r, group) * incoming_refs[0][i].astype(F32)
+                        through = growth_ref[r, group, span - 1 : span, :]
+                        through = jnp.concatenate([spread_pair(through, q, low) for q in range(PAIRS)], axis=1)
+                        value = value + through * incoming_ref[i].astype(F32)
                     out_ref[i] = value.astype(BF16)
                     if lanes is not None:
+                        decays_ref, initial_ref = refs[1:]
                         mine = decay_of(decays_ref, BEFORE_THROUGH, r, group, lanes) * initial_ref[r].astype(F32)
                         out_ref[i, :, lanes] = (value[:, lanes] + mine).astype(BF16)
 
@@ -415,6 +420,7 @@
     backward = [(k, k - 1) for k in range(1, toks)]
 
     def send_down(s, after=()):
+        initial, decays = started
         sent = initial
         if s:
             used = sorted(
@@ -470,6 +476,7 @@
         )(info, *(pin(a) for a in ins), in_hbm(z_in), *(pin(a) for a in after))
 
     def init_for(group):
+        initial = started[0]
         if unit == GROUP_LANES:
             inits = [initial] + arrived[:group]
             return inits, [group - k if k <= group else None for k in range(toks)]
@@ -480,6 +487,7 @@
     def finish(i, these, y_so_far, after):
         group = order[i]
         inits, init_of = init_for(group)
+        decays = started[1]
         ahead = [received[i * parts + part + HOP * k] for part in these for k in range(toks - 1)]
         ins = [*local[i], c_flat, growth, gain, decays, *ahead, *inits]
         n_ahead, n_init = len(ahead), len(inits)
@@ -508,17 +516,21 @@
                         state_buf[n * REQ_CHUNK + j] = value.astype(BF16)
 
             on_device(info_ref[0], toks, merge)
-            copies = []
-            for n in range(count):
-                r = these[n // REQ_CHUNK] * REQ_CHUNK + n % REQ_CHUNK
+            def store(n):
+                target = y_ref.at[these[0] * REQ_CHUNK + n, :, pl.ds(group * GROUP_LANES, GROUP_LANES)]
+                return pltpu.make_async_copy(y_buf.at[n], target, sems.at[n])
+
+            @pl.loop(0, count)
+            def _(n):
+                r = these[0] * REQ_CHUNK + n
                 valid = info_ref[3 + r] > 0
 
                 @pl.when(jnp.logical_not(valid))
-                def _(n=n):
-                    y_buf[n] = jnp.zeros_like(y_buf[n])
+                def _():
+                    y_buf[n] = jnp.zeros((span, GROUP_LANES), BF16)
 
                 @pl.when(valid)
-                def _(n=n, r=r):
+                def _():
                     low = low_half(span)
                     c_here = c_ref[r, :, group * STATE : (group + 1) * STATE]
                     carried = jnp.dot(c_here, state_buf[n], preferred_element_type=F32)
@@ -534,18 +546,15 @@
                         squares = squares + value * value
                     inverse = lax.rsqrt(jnp.sum(squares, axis=1, keepdims=True) * (1.0 / GROUP_LANES) + EPS)
                     for q in range(PAIRS):
-                        gain = gain_ref[:, group * GROUP_LANES + q * PAIR_LANES : group * GROUP_LANES + (q + 1) * PAIR_LANES]
-                        y_buf[n, :, pair_lanes(q)] = (gated[q] * inverse * gain).astype(BF16)
-
-                copy = pltpu.make_async_copy(
-                    y_buf.at[n],
-                    y_ref.at[r, :, pl.ds(group * GROUP_LANES, GROUP_LANES)],
-                    sems.at[n],
-                )
-                copy.start()
-                copies.append(copy)
-            for copy in copies:
-                copy.wait()
+                        first = group * GROUP_LANES + q * PAIR_LANES
+                        gain_here = gain_ref[:, first : first + PAIR_LANES]
+                        y_buf[n, :, pair_lanes(q)] = (gated[q] * inverse * gain_here).astype(BF16)
+
+                store(n).start()
+
+            @pl.loop(0, count)
+            def _(n):
+                store(n).wait()
 
         n_after = len(after)
 
@@ -570,6 +579,7 @@
         )(info, *pinned, *([y_so_far] if had else []))
 
     def final_states(after):
+        initial, decays = started
         ahead = {}
         for k in range(1, toks):
             i = where[k * unit // GROUP_LANES]
@@ -624,25 +634,60 @@
 
     slots = chunks + HOP * (toks - 2)
     lag = HOP * (toks - 2) + parts
+    started = []
+
+    def start_parents(previous):
+        initial = pl.pallas_call(
+            lambda *refs: parents_body(requests, *refs[: 5 + len(pieces)], *refs[6 + len(pieces) :]),
+            out_shape=VMEM((requests, STATE, unit), BF16),
+            in_specs=[smem_spec] * 4 + [hbm_spec] + [vmem_spec] * (len(pieces) + 1),
+            out_specs=vmem_spec,
+            scratch_shapes=[VMEM((requests, unit, STATE), F32), pltpu.SemaphoreType.DMA((requests,))],
+            compiler_params=pltpu.CompilerParams(vmem_limit_bytes=12 << 20),
+            cost_estimate=takes(0.5),
+            name="parents",
+        )(info, parent, state_dev, state_slot, cache_rows, *pieces, pin(previous))
+        decays = call(
+            decay_body,
+            ((4, requests, 1, width), F32),
+            (*all_dt, bias, rates),
+            scalars=(info,),
+            after=(initial,),
+            name="decays",
+            us=0.4,
+        )
+        started.extend((initial, decays))
+        send_down(0)
+        return decays
+
+    local = {}
+    previous = c_flat
+    merges_early = any(chain_lanes(order[h // parts], 0, unit) is not None for h in range(min(HOP, chunks)))
+    if merges_early:
+        previous = start_parents(previous)
     for h in range(HOP):
         send_up(h)
-    send_down(0)
-    local = {0: local_sums(0, (previous,))}
-    previous = local[0][0]
-    pending = list(range(1, groups))
+    if groups > 1:
+        previous = find_states(1, (previous,))
+    pending = list(range(groups))
     downs = list(range(1, toks))
     y_out, done, final = None, 0, None
     for h in range(HOP, slots):
         previous = send_up(h, (previous,))
-        if pending:
+        if downs and h >= round(HOP + (3 + 2 * (toks - 1 - len(downs))) * parts / 2):
+            previous = send_down(downs.pop(0), (previous,))
+        if h == HOP:
+            if not started:
+                previous = start_parents(previous)
+            for i in range(2, groups):
+                previous = find_states(i, (previous,))
+        elif pending:
             i = pending.pop(0)
             local[i] = local_sums(i, (previous,))
             previous = local[i][0]
         elif done < groups - 1 and done * parts + lag + 1 <= h:
             y_out, previous = finish(done, list(range(parts)), y_out, (previous,))
             done += 1
-        if downs and h >= round(HOP + (1 + 2.5 * (toks - 1 - len(downs))) * parts / 2):
-            previous = send_down(downs.pop(0), (previous,))
     for s in downs:
         previous = send_down(s, (previous,))
     while pending:

time: 147 us -> 143 us (0.973)
  waiting for transfers between devices: 49.8 us -> 37.6 us
  starting transfers between devices: 42.9 us -> 50.1 us
  Pallas kernels: 46.6 us -> 51 us
  local copies, waits for them, and re-layouts: 3.8 us -> 0.02 us
    ppermute x12, waiting for transfers between devices: 38.4 us -> 19.5 us  [send_up(): received[h] = lax.ppermute(sent, 'tok', pairs)]
    ppermute x4, starting transfers between devices: 19.3 us -> 25.2 us  [send_down(): arrived.append(lax.ppermute(sent, 'tok', backward))]
    ppermute x4, waiting for transfers between devices: 8.61 us -> 14 us  [send_down(): arrived.append(lax.ppermute(sent, 'tok', backward))]
    pallas_call x2 -> x3, Pallas kernels: 7.57 us -> 11 us  [the longest x1 5.87 us: shards(): pl.pallas_call(functools.partial(front_body, order), out_shape=(jax.Shape...]
    reshape x2 -> x0, local copies, waits for them, and re-layouts: 2.48 us -> none  [the longest x1 1.24 us: shards(): b_flat = pin(b_in.reshape(requests, span, groups * STATE))]
  transfers between devices with their start and end apart: 20 -> 20, of which waited for: 12 -> 8; matrix products, arithmetic and copies ran while one was open for 3% -> 0% of each run, Pallas kernels for 31% -> 30%
where the time goes in v4:
time: 143 us; the launch traced here: 140 us
  Pallas kernels  51 us (36%)
  starting transfers between devices  50.1 us (35%)
  waiting for transfers between devices  37.6 us (26%)
    ppermute x4, starting transfers between devices, send_down(): arrived.append(lax.ppermute(sent, 'tok', backward))  25.2 us
    ppermute x12, waiting for transfers between devices, send_up(): received[h] = lax.ppermute(sent, 'tok', pairs)  19.5 us
    ppermute x12, starting transfers between devices, send_up(): received[h] = lax.ppermute(sent, 'tok', pairs)  18.1 us
    pallas_call x17, Pallas kernels, call(): pl.pallas_call(kernel, out_shape=tuple((VMEM(shape, dtype) for shape, dty...  17.3 us
    ppermute x4, waiting for transfers between devices, send_down(): arrived.append(lax.ppermute(sent, 'tok', backward))  14 us
    pallas_call x5, Pallas kernels, finish(): pl.pallas_call(kernel, out_shape=(jax.ShapeDtypeStruct((requests, span, w...  12.9 us
    pallas_call x4, Pallas kernels, local_sums(): pl.pallas_call(lambda *refs: local_body(order[i], *refs[:1 + n_ins], refs...  7.11 us
    pallas_call x1, Pallas kernels, shards(): pl.pallas_call(functools.partial(front_body, order), out_shape=(jax.Shape...  5.87 us
  transfers between devices with their start and end apart: 20, of which 8 were waited for; matrix products, arithmetic and copies ran while one was open for 0% of the time, Pallas kernels for 30%

profile of v4, /device:TPU:16, one launch (start us, length us, event | category | flops | bytes accessed | tf_op | source)
XLA Modules:
  0.0 140.1 jit_solution(2946049086557658784)
XLA Ops:
  0.7 5.9 %front.1 = (s32[11]{0:T(128)S(1)}, f32[4,4,128,16]{3,2,1,0:T(8,128)S(1)}, f32[4,4,16,128]{3,2,1,0:T(8,128)S(1)}, f32[4,4,16,128]{3,2,1,0:T(8,128)S(1)}, f32[4,4,...) custom-call(s32[3]{0:T(128)S(1)} %pad_add_fusion.ids, ...), custom_call_target="tpu_custom_call" | custom-call | flops 20000000000 | bytes 70000000 | tf_op jit(solution)/shard_map/front/pallas_call | solution.py:290
  7.3 2.9 %loads.1 = (bf16[2,1024,128]{2,1,0:T(8,128)(2,1)S(1)}, bf16[4,128,512]{2,1,0:T(8,128)(2,1)S(1)}, bf16[4,128,1024]{2,1,0:T(8,128)(2,1)S(1)}, bf16[4,128,1024]{2,1,0:T(8,128)(2,1)S(1)}, bf16[4,128,1024]{2,1,0:T(8,128)(2,1)S(1)}) custom-call(s32[11]{0:T(128)S(1)} %get-tuple-element.47.info_ref.refs_0_.ids_ref, f32[2,2,1024,128]{3,2,1,0:T(8,128)} %bitcast.10, ...), custom_call_target="tpu_custom_call" | custom-call | flops 12000000000 | bytes 42000000 | tf_op jit(solution)/shard_map/loads/pallas_call | solution.py:339
  10.2 1.6 %collective-permute-start.3 = (bf16[2,1024,128]{2,1,0:T(8,128)(2,1)S(1)}, bf16[2,1024,128]{2,1,0:T(8,128)(2,1)S(1)}, u32[]{:S(2)}, u32[]{:S(2)}) collective-permute-start(bf16[2,1024,128]{2,1,0:T(8,128)(2,1)S(1)} %get-tuple-element.61), channel_id=1, source_target_pairs={{0,2},{2,0},{1,3},{3,1},{4,6},{6,4},{5,7},{7,5},{8,10},{10,8},{9,1... | collective-permute-start | bytes 1572872 | tf_op jit(solution)/shard_map/ppermute | solution.py:355
  11.8 1.0 collective-permute-start.2
  12.8 2.9 %collective-permute-start.1 = (bf16[4,64,128]{2,1,0:T(8,128)(2,1)S(1)}, bf16[4,64,128]{2,1,0:T(8,128)(2,1)S(1)}, u32[]{:S(2)}, u32[]{:S(2)}) collective-permute-start(bf16[4,64,128]{2,1,0:T(8,128)(2,1)S(1)} %get-tuple-element.58.refs_1_), channel_id=1, source_target_pairs={{0,8},{4,12},{8,0},{12,4},{1,9},{5,13},{9,1},{13,5},{2,10},{6,14},... | collective-permute-start | bytes 196616 | tf_op jit(solution)/shard_map/ppermute | solution.py:352
  15.7 1.2 collective-permute-start
  17.0 1.6 %block_states.3 = (bf16[2,128,1024]{2,1,0:T(8,128)(2,1)S(1)}, bf16[2,128,1024]{2,1,0:T(8,128)(2,1)S(1)}) custom-call(bf16[4,128,1024]{2,1,0:T(8,128)(2,1)S(1)} %get-tuple-element.62.refs_0_.refs_1_, bf16[4,128,512]{2,1,0:T(8,128)(2,1)S(1)} %get-tuple-element.50.refs_1_.refs_2_, f32[4,4,128,16]{3,2,1,0:T(8,128)S(1)} %get-tuple-element.56.refs_2_, ...), custom_call_target="tpu_custom_call" | custom-call | flops 1600000000 | bytes 5600000 | tf_op jit(solution)/shard_map/block_states/pallas_call | solution.py:54
  19.9 4.1 %collective-permute-done.3.refs_5_ = bf16[2,1024,128]{2,1,0:T(8,128)(2,1)S(1)} collective-permute-done((bf16[2,1024,128]{2,1,0:T(8,128)(2,1)S(1)}, bf16[2,1024,128]{2,1,0:T(8,128)(2,1)S(1)}, u32[]{:S(2)}, u32[]{:S(2)}) %collective-permute-start.3) | collective-permute-done | bytes 524320 | tf_op jit(solution)/shard_map/ppermute | solution.py:355
  24.0 1.3 collective-permute-start.5
  25.3 2.2 %parents.1.refs_7_.refs_13_.refs_6_.refs_10_.refs_1_ = bf16[4,128,1024]{2,1,0:T(8,128)(2,1)S(1)} custom-call(s32[11]{0:T(128)S(1)} %get-tuple-element.47.info_ref.refs_0_.ids_ref, s32[8]{0:T(128)S(1)} %copy-done, s32[4]{0:T(128)S(1)} %copy-done.1, s32[4]{0:T(128)S(1)} %copy-done.2, f32[2,2,1024,128]{3,2,1,0:T(8,128)} %bitcast.11, ...), custom_call_target="tpu_custom_call" | custom-call | flops 2000000000 | bytes 7000000 | tf_op jit(solution)/shard_map/parents/pallas_call | solution.py:640
  27.5 4.6 %collective-permute-start.8 = (bf16[4,128,1024]{2,1,0:T(8,128)(2,1)S(1)}, bf16[4,128,1024]{2,1,0:T(8,128)(2,1)S(1)}, u32[]{:S(2)}, u32[]{:S(2)}) collective-permute-start(bf16[4,128,1024]{2,1,0:T(8,128)(2,1)S(1)} %parents.1.refs_7_.refs_13_.refs_6_.refs_10_.refs_1_), channel_id=1, source_target_pairs={{4,0},{8,4},{12,8},{5,1},{9,5},{13,9},{6,2},{10,6},{14,10},{7,3},{... | collective-permute-start | bytes 3145736 | tf_op jit(solution)/shard_map/ppermute | solution.py:461
  32.1 1.8 %decays.1.refs_3_.refs_6_.refs_1_.refs_5_.refs_0_ = f32[4,4,1,4096]{3,2,1,0:T(1,128)S(1)} custom-call(s32[11]{0:T(128)S(1)} %get-tuple-element.47.info_ref.refs_0_.ids_ref, bf16[4,64,128]{2,1,0:T(8,128)(2,1)S(1)} %get-tuple-element.58.refs_1_, bf16[4,64,128]{2,1,0:T(8,128)(2,1)S(1)} %collective-permute-done.refs_2_, ...), custom_call_target="tpu_custom_call" | custom-call | flops 1600000000 | bytes 5600000 | tf_op jit(solution)/shard_map/decays/pallas_call | solution.py:54
  33.8 1.6 %block_states.4 = (bf16[2,128,1024]{2,1,0:T(8,128)(2,1)S(1)}, bf16[2,128,1024]{2,1,0:T(8,128)(2,1)S(1)}) custom-call(bf16[4,128,1024]{2,1,0:T(8,128)(2,1)S(1)} %get-tuple-element.57.refs_0_.refs_1_, bf16[4,128,512]{2,1,0:T(8,128)(2,1)S(1)} %get-tuple-element.50.refs_1_.refs_2_, f32[4,4,128,16]{3,2,1,0:T(8,128)S(1)} %get-tuple-element.56.refs_2_, ...), custom_call_target="tpu_custom_call" | custom-call | flops 1600000000 | bytes 5600000 | tf_op jit(solution)/shard_map/block_states/pallas_call | solution.py:54
  35.5 1.6 %block_states.5 = (bf16[2,128,1024]{2,1,0:T(8,128)(2,1)S(1)}, bf16[2,128,1024]{2,1,0:T(8,128)(2,1)S(1)}) custom-call(bf16[4,128,1024]{2,1,0:T(8,128)(2,1)S(1)} %get-tuple-element.49.refs_0_.refs_1_, bf16[4,128,512]{2,1,0:T(8,128)(2,1)S(1)} %get-tuple-element.50.refs_1_.refs_2_, f32[4,4,128,16]{3,2,1,0:T(8,128)S(1)} %get-tuple-element.56.refs_2_, ...), custom_call_target="tpu_custom_call" | custom-call | flops 1600000000 | bytes 5600000 | tf_op jit(solution)/shard_map/block_states/pallas_call | solution.py:54
  37.7 1.3 collective-permute-start.9
  39.0 1.8 %local_sums.4 = (f32[4,128,1024]{2,1,0:T(8,128)S(1)}, bf16[4,128,1024]{2,1,0:T(8,128)(2,1)S(1)}) custom-call(s32[11]{0:T(128)S(1)} %get-tuple-element.47.info_ref.refs_0_.ids_ref, bf16[4,128,1024]{2,1,0:T(8,128)(2,1)S(1)} %get-tuple-element.70.refs_1_, bf16[4,128,512]{2,1,0:T(8,128)(2,1)S(1)} %get-tuple-element.50.refs_1_.refs_2_, ...), custom_call_target="tpu_custom_call" | custom-call | flops 12000000000 | bytes 42000000 | tf_op jit(solution)/shard_map/local_sums/pallas_call | solution.py:467
  40.8 1.2 pass_on.12.refs_9_
  41.9 1.9 %collective-permute-start.7 = (bf16[2,128,1024]{2,1,0:T(8,128)(2,1)S(1)}, bf16[2,128,1024]{2,1,0:T(8,128)(2,1)S(1)}, u32[]{:S(2)}, u32[]{:S(2)}) collective-permute-start(bf16[2,128,1024]{2,1,0:T(8,128)(2,1)S(1)} %pass_on.12.refs_9_), channel_id=1, source_target_pairs={{0,4},{4,8},{8,12},{1,5},{5,9},{9,13},{2,6},{6,10},{10,14},{3,7},{... | collective-permute-start | bytes 1572872 | tf_op jit(solution)/shard_map/ppermute | solution.py:417
  43.8 1.8 %local_sums.5 = (f32[4,128,1024]{2,1,0:T(8,128)S(1)}, bf16[4,128,1024]{2,1,0:T(8,128)(2,1)S(1)}) custom-call(s32[11]{0:T(128)S(1)} %get-tuple-element.47.info_ref.refs_0_.ids_ref, bf16[4,128,1024]{2,1,0:T(8,128)(2,1)S(1)} %get-tuple-element.62.refs_0_.refs_1_, bf16[4,128,512]{2,1,0:T(8,128)(2,1)S(1)} %get-tuple-element.50.refs_1_.refs_2_, ...), custom_call_target="tpu_custom_call" | custom-call | flops 12000000000 | bytes 42000000 | tf_op jit(solution)/shard_map/local_sums/pallas_call | solution.py:467
  45.6 7.0 %collective-permute-done.9.refs_4_.refs_11_.refs_10_.refs_6_ = bf16[2,128,1024]{2,1,0:T(8,128)(2,1)S(1)} collective-permute-done((bf16[2,128,1024]{2,1,0:T(8,128)(2,1)S(1)}, bf16[2,128,1024]{2,1,0:T(8,128)(2,1)S(1)}, u32[]{:S(2)}, u32[]{:S(2)}) %collective-permute-start.9) | collective-permute-done | bytes 524320 | tf_op jit(solution)/shard_map/ppermute | solution.py:417
  52.6 1.0 pass_on.13.refs_5_
  53.6 1.9 %collective-permute-start.10 = (bf16[2,128,1024]{2,1,0:T(8,128)(2,1)S(1)}, bf16[2,128,1024]{2,1,0:T(8,128)(2,1)S(1)}, u32[]{:S(2)}, u32[]{:S(2)}) collective-permute-start(bf16[2,128,1024]{2,1,0:T(8,128)(2,1)S(1)} %pass_on.13.refs_5_), channel_id=1, source_target_pairs={{0,4},{4,8},{8,12},{1,5},{5,9},{9,13},{2,6},{6,10},{10,14},{3,7},{... | collective-permute-start | bytes 1572872 | tf_op jit(solution)/shard_map/ppermute | solution.py:417
  56.1 12.1 %collective-permute-start.13 = (bf16[4,128,1024]{2,1,0:T(8,128)(2,1)S(1)}, bf16[4,128,1024]{2,1,0:T(8,128)(2,1)S(1)}, u32[]{:S(2)}, u32[]{:S(2)}) collective-permute-start(bf16[4,128,1024]{2,1,0:T(8,128)(2,1)S(1)} %pass_down.3.refs_9_), channel_id=1, source_target_pairs={{4,0},{8,4},{12,8},{5,1},{9,5},{13,9},{6,2},{10,6},{14,10},{7,3},{... | collective-permute-start | bytes 3145736 | tf_op jit(solution)/shard_map/ppermute | solution.py:461
  68.3 1.8 %local_sums.6 = (f32[4,128,1024]{2,1,0:T(8,128)S(1)}, bf16[4,128,1024]{2,1,0:T(8,128)(2,1)S(1)}) custom-call(s32[11]{0:T(128)S(1)} %get-tuple-element.47.info_ref.refs_0_.ids_ref, bf16[4,128,1024]{2,1,0:T(8,128)(2,1)S(1)} %get-tuple-element.57.refs_0_.refs_1_, bf16[4,128,512]{2,1,0:T(8,128)(2,1)S(1)} %get-tuple-element.50.refs_1_.refs_2_, ...), custom_call_target="tpu_custom_call" | custom-call | flops 12000000000 | bytes 42000000 | tf_op jit(solution)/shard_map/local_sums/pallas_call | solution.py:467
  70.9 1.8 %local_sums.7 = (f32[4,128,1024]{2,1,0:T(8,128)S(1)}, bf16[4,128,1024]{2,1,0:T(8,128)(2,1)S(1)}) custom-call(s32[11]{0:T(128)S(1)} %get-tuple-element.47.info_ref.refs_0_.ids_ref, bf16[4,128,1024]{2,1,0:T(8,128)(2,1)S(1)} %get-tuple-element.49.refs_0_.refs_1_, bf16[4,128,512]{2,1,0:T(8,128)(2,1)S(1)} %get-tuple-element.50.refs_1_.refs_2_, ...), custom_call_target="tpu_custom_call" | custom-call | flops 12000000000 | bytes 42000000 | tf_op jit(solution)/shard_map/local_sums/pallas_call | solution.py:467
  72.7 1.9 %collective-permute-start.12 = (bf16[2,128,1024]{2,1,0:T(8,128)(2,1)S(1)}, bf16[2,128,1024]{2,1,0:T(8,128)(2,1)S(1)}, u32[]{:S(2)}, u32[]{:S(2)}) collective-permute-start(bf16[2,128,1024]{2,1,0:T(8,128)(2,1)S(1)} %pass_on.14.refs_9_), channel_id=1, source_target_pairs={{0,4},{4,8},{8,12},{1,5},{5,9},{9,13},{2,6},{6,10},{10,14},{3,7},{... | collective-permute-start | bytes 1572872 | tf_op jit(solution)/shard_map/ppermute | solution.py:417
  75.5 1.9 %collective-permute-start.11 = (bf16[2,128,1024]{2,1,0:T(8,128)(2,1)S(1)}, bf16[2,128,1024]{2,1,0:T(8,128)(2,1)S(1)}, u32[]{:S(2)}, u32[]{:S(2)}) collective-permute-start(bf16[2,128,1024]{2,1,0:T(8,128)(2,1)S(1)} %pass_on.15.refs_7_), channel_id=1, source_target_pairs={{0,4},{4,8},{8,12},{1,5},{5,9},{9,13},{2,6},{6,10},{10,14},{3,7},{... | collective-permute-start | bytes 1572872 | tf_op jit(solution)/shard_map/ppermute | solution.py:417
  77.4 8.7 %collective-permute-done.13.refs_2_.refs_15_ = bf16[4,128,1024]{2,1,0:T(8,128)(2,1)S(1)} collective-permute-done((bf16[4,128,1024]{2,1,0:T(8,128)(2,1)S(1)}, bf16[4,128,1024]{2,1,0:T(8,128)(2,1)S(1)}, u32[]{:S(2)}, u32[]{:S(2)}) %collective-permute-start.13) | collective-permute-done | bytes 1048608 | tf_op jit(solution)/shard_map/ppermute | solution.py:461
  86.1 0.9 pass_down.4.refs_16_
  87.0 4.1 %collective-permute-start.16 = (bf16[4,128,1024]{2,1,0:T(8,128)(2,1)S(1)}, bf16[4,128,1024]{2,1,0:T(8,128)(2,1)S(1)}, u32[]{:S(2)}, u32[]{:S(2)}) collective-permute-start(bf16[4,128,1024]{2,1,0:T(8,128)(2,1)S(1)} %pass_down.4.refs_16_), channel_id=1, source_target_pairs={{4,0},{8,4},{12,8},{5,1},{9,5},{13,9},{6,2},{10,6},{14,10},{7,3},{... | collective-permute-start | bytes 3145736 | tf_op jit(solution)/shard_map/ppermute | solution.py:461
  91.1 2.9 %finish.5 = (bf16[4,128,4096]{2,1,0:T(8,128)(2,1)}, f32[8,128]{1,0:T(8,128)S(1)}) custom-call(s32[11]{0:T(128)S(1)} %get-tuple-element.47.info_ref.refs_0_.ids_ref, f32[4,128,1024]{2,1,0:T(8,128)S(1)} %get-tuple-element.72.refs_8_.refs_1_, bf16[4,128,1024]{2,1,0:T(8,128)(2,1)S(1)} %get-tuple-element.78.refs_2_, ...), custom_call_target="tpu_custom_call" | custom-call | flops 16000000000 | bytes 56000000 | tf_op jit(solution)/shard_map/finish/pallas_call | solution.py:565
  94.8 1.9 %collective-permute-start.15 = (bf16[2,128,1024]{2,1,0:T(8,128)(2,1)S(1)}, bf16[2,128,1024]{2,1,0:T(8,128)(2,1)S(1)}, u32[]{:S(2)}, u32[]{:S(2)}) collective-permute-start(bf16[2,128,1024]{2,1,0:T(8,128)(2,1)S(1)} %pass_on.16.refs_7_), channel_id=1, source_target_pairs={{4,8},{8,12},{5,9},{9,13},{6,10},{10,14},{7,11},{11,15},{20,24},{2... | collective-permute-start | bytes 1572872 | tf_op jit(solution)/shard_map/ppermute | solution.py:417
  96.7 3.9 %collective-permute-done.11.refs_3_.refs_12_.refs_11_.refs_4_.refs_8_.refs_7_ = bf16[2,128,1024]{2,1,0:T(8,128)(2,1)S(1)} collective-permute-done((bf16[2,128,1024]{2,1,0:T(8,128)(2,1)S(1)}, bf16[2,128,1024]{2,1,0:T(8,128)(2,1)S(1)}, u32[]{:S(2)}, u32[]{:S(2)}) %collective-permute-start.11) | collective-permute-done | bytes 524320 | tf_op jit(solution)/shard_map/ppermute | solution.py:417
  101.4 1.9 %collective-permute-start.14 = (bf16[2,128,1024]{2,1,0:T(8,128)(2,1)S(1)}, bf16[2,128,1024]{2,1,0:T(8,128)(2,1)S(1)}, u32[]{:S(2)}, u32[]{:S(2)}) collective-permute-start(bf16[2,128,1024]{2,1,0:T(8,128)(2,1)S(1)} %pass_on.17.refs_9_), channel_id=1, source_target_pairs={{4,8},{8,12},{5,9},{9,13},{6,10},{10,14},{7,11},{11,15},{20,24},{2... | collective-permute-start | bytes 1572872 | tf_op jit(solution)/shard_map/ppermute | solution.py:417
  103.4 5.3 %collective-permute-done.16.refs_2_.refs_16_ = bf16[4,128,1024]{2,1,0:T(8,128)(2,1)S(1)} collective-permute-done((bf16[4,128,1024]{2,1,0:T(8,128)(2,1)S(1)}, bf16[4,128,1024]{2,1,0:T(8,128)(2,1)S(1)}, u32[]{:S(2)}, u32[]{:S(2)}) %collective-permute-start.16) | collective-permute-done | bytes 1048608 | tf_op jit(solution)/shard_map/ppermute | solution.py:461
  108.7 0.9 pass_down.5.refs_17_
  109.5 4.4 %collective-permute-start.18 = (bf16[4,128,1024]{2,1,0:T(8,128)(2,1)S(1)}, bf16[4,128,1024]{2,1,0:T(8,128)(2,1)S(1)}, u32[]{:S(2)}, u32[]{:S(2)}) collective-permute-start(bf16[4,128,1024]{2,1,0:T(8,128)(2,1)S(1)} %pass_down.5.refs_17_), channel_id=1, source_target_pairs={{4,0},{8,4},{12,8},{5,1},{9,5},{13,9},{6,2},{10,6},{14,10},{7,3},{... | collective-permute-start | bytes 3145736 | tf_op jit(solution)/shard_map/ppermute | solution.py:461
  114.0 2.9 %finish.6 = (bf16[4,128,4096]{2,1,0:T(8,128)(2,1)}, f32[8,128]{1,0:T(8,128)S(1)}) custom-call(s32[11]{0:T(128)S(1)} %get-tuple-element.47.info_ref.refs_0_.ids_ref, f32[4,128,1024]{2,1,0:T(8,128)S(1)} %get-tuple-element.73.refs_8_.refs_1_, bf16[4,128,1024]{2,1,0:T(8,128)(2,1)S(1)} %get-tuple-element.80.refs_2_, ...), custom_call_target="tpu_custom_call", output_to_operand_aliasing={{0}: (18, {})} | custom-call | flops 16000000000 | bytes 56000000 | tf_op jit(solution)/shard_map/finish/pallas_call | solution.py:565
  116.9 1.0 pass_on.18.refs_4_
  117.9 1.3 collective-permute-start.19
  119.2 1.1 collective-permute-done.14.refs_2_.refs_12_.refs_8_
  121.1 1.3 collective-permute-start.17
  122.5 2.6 %finish.7 = (bf16[4,128,4096]{2,1,0:T(8,128)(2,1)}, f32[8,128]{1,0:T(8,128)S(1)}) custom-call(s32[11]{0:T(128)S(1)} %get-tuple-element.47.info_ref.refs_0_.ids_ref, f32[4,128,1024]{2,1,0:T(8,128)S(1)} %get-tuple-element.74.refs_6_.refs_1_, bf16[4,128,1024]{2,1,0:T(8,128)(2,1)S(1)} %get-tuple-element.83.refs_2_, ...), custom_call_target="tpu_custom_call", output_to_operand_aliasing={{0}: (15, {})} | custom-call | flops 16000000000 | bytes 56000000 | tf_op jit(solution)/shard_map/finish/pallas_call | solution.py:565
  125.1 6.5 %collective-permute-done.19.refs_9_ = bf16[2,128,1024]{2,1,0:T(8,128)(2,1)S(1)} collective-permute-done((bf16[2,128,1024]{2,1,0:T(8,128)(2,1)S(1)}, bf16[2,128,1024]{2,1,0:T(8,128)(2,1)S(1)}, u32[]{:S(2)}, u32[]{:S(2)}) %collective-permute-start.19) | collective-permute-done | bytes 524320 | tf_op jit(solution)/shard_map/ppermute | solution.py:417
  131.6 2.0 %finish.8 = (bf16[4,128,4096]{2,1,0:T(8,128)(2,1)}, f32[8,128]{1,0:T(8,128)S(1)}) custom-call(s32[11]{0:T(128)S(1)} %get-tuple-element.47.info_ref.refs_0_.ids_ref, f32[4,128,1024]{2,1,0:T(8,128)S(1)} %get-tuple-element.75.refs_6_.refs_1_, bf16[4,128,1024]{2,1,0:T(8,128)(2,1)S(1)} %get-tuple-element.76.refs_2_, ...), custom_call_target="tpu_custom_call", output_to_operand_aliasing={{0}: (13, {})} | custom-call | flops 16000000000 | bytes 56000000 | tf_op jit(solution)/shard_map/finish/pallas_call | solution.py:565
  133.5 2.7 %final_states.1 = (f32[4,1024,128]{2,1,0:T(8,128)}, f32[8,128]{1,0:T(8,128)S(1)}) custom-call(s32[11]{0:T(128)S(1)} %get-tuple-element.47.info_ref.refs_0_.ids_ref, f32[4,4,1,4096]{3,2,1,0:T(1,128)S(1)} %decays.1.refs_3_.refs_6_.refs_1_.refs_5_.refs_0_, bf16[4,128,1024]{2,1,0:T(8,128)(2,1)S(1)} %parents.1.refs_7_.refs_13_.refs_6_.refs_10_.refs_1_, ...), custom_call_target="tpu_custom_call" | custom-call | flops 10800000000 | bytes 37800000 | tf_op jit(solution)/shard_map/final_states/pallas_call | solution.py:623
  136.2 1.1 collective-permute-done.17.refs_9_
  137.3 2.5 %finish.9 = (bf16[4,128,4096]{2,1,0:T(8,128)(2,1)}, f32[8,128]{1,0:T(8,128)}) custom-call(s32[11]{0:T(128)S(1)} %get-tuple-element.47.info_ref.refs_0_.ids_ref, f32[4,128,1024]{2,1,0:T(8,128)S(1)} %get-tuple-element.75.refs_6_.refs_1_, bf16[4,128,1024]{2,1,0:T(8,128)(2,1)S(1)} %get-tuple-element.76.refs_2_, ...), custom_call_target="tpu_custom_call", output_to_operand_aliasing={{0}: (13, {})} | custom-call | flops 16000000000 | bytes 56000000 | tf_op jit(solution)/shard_map/finish/pallas_call | solution.py:565
  (29 shorter events, 7.3 us)
Async XLA Ops:
  6.6 12.0 %collective-permute-start.4 = (bf16[2,128,1024]{2,1,0:T(8,128)(2,1)S(1)}, bf16[2,128,1024]{2,1,0:T(8,128)(2,1)S(1)}, u32[]{:S(2)}, u32[]{:S(2)}) collective-permute-start(bf16[2,128,1024]{2,1,0:T(8,128)(2,1)S(1)} %get-tuple-element.64.refs_2_.refs_3_.refs_9_), channel_id=1, source_target_pairs={{0,4},{1,5},{2,6},{3,7},{16,20},{17,21},{18,22},{19,23}} | collective-permute-start | bytes 1572872 | tf_op jit(solution)/shard_map/ppermute | solution.py:417
  10.2 13.7 %collective-permute-start.3 = (bf16[2,1024,128]{2,1,0:T(8,128)(2,1)S(1)}, bf16[2,1024,128]{2,1,0:T(8,128)(2,1)S(1)}, u32[]{:S(2)}, u32[]{:S(2)}) collective-permute-start(bf16[2,1024,128]{2,1,0:T(8,128)(2,1)S(1)} %get-tuple-element.61), channel_id=1, source_target_pairs={{0,2},{2,0},{1,3},{3,1},{4,6},{6,4},{5,7},{7,5},{8,10},{10,8},{9,1... | collective-permute-start | bytes 1572872 | tf_op jit(solution)/shard_map/ppermute | solution.py:355
  11.8 15.7 %collective-permute-start.2 = (bf16[4,64,128]{2,1,0:T(8,128)(2,1)S(1)}, bf16[4,64,128]{2,1,0:T(8,128)(2,1)S(1)}, u32[]{:S(2)}, u32[]{:S(2)}) collective-permute-start(bf16[4,64,128]{2,1,0:T(8,128)(2,1)S(1)} %get-tuple-element.58.refs_1_), channel_id=1, source_target_pairs={{0,12},{4,0},{8,4},{12,8},{1,13},{5,1},{9,5},{13,9},{2,14},{6,2},{... | collective-permute-start | bytes 196616 | tf_op jit(solution)/shard_map/ppermute | solution.py:352
  12.8 19.2 %collective-permute-start.1 = (bf16[4,64,128]{2,1,0:T(8,128)(2,1)S(1)}, bf16[4,64,128]{2,1,0:T(8,128)(2,1)S(1)}, u32[]{:S(2)}, u32[]{:S(2)}) collective-permute-start(bf16[4,64,128]{2,1,0:T(8,128)(2,1)S(1)} %get-tuple-element.58.refs_1_), channel_id=1, source_target_pairs={{0,8},{4,12},{8,0},{12,4},{1,9},{5,13},{9,1},{13,5},{2,10},{6,14},... | collective-permute-start | bytes 196616 | tf_op jit(solution)/shard_map/ppermute | solution.py:352
  15.7 16.3 %collective-permute-start = (bf16[4,64,128]{2,1,0:T(8,128)(2,1)S(1)}, bf16[4,64,128]{2,1,0:T(8,128)(2,1)S(1)}, u32[]{:S(2)}, u32[]{:S(2)}) collective-permute-start(bf16[4,64,128]{2,1,0:T(8,128)(2,1)S(1)} %get-tuple-element.58.refs_1_), channel_id=1, source_target_pairs={{0,4},{4,8},{8,12},{12,0},{1,5},{5,9},{9,13},{13,1},{2,6},{6,10},{... | collective-permute-start | bytes 196616 | tf_op jit(solution)/shard_map/ppermute | solution.py:352
  18.6 18.5 %collective-permute-start.6 = (bf16[2,128,1024]{2,1,0:T(8,128)(2,1)S(1)}, bf16[2,128,1024]{2,1,0:T(8,128)(2,1)S(1)}, u32[]{:S(2)}, u32[]{:S(2)}) collective-permute-start(bf16[2,128,1024]{2,1,0:T(8,128)(2,1)S(1)} %get-tuple-element.48._.refs_2_.refs_3_.refs_4_.refs_10_), channel_id=1, source_target_pairs={{0,4},{1,5},{2,6},{3,7},{16,20},{17,21},{18,22},{19,23}} | collective-permute-start | bytes 1572872 | tf_op jit(solution)/shard_map/ppermute | solution.py:417
  19.3 5.9 %copy-start = (s32[8]{0:T(128)S(1)}, s32[8]{0:T(128)}, u32[]{:S(2)}) copy-start(s32[8]{0:T(128)} %refs_1_.1) | copy-start | bytes 100
  19.3 5.9 %copy-start.1 = (s32[4]{0:T(128)S(1)}, s32[4]{0:T(128)}, u32[]{:S(2)}) copy-start(s32[4]{0:T(128)} %refs_2_.1) | copy-start | bytes 52
  19.3 5.9 %copy-start.2 = (s32[4]{0:T(128)S(1)}, s32[4]{0:T(128)}, u32[]{:S(2)}) copy-start(s32[4]{0:T(128)} %refs_3_.1) | copy-start | bytes 52
  24.0 16.8 %collective-permute-start.5 = (bf16[2,128,1024]{2,1,0:T(8,128)(2,1)S(1)}, bf16[2,128,1024]{2,1,0:T(8,128)(2,1)S(1)}, u32[]{:S(2)}, u32[]{:S(2)}) collective-permute-start(bf16[2,128,1024]{2,1,0:T(8,128)(2,1)S(1)} %pass_on.10.refs_6_), channel_id=1, source_target_pairs={{0,4},{4,8},{1,5},{5,9},{2,6},{6,10},{3,7},{7,11},{16,20},{20,24},... | collective-permute-start | bytes 1572872 | tf_op jit(solution)/shard_map/ppermute | solution.py:417
  27.5 28.0 %collective-permute-start.8 = (bf16[4,128,1024]{2,1,0:T(8,128)(2,1)S(1)}, bf16[4,128,1024]{2,1,0:T(8,128)(2,1)S(1)}, u32[]{:S(2)}, u32[]{:S(2)}) collective-permute-start(bf16[4,128,1024]{2,1,0:T(8,128)(2,1)S(1)} %parents.1.refs_7_.refs_13_.refs_6_.refs_10_.refs_1_), channel_id=1, source_target_pairs={{4,0},{8,4},{12,8},{5,1},{9,5},{13,9},{6,2},{10,6},{14,10},{7,3},{... | collective-permute-start | bytes 3145736 | tf_op jit(solution)/shard_map/ppermute | solution.py:461
  37.7 14.9 %collective-permute-start.9 = (bf16[2,128,1024]{2,1,0:T(8,128)(2,1)S(1)}, bf16[2,128,1024]{2,1,0:T(8,128)(2,1)S(1)}, u32[]{:S(2)}, u32[]{:S(2)}) collective-permute-start(bf16[2,128,1024]{2,1,0:T(8,128)(2,1)S(1)} %pass_on.11.refs_9_), channel_id=1, source_target_pairs={{0,4},{4,8},{1,5},{5,9},{2,6},{6,10},{3,7},{7,11},{16,20},{20,24},... | collective-permute-start | bytes 1572872 | tf_op jit(solution)/shard_map/ppermute | solution.py:417
  41.9 28.1 %collective-permute-start.7 = (bf16[2,128,1024]{2,1,0:T(8,128)(2,1)S(1)}, bf16[2,128,1024]{2,1,0:T(8,128)(2,1)S(1)}, u32[]{:S(2)}, u32[]{:S(2)}) collective-permute-start(bf16[2,128,1024]{2,1,0:T(8,128)(2,1)S(1)} %pass_on.12.refs_9_), channel_id=1, source_target_pairs={{0,4},{4,8},{8,12},{1,5},{5,9},{9,13},{2,6},{6,10},{10,14},{3,7},{... | collective-permute-start | bytes 1572872 | tf_op jit(solution)/shard_map/ppermute | solution.py:417
  53.6 21.0 %collective-permute-start.10 = (bf16[2,128,1024]{2,1,0:T(8,128)(2,1)S(1)}, bf16[2,128,1024]{2,1,0:T(8,128)(2,1)S(1)}, u32[]{:S(2)}, u32[]{:S(2)}) collective-permute-start(bf16[2,128,1024]{2,1,0:T(8,128)(2,1)S(1)} %pass_on.13.refs_5_), channel_id=1, source_target_pairs={{0,4},{4,8},{8,12},{1,5},{5,9},{9,13},{2,6},{6,10},{10,14},{3,7},{... | collective-permute-start | bytes 1572872 | tf_op jit(solution)/shard_map/ppermute | solution.py:417
  56.1 29.9 %collective-permute-start.13 = (bf16[4,128,1024]{2,1,0:T(8,128)(2,1)S(1)}, bf16[4,128,1024]{2,1,0:T(8,128)(2,1)S(1)}, u32[]{:S(2)}, u32[]{:S(2)}) collective-permute-start(bf16[4,128,1024]{2,1,0:T(8,128)(2,1)S(1)} %pass_down.3.refs_9_), channel_id=1, source_target_pairs={{4,0},{8,4},{12,8},{5,1},{9,5},{13,9},{6,2},{10,6},{14,10},{7,3},{... | collective-permute-start | bytes 3145736 | tf_op jit(solution)/shard_map/ppermute | solution.py:461
  72.7 21.3 %collective-permute-start.12 = (bf16[2,128,1024]{2,1,0:T(8,128)(2,1)S(1)}, bf16[2,128,1024]{2,1,0:T(8,128)(2,1)S(1)}, u32[]{:S(2)}, u32[]{:S(2)}) collective-permute-start(bf16[2,128,1024]{2,1,0:T(8,128)(2,1)S(1)} %pass_on.14.refs_9_), channel_id=1, source_target_pairs={{0,4},{4,8},{8,12},{1,5},{5,9},{9,13},{2,6},{6,10},{10,14},{3,7},{... | collective-permute-start | bytes 1572872 | tf_op jit(solution)/shard_map/ppermute | solution.py:417
  75.5 25.2 %collective-permute-start.11 = (bf16[2,128,1024]{2,1,0:T(8,128)(2,1)S(1)}, bf16[2,128,1024]{2,1,0:T(8,128)(2,1)S(1)}, u32[]{:S(2)}, u32[]{:S(2)}) collective-permute-start(bf16[2,128,1024]{2,1,0:T(8,128)(2,1)S(1)} %pass_on.15.refs_7_), channel_id=1, source_target_pairs={{0,4},{4,8},{8,12},{1,5},{5,9},{9,13},{2,6},{6,10},{10,14},{3,7},{... | collective-permute-start | bytes 1572872 | tf_op jit(solution)/shard_map/ppermute | solution.py:417
  87.0 21.7 %collective-permute-start.16 = (bf16[4,128,1024]{2,1,0:T(8,128)(2,1)S(1)}, bf16[4,128,1024]{2,1,0:T(8,128)(2,1)S(1)}, u32[]{:S(2)}, u32[]{:S(2)}) collective-permute-start(bf16[4,128,1024]{2,1,0:T(8,128)(2,1)S(1)} %pass_down.4.refs_16_), channel_id=1, source_target_pairs={{4,0},{8,4},{12,8},{5,1},{9,5},{13,9},{6,2},{10,6},{14,10},{7,3},{... | collective-permute-start | bytes 3145736 | tf_op jit(solution)/shard_map/ppermute | solution.py:461
  94.8 22.1 %collective-permute-start.15 = (bf16[2,128,1024]{2,1,0:T(8,128)(2,1)S(1)}, bf16[2,128,1024]{2,1,0:T(8,128)(2,1)S(1)}, u32[]{:S(2)}, u32[]{:S(2)}) collective-permute-start(bf16[2,128,1024]{2,1,0:T(8,128)(2,1)S(1)} %pass_on.16.refs_7_), channel_id=1, source_target_pairs={{4,8},{8,12},{5,9},{9,13},{6,10},{10,14},{7,11},{11,15},{20,24},{2... | collective-permute-start | bytes 1572872 | tf_op jit(solution)/shard_map/ppermute | solution.py:417
  101.4 18.9 %collective-permute-start.14 = (bf16[2,128,1024]{2,1,0:T(8,128)(2,1)S(1)}, bf16[2,128,1024]{2,1,0:T(8,128)(2,1)S(1)}, u32[]{:S(2)}, u32[]{:S(2)}) collective-permute-start(bf16[2,128,1024]{2,1,0:T(8,128)(2,1)S(1)} %pass_on.17.refs_9_), channel_id=1, source_target_pairs={{4,8},{8,12},{5,9},{9,13},{6,10},{10,14},{7,11},{11,15},{20,24},{2... | collective-permute-start | bytes 1572872 | tf_op jit(solution)/shard_map/ppermute | solution.py:417
  109.5 24.0 %collective-permute-start.18 = (bf16[4,128,1024]{2,1,0:T(8,128)(2,1)S(1)}, bf16[4,128,1024]{2,1,0:T(8,128)(2,1)S(1)}, u32[]{:S(2)}, u32[]{:S(2)}) collective-permute-start(bf16[4,128,1024]{2,1,0:T(8,128)(2,1)S(1)} %pass_down.5.refs_17_), channel_id=1, source_target_pairs={{4,0},{8,4},{12,8},{5,1},{9,5},{13,9},{6,2},{10,6},{14,10},{7,3},{... | collective-permute-start | bytes 3145736 | tf_op jit(solution)/shard_map/ppermute | solution.py:461
  117.9 13.7 %collective-permute-start.19 = (bf16[2,128,1024]{2,1,0:T(8,128)(2,1)S(1)}, bf16[2,128,1024]{2,1,0:T(8,128)(2,1)S(1)}, u32[]{:S(2)}, u32[]{:S(2)}) collective-permute-start(bf16[2,128,1024]{2,1,0:T(8,128)(2,1)S(1)} %pass_on.18.refs_4_), channel_id=1, source_target_pairs={{8,12},{9,13},{10,14},{11,15},{24,28},{25,29},{26,30},{27,31}} | collective-permute-start | bytes 1572872 | tf_op jit(solution)/shard_map/ppermute | solution.py:417
  121.1 16.2 %collective-permute-start.17 = (bf16[2,128,1024]{2,1,0:T(8,128)(2,1)S(1)}, bf16[2,128,1024]{2,1,0:T(8,128)(2,1)S(1)}, u32[]{:S(2)}, u32[]{:S(2)}) collective-permute-start(bf16[2,128,1024]{2,1,0:T(8,128)(2,1)S(1)} %pass_on.19.refs_14_), channel_id=1, source_target_pairs={{8,12},{9,13},{10,14},{11,15},{24,28},{25,29},{26,30},{27,31}} | collective-permute-start | bytes 1572872 | tf_op jit(solution)/shard_map/ppermute | solution.py:417

commit v5 on v4

--- a/solution.py
+++ b/solution.py
@@ -471,7 +471,7 @@
             out_specs=(vmem_spec, vmem_spec),
             scratch_shapes=[pltpu.SemaphoreType.DMA],
             compiler_params=pltpu.CompilerParams(vmem_limit_bytes=12 << 20),
-            cost_estimate=takes(3.0),
+            cost_estimate=takes(1.0),
             name="local_sums",
         )(info, *(pin(a) for a in ins), in_hbm(z_in), *(pin(a) for a in after))
 
@@ -574,7 +574,7 @@
                 pltpu.SemaphoreType.DMA((count,)),
             ],
             compiler_params=pltpu.CompilerParams(vmem_limit_bytes=12 << 20),
-            cost_estimate=takes(4.0),
+            cost_estimate=takes(1.5),
             name="finish",
         )(info, *pinned, *([y_so_far] if had else []))
 

time: 143 us -> 142 us (level)
    ppermute x4, waiting for transfers between devices: 14 us -> 15.6 us  [send_down(): arrived.append(lax.ppermute(sent, 'tok', backward))]
where the time goes in v5:
time: 142 us; the launch traced here: 140 us
  Pallas kernels  50.7 us (36%)
  starting transfers between devices  50 us (35%)
  waiting for transfers between devices  38.2 us (27%)
    ppermute x4, starting transfers between devices, send_down(): arrived.append(lax.ppermute(sent, 'tok', backward))  25.1 us
    ppermute x12, waiting for transfers between devices, send_up(): received[h] = lax.ppermute(sent, 'tok', pairs)  18.5 us
    ppermute x12, starting transfers between devices, send_up(): received[h] = lax.ppermute(sent, 'tok', pairs)  18.1 us
    pallas_call x17, Pallas kernels, call(): pl.pallas_call(kernel, out_shape=tuple((VMEM(shape, dtype) for shape, dty...  17.3 us
    ppermute x4, waiting for transfers between devices, send_down(): arrived.append(lax.ppermute(sent, 'tok', backward))  15.6 us
    pallas_call x5, Pallas kernels, finish(): pl.pallas_call(kernel, out_shape=(jax.ShapeDtypeStruct((requests, span, w...  12.7 us
    pallas_call x4, Pallas kernels, local_sums(): pl.pallas_call(lambda *refs: local_body(order[i], *refs[:1 + n_ins], refs...  7.11 us
    pallas_call x1, Pallas kernels, shards(): pl.pallas_call(functools.partial(front_body, order), out_shape=(jax.Shape...  5.87 us
  transfers between devices with their start and end apart: 20, of which 8 were waited for; matrix products, arithmetic and copies ran while one was open for 0% of the time, Pallas kernels for 30%

profile of v5, /device:TPU:16, one launch (start us, length us, event | category | flops | bytes accessed | tf_op | source)
XLA Modules:
  0.0 140.3 jit_solution(16997152327156167225)
XLA Ops:
  0.7 5.9 %front.1 = (s32[11]{0:T(128)S(1)}, f32[4,4,128,16]{3,2,1,0:T(8,128)S(1)}, f32[4,4,16,128]{3,2,1,0:T(8,128)S(1)}, f32[4,4,16,128]{3,2,1,0:T(8,128)S(1)}, f32[4,4,...) custom-call(s32[3]{0:T(128)S(1)} %pad_add_fusion.ids, ...), custom_call_target="tpu_custom_call" | custom-call | flops 20000000000 | bytes 70000000 | tf_op jit(solution)/shard_map/front/pallas_call | solution.py:290
  7.3 2.9 %loads.1 = (bf16[2,1024,128]{2,1,0:T(8,128)(2,1)S(1)}, bf16[4,128,512]{2,1,0:T(8,128)(2,1)S(1)}, bf16[4,128,1024]{2,1,0:T(8,128)(2,1)S(1)}, bf16[4,128,1024]{2,1,0:T(8,128)(2,1)S(1)}, bf16[4,128,1024]{2,1,0:T(8,128)(2,1)S(1)}) custom-call(s32[11]{0:T(128)S(1)} %get-tuple-element.47.info_ref.refs_0_.ids_ref, f32[2,2,1024,128]{3,2,1,0:T(8,128)} %bitcast.10, ...), custom_call_target="tpu_custom_call" | custom-call | flops 12000000000 | bytes 42000000 | tf_op jit(solution)/shard_map/loads/pallas_call | solution.py:339
  10.2 1.6 %collective-permute-start.3 = (bf16[2,1024,128]{2,1,0:T(8,128)(2,1)S(1)}, bf16[2,1024,128]{2,1,0:T(8,128)(2,1)S(1)}, u32[]{:S(2)}, u32[]{:S(2)}) collective-permute-start(bf16[2,1024,128]{2,1,0:T(8,128)(2,1)S(1)} %get-tuple-element.61), channel_id=1, source_target_pairs={{0,2},{2,0},{1,3},{3,1},{4,6},{6,4},{5,7},{7,5},{8,10},{10,8},{9,1... | collective-permute-start | bytes 1572872 | tf_op jit(solution)/shard_map/ppermute | solution.py:355
  11.8 1.0 collective-permute-start.2
  12.8 2.9 %collective-permute-start.1 = (bf16[4,64,128]{2,1,0:T(8,128)(2,1)S(1)}, bf16[4,64,128]{2,1,0:T(8,128)(2,1)S(1)}, u32[]{:S(2)}, u32[]{:S(2)}) collective-permute-start(bf16[4,64,128]{2,1,0:T(8,128)(2,1)S(1)} %get-tuple-element.58.refs_1_), channel_id=1, source_target_pairs={{0,8},{4,12},{8,0},{12,4},{1,9},{5,13},{9,1},{13,5},{2,10},{6,14},... | collective-permute-start | bytes 196616 | tf_op jit(solution)/shard_map/ppermute | solution.py:352
  15.7 1.2 collective-permute-start
  17.0 1.6 %block_states.3 = (bf16[2,128,1024]{2,1,0:T(8,128)(2,1)S(1)}, bf16[2,128,1024]{2,1,0:T(8,128)(2,1)S(1)}) custom-call(bf16[4,128,1024]{2,1,0:T(8,128)(2,1)S(1)} %get-tuple-element.62.refs_0_.refs_1_, bf16[4,128,512]{2,1,0:T(8,128)(2,1)S(1)} %get-tuple-element.50.refs_1_.refs_2_, f32[4,4,128,16]{3,2,1,0:T(8,128)S(1)} %get-tuple-element.56.refs_2_, ...), custom_call_target="tpu_custom_call" | custom-call | flops 1600000000 | bytes 5600000 | tf_op jit(solution)/shard_map/block_states/pallas_call | solution.py:54
  19.9 4.1 %collective-permute-done.3.refs_5_ = bf16[2,1024,128]{2,1,0:T(8,128)(2,1)S(1)} collective-permute-done((bf16[2,1024,128]{2,1,0:T(8,128)(2,1)S(1)}, bf16[2,1024,128]{2,1,0:T(8,128)(2,1)S(1)}, u32[]{:S(2)}, u32[]{:S(2)}) %collective-permute-start.3) | collective-permute-done | bytes 524320 | tf_op jit(solution)/shard_map/ppermute | solution.py:355
  24.0 1.3 collective-permute-start.5
  25.3 2.1 %parents.1.refs_7_.refs_13_.refs_6_.refs_10_.refs_1_ = bf16[4,128,1024]{2,1,0:T(8,128)(2,1)S(1)} custom-call(s32[11]{0:T(128)S(1)} %get-tuple-element.47.info_ref.refs_0_.ids_ref, s32[8]{0:T(128)S(1)} %copy-done, s32[4]{0:T(128)S(1)} %copy-done.1, s32[4]{0:T(128)S(1)} %copy-done.2, f32[2,2,1024,128]{3,2,1,0:T(8,128)} %bitcast.11, ...), custom_call_target="tpu_custom_call" | custom-call | flops 2000000000 | bytes 7000000 | tf_op jit(solution)/shard_map/parents/pallas_call | solution.py:640
  27.4 4.6 %collective-permute-start.8 = (bf16[4,128,1024]{2,1,0:T(8,128)(2,1)S(1)}, bf16[4,128,1024]{2,1,0:T(8,128)(2,1)S(1)}, u32[]{:S(2)}, u32[]{:S(2)}) collective-permute-start(bf16[4,128,1024]{2,1,0:T(8,128)(2,1)S(1)} %parents.1.refs_7_.refs_13_.refs_6_.refs_10_.refs_1_), channel_id=1, source_target_pairs={{4,0},{8,4},{12,8},{5,1},{9,5},{13,9},{6,2},{10,6},{14,10},{7,3},{... | collective-permute-start | bytes 3145736 | tf_op jit(solution)/shard_map/ppermute | solution.py:461
  32.0 1.8 %decays.1.refs_3_.refs_6_.refs_1_.refs_5_.refs_0_ = f32[4,4,1,4096]{3,2,1,0:T(1,128)S(1)} custom-call(s32[11]{0:T(128)S(1)} %get-tuple-element.47.info_ref.refs_0_.ids_ref, bf16[4,64,128]{2,1,0:T(8,128)(2,1)S(1)} %get-tuple-element.58.refs_1_, bf16[4,64,128]{2,1,0:T(8,128)(2,1)S(1)} %collective-permute-done.refs_2_, ...), custom_call_target="tpu_custom_call" | custom-call | flops 1600000000 | bytes 5600000 | tf_op jit(solution)/shard_map/decays/pallas_call | solution.py:54
  33.8 1.6 %block_states.4 = (bf16[2,128,1024]{2,1,0:T(8,128)(2,1)S(1)}, bf16[2,128,1024]{2,1,0:T(8,128)(2,1)S(1)}) custom-call(bf16[4,128,1024]{2,1,0:T(8,128)(2,1)S(1)} %get-tuple-element.57.refs_0_.refs_1_, bf16[4,128,512]{2,1,0:T(8,128)(2,1)S(1)} %get-tuple-element.50.refs_1_.refs_2_, f32[4,4,128,16]{3,2,1,0:T(8,128)S(1)} %get-tuple-element.56.refs_2_, ...), custom_call_target="tpu_custom_call" | custom-call | flops 1600000000 | bytes 5600000 | tf_op jit(solution)/shard_map/block_states/pallas_call | solution.py:54
  35.4 1.6 %block_states.5 = (bf16[2,128,1024]{2,1,0:T(8,128)(2,1)S(1)}, bf16[2,128,1024]{2,1,0:T(8,128)(2,1)S(1)}) custom-call(bf16[4,128,1024]{2,1,0:T(8,128)(2,1)S(1)} %get-tuple-element.49.refs_0_.refs_1_, bf16[4,128,512]{2,1,0:T(8,128)(2,1)S(1)} %get-tuple-element.50.refs_1_.refs_2_, f32[4,4,128,16]{3,2,1,0:T(8,128)S(1)} %get-tuple-element.56.refs_2_, ...), custom_call_target="tpu_custom_call" | custom-call | flops 1600000000 | bytes 5600000 | tf_op jit(solution)/shard_map/block_states/pallas_call | solution.py:54
  37.6 1.3 collective-permute-start.9
  38.9 1.8 %local_sums.4 = (f32[4,128,1024]{2,1,0:T(8,128)S(1)}, bf16[4,128,1024]{2,1,0:T(8,128)(2,1)S(1)}) custom-call(s32[11]{0:T(128)S(1)} %get-tuple-element.47.info_ref.refs_0_.ids_ref, bf16[4,128,1024]{2,1,0:T(8,128)(2,1)S(1)} %get-tuple-element.70.refs_1_, bf16[4,128,512]{2,1,0:T(8,128)(2,1)S(1)} %get-tuple-element.50.refs_1_.refs_2_, ...), custom_call_target="tpu_custom_call" | custom-call | flops 4000000000 | bytes 14000000 | tf_op jit(solution)/shard_map/local_sums/pallas_call | solution.py:467
  40.7 1.2 pass_on.12.refs_9_
  41.9 1.9 %collective-permute-start.7 = (bf16[2,128,1024]{2,1,0:T(8,128)(2,1)S(1)}, bf16[2,128,1024]{2,1,0:T(8,128)(2,1)S(1)}, u32[]{:S(2)}, u32[]{:S(2)}) collective-permute-start(bf16[2,128,1024]{2,1,0:T(8,128)(2,1)S(1)} %pass_on.12.refs_9_), channel_id=1, source_target_pairs={{0,4},{4,8},{8,12},{1,5},{5,9},{9,13},{2,6},{6,10},{10,14},{3,7},{... | collective-permute-start | bytes 1572872 | tf_op jit(solution)/shard_map/ppermute | solution.py:417
  43.8 1.8 %local_sums.5 = (f32[4,128,1024]{2,1,0:T(8,128)S(1)}, bf16[4,128,1024]{2,1,0:T(8,128)(2,1)S(1)}) custom-call(s32[11]{0:T(128)S(1)} %get-tuple-element.47.info_ref.refs_0_.ids_ref, bf16[4,128,1024]{2,1,0:T(8,128)(2,1)S(1)} %get-tuple-element.62.refs_0_.refs_1_, bf16[4,128,512]{2,1,0:T(8,128)(2,1)S(1)} %get-tuple-element.50.refs_1_.refs_2_, ...), custom_call_target="tpu_custom_call" | custom-call | flops 4000000000 | bytes 14000000 | tf_op jit(solution)/shard_map/local_sums/pallas_call | solution.py:467
  45.6 7.1 %collective-permute-done.9.refs_4_.refs_11_.refs_10_.refs_6_ = bf16[2,128,1024]{2,1,0:T(8,128)(2,1)S(1)} collective-permute-done((bf16[2,128,1024]{2,1,0:T(8,128)(2,1)S(1)}, bf16[2,128,1024]{2,1,0:T(8,128)(2,1)S(1)}, u32[]{:S(2)}, u32[]{:S(2)}) %collective-permute-start.9) | collective-permute-done | bytes 524320 | tf_op jit(solution)/shard_map/ppermute | solution.py:417
  52.7 1.0 pass_on.13.refs_5_
  53.7 1.9 %collective-permute-start.10 = (bf16[2,128,1024]{2,1,0:T(8,128)(2,1)S(1)}, bf16[2,128,1024]{2,1,0:T(8,128)(2,1)S(1)}, u32[]{:S(2)}, u32[]{:S(2)}) collective-permute-start(bf16[2,128,1024]{2,1,0:T(8,128)(2,1)S(1)} %pass_on.13.refs_5_), channel_id=1, source_target_pairs={{0,4},{4,8},{8,12},{1,5},{5,9},{9,13},{2,6},{6,10},{10,14},{3,7},{... | collective-permute-start | bytes 1572872 | tf_op jit(solution)/shard_map/ppermute | solution.py:417
  56.2 12.0 %collective-permute-start.13 = (bf16[4,128,1024]{2,1,0:T(8,128)(2,1)S(1)}, bf16[4,128,1024]{2,1,0:T(8,128)(2,1)S(1)}, u32[]{:S(2)}, u32[]{:S(2)}) collective-permute-start(bf16[4,128,1024]{2,1,0:T(8,128)(2,1)S(1)} %pass_down.3.refs_9_), channel_id=1, source_target_pairs={{4,0},{8,4},{12,8},{5,1},{9,5},{13,9},{6,2},{10,6},{14,10},{7,3},{... | collective-permute-start | bytes 3145736 | tf_op jit(solution)/shard_map/ppermute | solution.py:461
  68.3 1.8 %local_sums.6 = (f32[4,128,1024]{2,1,0:T(8,128)S(1)}, bf16[4,128,1024]{2,1,0:T(8,128)(2,1)S(1)}) custom-call(s32[11]{0:T(128)S(1)} %get-tuple-element.47.info_ref.refs_0_.ids_ref, bf16[4,128,1024]{2,1,0:T(8,128)(2,1)S(1)} %get-tuple-element.57.refs_0_.refs_1_, bf16[4,128,512]{2,1,0:T(8,128)(2,1)S(1)} %get-tuple-element.50.refs_1_.refs_2_, ...), custom_call_target="tpu_custom_call" | custom-call | flops 4000000000 | bytes 14000000 | tf_op jit(solution)/shard_map/local_sums/pallas_call | solution.py:467
  70.1 0.8 pass_on.14.refs_9_
  70.9 1.9 %collective-permute-start.12 = (bf16[2,128,1024]{2,1,0:T(8,128)(2,1)S(1)}, bf16[2,128,1024]{2,1,0:T(8,128)(2,1)S(1)}, u32[]{:S(2)}, u32[]{:S(2)}) collective-permute-start(bf16[2,128,1024]{2,1,0:T(8,128)(2,1)S(1)} %pass_on.14.refs_9_), channel_id=1, source_target_pairs={{0,4},{4,8},{8,12},{1,5},{5,9},{9,13},{2,6},{6,10},{10,14},{3,7},{... | collective-permute-start | bytes 1572872 | tf_op jit(solution)/shard_map/ppermute | solution.py:417
  72.8 1.8 %local_sums.7 = (f32[4,128,1024]{2,1,0:T(8,128)S(1)}, bf16[4,128,1024]{2,1,0:T(8,128)(2,1)S(1)}) custom-call(s32[11]{0:T(128)S(1)} %get-tuple-element.47.info_ref.refs_0_.ids_ref, bf16[4,128,1024]{2,1,0:T(8,128)(2,1)S(1)} %get-tuple-element.49.refs_0_.refs_1_, bf16[4,128,512]{2,1,0:T(8,128)(2,1)S(1)} %get-tuple-element.50.refs_1_.refs_2_, ...), custom_call_target="tpu_custom_call" | custom-call | flops 4000000000 | bytes 14000000 | tf_op jit(solution)/shard_map/local_sums/pallas_call | solution.py:467
  76.2 1.9 %collective-permute-start.11 = (bf16[2,128,1024]{2,1,0:T(8,128)(2,1)S(1)}, bf16[2,128,1024]{2,1,0:T(8,128)(2,1)S(1)}, u32[]{:S(2)}, u32[]{:S(2)}) collective-permute-start(bf16[2,128,1024]{2,1,0:T(8,128)(2,1)S(1)} %pass_on.15.refs_7_), channel_id=1, source_target_pairs={{0,4},{4,8},{8,12},{1,5},{5,9},{9,13},{2,6},{6,10},{10,14},{3,7},{... | collective-permute-start | bytes 1572872 | tf_op jit(solution)/shard_map/ppermute | solution.py:417
  78.1 8.0 %collective-permute-done.13.refs_2_.refs_15_ = bf16[4,128,1024]{2,1,0:T(8,128)(2,1)S(1)} collective-permute-done((bf16[4,128,1024]{2,1,0:T(8,128)(2,1)S(1)}, bf16[4,128,1024]{2,1,0:T(8,128)(2,1)S(1)}, u32[]{:S(2)}, u32[]{:S(2)}) %collective-permute-start.13) | collective-permute-done | bytes 1048608 | tf_op jit(solution)/shard_map/ppermute | solution.py:461
  86.1 0.9 pass_down.4.refs_16_
  87.0 4.1 %collective-permute-start.16 = (bf16[4,128,1024]{2,1,0:T(8,128)(2,1)S(1)}, bf16[4,128,1024]{2,1,0:T(8,128)(2,1)S(1)}, u32[]{:S(2)}, u32[]{:S(2)}) collective-permute-start(bf16[4,128,1024]{2,1,0:T(8,128)(2,1)S(1)} %pass_down.4.refs_16_), channel_id=1, source_target_pairs={{4,0},{8,4},{12,8},{5,1},{9,5},{13,9},{6,2},{10,6},{14,10},{7,3},{... | collective-permute-start | bytes 3145736 | tf_op jit(solution)/shard_map/ppermute | solution.py:461
  91.1 2.8 %finish.5 = (bf16[4,128,4096]{2,1,0:T(8,128)(2,1)}, f32[8,128]{1,0:T(8,128)S(1)}) custom-call(s32[11]{0:T(128)S(1)} %get-tuple-element.47.info_ref.refs_0_.ids_ref, f32[4,128,1024]{2,1,0:T(8,128)S(1)} %get-tuple-element.72.refs_8_.refs_1_, bf16[4,128,1024]{2,1,0:T(8,128)(2,1)S(1)} %get-tuple-element.78.refs_2_, ...), custom_call_target="tpu_custom_call" | custom-call | flops 6000000000 | bytes 21000000 | tf_op jit(solution)/shard_map/finish/pallas_call | solution.py:565
  94.8 1.9 %collective-permute-start.15 = (bf16[2,128,1024]{2,1,0:T(8,128)(2,1)S(1)}, bf16[2,128,1024]{2,1,0:T(8,128)(2,1)S(1)}, u32[]{:S(2)}, u32[]{:S(2)}) collective-permute-start(bf16[2,128,1024]{2,1,0:T(8,128)(2,1)S(1)} %pass_on.16.refs_7_), channel_id=1, source_target_pairs={{4,8},{8,12},{5,9},{9,13},{6,10},{10,14},{7,11},{11,15},{20,24},{2... | collective-permute-start | bytes 1572872 | tf_op jit(solution)/shard_map/ppermute | solution.py:417
  96.7 1.6 %collective-permute-done.11.refs_3_.refs_12_.refs_11_.refs_4_.refs_8_.refs_7_ = bf16[2,128,1024]{2,1,0:T(8,128)(2,1)S(1)} collective-permute-done((bf16[2,128,1024]{2,1,0:T(8,128)(2,1)S(1)}, bf16[2,128,1024]{2,1,0:T(8,128)(2,1)S(1)}, u32[]{:S(2)}, u32[]{:S(2)}) %collective-permute-start.11) | collective-permute-done | bytes 524320 | tf_op jit(solution)/shard_map/ppermute | solution.py:417
  99.1 1.9 %collective-permute-start.14 = (bf16[2,128,1024]{2,1,0:T(8,128)(2,1)S(1)}, bf16[2,128,1024]{2,1,0:T(8,128)(2,1)S(1)}, u32[]{:S(2)}, u32[]{:S(2)}) collective-permute-start(bf16[2,128,1024]{2,1,0:T(8,128)(2,1)S(1)} %pass_on.17.refs_9_), channel_id=1, source_target_pairs={{4,8},{8,12},{5,9},{9,13},{6,10},{10,14},{7,11},{11,15},{20,24},{2... | collective-permute-start | bytes 1572872 | tf_op jit(solution)/shard_map/ppermute | solution.py:417
  101.0 7.6 %collective-permute-done.16.refs_2_.refs_16_ = bf16[4,128,1024]{2,1,0:T(8,128)(2,1)S(1)} collective-permute-done((bf16[4,128,1024]{2,1,0:T(8,128)(2,1)S(1)}, bf16[4,128,1024]{2,1,0:T(8,128)(2,1)S(1)}, u32[]{:S(2)}, u32[]{:S(2)}) %collective-permute-start.16) | collective-permute-done | bytes 1048608 | tf_op jit(solution)/shard_map/ppermute | solution.py:461
  108.7 0.9 pass_down.5.refs_17_
  109.5 4.4 %collective-permute-start.18 = (bf16[4,128,1024]{2,1,0:T(8,128)(2,1)S(1)}, bf16[4,128,1024]{2,1,0:T(8,128)(2,1)S(1)}, u32[]{:S(2)}, u32[]{:S(2)}) collective-permute-start(bf16[4,128,1024]{2,1,0:T(8,128)(2,1)S(1)} %pass_down.5.refs_17_), channel_id=1, source_target_pairs={{4,0},{8,4},{12,8},{5,1},{9,5},{13,9},{6,2},{10,6},{14,10},{7,3},{... | collective-permute-start | bytes 3145736 | tf_op jit(solution)/shard_map/ppermute | solution.py:461
  114.0 2.9 %finish.6 = (bf16[4,128,4096]{2,1,0:T(8,128)(2,1)}, f32[8,128]{1,0:T(8,128)S(1)}) custom-call(s32[11]{0:T(128)S(1)} %get-tuple-element.47.info_ref.refs_0_.ids_ref, f32[4,128,1024]{2,1,0:T(8,128)S(1)} %get-tuple-element.73.refs_8_.refs_1_, bf16[4,128,1024]{2,1,0:T(8,128)(2,1)S(1)} %get-tuple-element.80.refs_2_, ...), custom_call_target="tpu_custom_call", output_to_operand_aliasing={{0}: (18, {})} | custom-call | flops 6000000000 | bytes 21000000 | tf_op jit(solution)/shard_map/finish/pallas_call | solution.py:565
  116.8 1.0 pass_on.18.refs_4_
  117.9 1.3 collective-permute-start.19
  120.0 1.3 collective-permute-start.17
  121.4 2.6 %finish.7 = (bf16[4,128,4096]{2,1,0:T(8,128)(2,1)}, f32[8,128]{1,0:T(8,128)S(1)}) custom-call(s32[11]{0:T(128)S(1)} %get-tuple-element.47.info_ref.refs_0_.ids_ref, f32[4,128,1024]{2,1,0:T(8,128)S(1)} %get-tuple-element.74.refs_6_.refs_1_, bf16[4,128,1024]{2,1,0:T(8,128)(2,1)S(1)} %get-tuple-element.83.refs_2_, ...), custom_call_target="tpu_custom_call", output_to_operand_aliasing={{0}: (15, {})} | custom-call | flops 6000000000 | bytes 21000000 | tf_op jit(solution)/shard_map/finish/pallas_call | solution.py:565
  123.9 7.6 %collective-permute-done.19.refs_9_ = bf16[2,128,1024]{2,1,0:T(8,128)(2,1)S(1)} collective-permute-done((bf16[2,128,1024]{2,1,0:T(8,128)(2,1)S(1)}, bf16[2,128,1024]{2,1,0:T(8,128)(2,1)S(1)}, u32[]{:S(2)}, u32[]{:S(2)}) %collective-permute-start.19) | collective-permute-done | bytes 524320 | tf_op jit(solution)/shard_map/ppermute | solution.py:417
  131.5 1.9 %finish.8 = (bf16[4,128,4096]{2,1,0:T(8,128)(2,1)}, f32[8,128]{1,0:T(8,128)S(1)}) custom-call(s32[11]{0:T(128)S(1)} %get-tuple-element.47.info_ref.refs_0_.ids_ref, f32[4,128,1024]{2,1,0:T(8,128)S(1)} %get-tuple-element.75.refs_6_.refs_1_, bf16[4,128,1024]{2,1,0:T(8,128)(2,1)S(1)} %get-tuple-element.76.refs_2_, ...), custom_call_target="tpu_custom_call", output_to_operand_aliasing={{0}: (13, {})} | custom-call | flops 6000000000 | bytes 21000000 | tf_op jit(solution)/shard_map/finish/pallas_call | solution.py:565
  133.5 2.7 %final_states.1 = (f32[4,1024,128]{2,1,0:T(8,128)}, f32[8,128]{1,0:T(8,128)S(1)}) custom-call(s32[11]{0:T(128)S(1)} %get-tuple-element.47.info_ref.refs_0_.ids_ref, f32[4,4,1,4096]{3,2,1,0:T(1,128)S(1)} %decays.1.refs_3_.refs_6_.refs_1_.refs_5_.refs_0_, bf16[4,128,1024]{2,1,0:T(8,128)(2,1)S(1)} %parents.1.refs_7_.refs_13_.refs_6_.refs_10_.refs_1_, ...), custom_call_target="tpu_custom_call" | custom-call | flops 10800000000 | bytes 37800000 | tf_op jit(solution)/shard_map/final_states/pallas_call | solution.py:623
  136.1 1.5 %collective-permute-done.17.refs_9_ = bf16[2,128,1024]{2,1,0:T(8,128)(2,1)S(1)} collective-permute-done((bf16[2,128,1024]{2,1,0:T(8,128)(2,1)S(1)}, bf16[2,128,1024]{2,1,0:T(8,128)(2,1)S(1)}, u32[]{:S(2)}, u32[]{:S(2)}) %collective-permute-start.17) | collective-permute-done | bytes 524320 | tf_op jit(solution)/shard_map/ppermute | solution.py:417
  137.7 2.5 %finish.9 = (bf16[4,128,4096]{2,1,0:T(8,128)(2,1)}, f32[8,128]{1,0:T(8,128)}) custom-call(s32[11]{0:T(128)S(1)} %get-tuple-element.47.info_ref.refs_0_.ids_ref, f32[4,128,1024]{2,1,0:T(8,128)S(1)} %get-tuple-element.75.refs_6_.refs_1_, bf16[4,128,1024]{2,1,0:T(8,128)(2,1)S(1)} %get-tuple-element.76.refs_2_, ...), custom_call_target="tpu_custom_call", output_to_operand_aliasing={{0}: (13, {})} | custom-call | flops 6000000000 | bytes 21000000 | tf_op jit(solution)/shard_map/finish/pallas_call | solution.py:565
  (29 shorter events, 7.2 us)
Async XLA Ops:
  6.6 12.0 %collective-permute-start.4 = (bf16[2,128,1024]{2,1,0:T(8,128)(2,1)S(1)}, bf16[2,128,1024]{2,1,0:T(8,128)(2,1)S(1)}, u32[]{:S(2)}, u32[]{:S(2)}) collective-permute-start(bf16[2,128,1024]{2,1,0:T(8,128)(2,1)S(1)} %get-tuple-element.64.refs_2_.refs_3_.refs_9_), channel_id=1, source_target_pairs={{0,4},{1,5},{2,6},{3,7},{16,20},{17,21},{18,22},{19,23}} | collective-permute-start | bytes 1572872 | tf_op jit(solution)/shard_map/ppermute | solution.py:417
  10.2 13.7 %collective-permute-start.3 = (bf16[2,1024,128]{2,1,0:T(8,128)(2,1)S(1)}, bf16[2,1024,128]{2,1,0:T(8,128)(2,1)S(1)}, u32[]{:S(2)}, u32[]{:S(2)}) collective-permute-start(bf16[2,1024,128]{2,1,0:T(8,128)(2,1)S(1)} %get-tuple-element.61), channel_id=1, source_target_pairs={{0,2},{2,0},{1,3},{3,1},{4,6},{6,4},{5,7},{7,5},{8,10},{10,8},{9,1... | collective-permute-start | bytes 1572872 | tf_op jit(solution)/shard_map/ppermute | solution.py:355
  11.8 15.6 %collective-permute-start.2 = (bf16[4,64,128]{2,1,0:T(8,128)(2,1)S(1)}, bf16[4,64,128]{2,1,0:T(8,128)(2,1)S(1)}, u32[]{:S(2)}, u32[]{:S(2)}) collective-permute-start(bf16[4,64,128]{2,1,0:T(8,128)(2,1)S(1)} %get-tuple-element.58.refs_1_), channel_id=1, source_target_pairs={{0,12},{4,0},{8,4},{12,8},{1,13},{5,1},{9,5},{13,9},{2,14},{6,2},{... | collective-permute-start | bytes 196616 | tf_op jit(solution)/shard_map/ppermute | solution.py:352
  12.8 19.2 %collective-permute-start.1 = (bf16[4,64,128]{2,1,0:T(8,128)(2,1)S(1)}, bf16[4,64,128]{2,1,0:T(8,128)(2,1)S(1)}, u32[]{:S(2)}, u32[]{:S(2)}) collective-permute-start(bf16[4,64,128]{2,1,0:T(8,128)(2,1)S(1)} %get-tuple-element.58.refs_1_), channel_id=1, source_target_pairs={{0,8},{4,12},{8,0},{12,4},{1,9},{5,13},{9,1},{13,5},{2,10},{6,14},... | collective-permute-start | bytes 196616 | tf_op jit(solution)/shard_map/ppermute | solution.py:352
  15.7 16.3 %collective-permute-start = (bf16[4,64,128]{2,1,0:T(8,128)(2,1)S(1)}, bf16[4,64,128]{2,1,0:T(8,128)(2,1)S(1)}, u32[]{:S(2)}, u32[]{:S(2)}) collective-permute-start(bf16[4,64,128]{2,1,0:T(8,128)(2,1)S(1)} %get-tuple-element.58.refs_1_), channel_id=1, source_target_pairs={{0,4},{4,8},{8,12},{12,0},{1,5},{5,9},{9,13},{13,1},{2,6},{6,10},{... | collective-permute-start | bytes 196616 | tf_op jit(solution)/shard_map/ppermute | solution.py:352
  18.6 18.4 %collective-permute-start.6 = (bf16[2,128,1024]{2,1,0:T(8,128)(2,1)S(1)}, bf16[2,128,1024]{2,1,0:T(8,128)(2,1)S(1)}, u32[]{:S(2)}, u32[]{:S(2)}) collective-permute-start(bf16[2,128,1024]{2,1,0:T(8,128)(2,1)S(1)} %get-tuple-element.48._.refs_2_.refs_3_.refs_4_.refs_10_), channel_id=1, source_target_pairs={{0,4},{1,5},{2,6},{3,7},{16,20},{17,21},{18,22},{19,23}} | collective-permute-start | bytes 1572872 | tf_op jit(solution)/shard_map/ppermute | solution.py:417
  19.3 5.9 %copy-start = (s32[8]{0:T(128)S(1)}, s32[8]{0:T(128)}, u32[]{:S(2)}) copy-start(s32[8]{0:T(128)} %refs_1_.1) | copy-start | bytes 100
  19.3 5.9 %copy-start.1 = (s32[4]{0:T(128)S(1)}, s32[4]{0:T(128)}, u32[]{:S(2)}) copy-start(s32[4]{0:T(128)} %refs_2_.1) | copy-start | bytes 52
  19.3 5.9 %copy-start.2 = (s32[4]{0:T(128)S(1)}, s32[4]{0:T(128)}, u32[]{:S(2)}) copy-start(s32[4]{0:T(128)} %refs_3_.1) | copy-start | bytes 52
  24.0 16.7 %collective-permute-start.5 = (bf16[2,128,1024]{2,1,0:T(8,128)(2,1)S(1)}, bf16[2,128,1024]{2,1,0:T(8,128)(2,1)S(1)}, u32[]{:S(2)}, u32[]{:S(2)}) collective-permute-start(bf16[2,128,1024]{2,1,0:T(8,128)(2,1)S(1)} %pass_on.10.refs_6_), channel_id=1, source_target_pairs={{0,4},{4,8},{1,5},{5,9},{2,6},{6,10},{3,7},{7,11},{16,20},{20,24},... | collective-permute-start | bytes 1572872 | tf_op jit(solution)/shard_map/ppermute | solution.py:417
  27.4 28.1 %collective-permute-start.8 = (bf16[4,128,1024]{2,1,0:T(8,128)(2,1)S(1)}, bf16[4,128,1024]{2,1,0:T(8,128)(2,1)S(1)}, u32[]{:S(2)}, u32[]{:S(2)}) collective-permute-start(bf16[4,128,1024]{2,1,0:T(8,128)(2,1)S(1)} %parents.1.refs_7_.refs_13_.refs_6_.refs_10_.refs_1_), channel_id=1, source_target_pairs={{4,0},{8,4},{12,8},{5,1},{9,5},{13,9},{6,2},{10,6},{14,10},{7,3},{... | collective-permute-start | bytes 3145736 | tf_op jit(solution)/shard_map/ppermute | solution.py:461
  37.6 15.1 %collective-permute-start.9 = (bf16[2,128,1024]{2,1,0:T(8,128)(2,1)S(1)}, bf16[2,128,1024]{2,1,0:T(8,128)(2,1)S(1)}, u32[]{:S(2)}, u32[]{:S(2)}) collective-permute-start(bf16[2,128,1024]{2,1,0:T(8,128)(2,1)S(1)} %pass_on.11.refs_9_), channel_id=1, source_target_pairs={{0,4},{4,8},{1,5},{5,9},{2,6},{6,10},{3,7},{7,11},{16,20},{20,24},... | collective-permute-start | bytes 1572872 | tf_op jit(solution)/shard_map/ppermute | solution.py:417
  41.9 28.2 %collective-permute-start.7 = (bf16[2,128,1024]{2,1,0:T(8,128)(2,1)S(1)}, bf16[2,128,1024]{2,1,0:T(8,128)(2,1)S(1)}, u32[]{:S(2)}, u32[]{:S(2)}) collective-permute-start(bf16[2,128,1024]{2,1,0:T(8,128)(2,1)S(1)} %pass_on.12.refs_9_), channel_id=1, source_target_pairs={{0,4},{4,8},{8,12},{1,5},{5,9},{9,13},{2,6},{6,10},{10,14},{3,7},{... | collective-permute-start | bytes 1572872 | tf_op jit(solution)/shard_map/ppermute | solution.py:417
  53.7 21.7 %collective-permute-start.10 = (bf16[2,128,1024]{2,1,0:T(8,128)(2,1)S(1)}, bf16[2,128,1024]{2,1,0:T(8,128)(2,1)S(1)}, u32[]{:S(2)}, u32[]{:S(2)}) collective-permute-start(bf16[2,128,1024]{2,1,0:T(8,128)(2,1)S(1)} %pass_on.13.refs_5_), channel_id=1, source_target_pairs={{0,4},{4,8},{8,12},{1,5},{5,9},{9,13},{2,6},{6,10},{10,14},{3,7},{... | collective-permute-start | bytes 1572872 | tf_op jit(solution)/shard_map/ppermute | solution.py:417
  56.2 29.8 %collective-permute-start.13 = (bf16[4,128,1024]{2,1,0:T(8,128)(2,1)S(1)}, bf16[4,128,1024]{2,1,0:T(8,128)(2,1)S(1)}, u32[]{:S(2)}, u32[]{:S(2)}) collective-permute-start(bf16[4,128,1024]{2,1,0:T(8,128)(2,1)S(1)} %pass_down.3.refs_9_), channel_id=1, source_target_pairs={{4,0},{8,4},{12,8},{5,1},{9,5},{13,9},{6,2},{10,6},{14,10},{7,3},{... | collective-permute-start | bytes 3145736 | tf_op jit(solution)/shard_map/ppermute | solution.py:461
  70.9 23.0 %collective-permute-start.12 = (bf16[2,128,1024]{2,1,0:T(8,128)(2,1)S(1)}, bf16[2,128,1024]{2,1,0:T(8,128)(2,1)S(1)}, u32[]{:S(2)}, u32[]{:S(2)}) collective-permute-start(bf16[2,128,1024]{2,1,0:T(8,128)(2,1)S(1)} %pass_on.14.refs_9_), channel_id=1, source_target_pairs={{0,4},{4,8},{8,12},{1,5},{5,9},{9,13},{2,6},{6,10},{10,14},{3,7},{... | collective-permute-start | bytes 1572872 | tf_op jit(solution)/shard_map/ppermute | solution.py:417
  76.2 22.1 %collective-permute-start.11 = (bf16[2,128,1024]{2,1,0:T(8,128)(2,1)S(1)}, bf16[2,128,1024]{2,1,0:T(8,128)(2,1)S(1)}, u32[]{:S(2)}, u32[]{:S(2)}) collective-permute-start(bf16[2,128,1024]{2,1,0:T(8,128)(2,1)S(1)} %pass_on.15.refs_7_), channel_id=1, source_target_pairs={{0,4},{4,8},{8,12},{1,5},{5,9},{9,13},{2,6},{6,10},{10,14},{3,7},{... | collective-permute-start | bytes 1572872 | tf_op jit(solution)/shard_map/ppermute | solution.py:417
  87.0 21.7 %collective-permute-start.16 = (bf16[4,128,1024]{2,1,0:T(8,128)(2,1)S(1)}, bf16[4,128,1024]{2,1,0:T(8,128)(2,1)S(1)}, u32[]{:S(2)}, u32[]{:S(2)}) collective-permute-start(bf16[4,128,1024]{2,1,0:T(8,128)(2,1)S(1)} %pass_down.4.refs_16_), channel_id=1, source_target_pairs={{4,0},{8,4},{12,8},{5,1},{9,5},{13,9},{6,2},{10,6},{14,10},{7,3},{... | collective-permute-start | bytes 3145736 | tf_op jit(solution)/shard_map/ppermute | solution.py:461
  94.8 22.1 %collective-permute-start.15 = (bf16[2,128,1024]{2,1,0:T(8,128)(2,1)S(1)}, bf16[2,128,1024]{2,1,0:T(8,128)(2,1)S(1)}, u32[]{:S(2)}, u32[]{:S(2)}) collective-permute-start(bf16[2,128,1024]{2,1,0:T(8,128)(2,1)S(1)} %pass_on.16.refs_7_), channel_id=1, source_target_pairs={{4,8},{8,12},{5,9},{9,13},{6,10},{10,14},{7,11},{11,15},{20,24},{2... | collective-permute-start | bytes 1572872 | tf_op jit(solution)/shard_map/ppermute | solution.py:417
  99.1 20.1 %collective-permute-start.14 = (bf16[2,128,1024]{2,1,0:T(8,128)(2,1)S(1)}, bf16[2,128,1024]{2,1,0:T(8,128)(2,1)S(1)}, u32[]{:S(2)}, u32[]{:S(2)}) collective-permute-start(bf16[2,128,1024]{2,1,0:T(8,128)(2,1)S(1)} %pass_on.17.refs_9_), channel_id=1, source_target_pairs={{4,8},{8,12},{5,9},{9,13},{6,10},{10,14},{7,11},{11,15},{20,24},{2... | collective-permute-start | bytes 1572872 | tf_op jit(solution)/shard_map/ppermute | solution.py:417
  109.5 23.9 %collective-permute-start.18 = (bf16[4,128,1024]{2,1,0:T(8,128)(2,1)S(1)}, bf16[4,128,1024]{2,1,0:T(8,128)(2,1)S(1)}, u32[]{:S(2)}, u32[]{:S(2)}) collective-permute-start(bf16[4,128,1024]{2,1,0:T(8,128)(2,1)S(1)} %pass_down.5.refs_17_), channel_id=1, source_target_pairs={{4,0},{8,4},{12,8},{5,1},{9,5},{13,9},{6,2},{10,6},{14,10},{7,3},{... | collective-permute-start | bytes 3145736 | tf_op jit(solution)/shard_map/ppermute | solution.py:461
  117.9 13.7 %collective-permute-start.19 = (bf16[2,128,1024]{2,1,0:T(8,128)(2,1)S(1)}, bf16[2,128,1024]{2,1,0:T(8,128)(2,1)S(1)}, u32[]{:S(2)}, u32[]{:S(2)}) collective-permute-start(bf16[2,128,1024]{2,1,0:T(8,128)(2,1)S(1)} %pass_on.18.refs_4_), channel_id=1, source_target_pairs={{8,12},{9,13},{10,14},{11,15},{24,28},{25,29},{26,30},{27,31}} | collective-permute-start | bytes 1572872 | tf_op jit(solution)/shard_map/ppermute | solution.py:417
  120.0 17.6 %collective-permute-start.17 = (bf16[2,128,1024]{2,1,0:T(8,128)(2,1)S(1)}, bf16[2,128,1024]{2,1,0:T(8,128)(2,1)S(1)}, u32[]{:S(2)}, u32[]{:S(2)}) collective-permute-start(bf16[2,128,1024]{2,1,0:T(8,128)(2,1)S(1)} %pass_on.19.refs_14_), channel_id=1, source_target_pairs={{8,12},{9,13},{10,14},{11,15},{24,28},{25,29},{26,30},{27,31}} | collective-permute-start | bytes 1572872 | tf_op jit(solution)/shard_map/ppermute | solution.py:417

commit v6 on v5

--- a/solution.py
+++ b/solution.py
@@ -540,8 +540,8 @@
                     for q in range(PAIRS):
                         here = pair_lanes(q)
                         summed = local_ref[r, :, here] + carried[:, here] * spread_pair(grown, q, low)
-                        gate = z_ref[r, :, here].astype(F32)
-                        value = summed.astype(BF16).astype(F32) * (gate / (1.0 + jnp.exp(-gate)))
+                        half = 0.5 * z_ref[r, :, here].astype(F32)
+                        value = summed.astype(BF16).astype(F32) * (half + half * jnp.tanh(half))
                         gated.append(value)
                         squares = squares + value * value
                     inverse = lax.rsqrt(jnp.sum(squares, axis=1, keepdims=True) * (1.0 / GROUP_LANES) + EPS)

time: 142 us -> 142 us (level)
  waiting for transfers between devices: 38.2 us -> 36.1 us
    ppermute x12, waiting for transfers between devices: 18.5 us -> 15.5 us  [send_up(): received[h] = lax.ppermute(sent, 'tok', pairs)]
  transfers between devices with their start and end apart: 20 -> 20, of which waited for: 8 -> 8; matrix products, arithmetic and copies ran while one was open for 0% -> 0% of each run, Pallas kernels for 30% -> 31%
where the time goes in v6:
time: 142 us; the launch traced here: 139 us
  Pallas kernels  51.4 us (36%)
  starting transfers between devices  50.5 us (36%)
  waiting for transfers between devices  36.1 us (25%)
    ppermute x4, starting transfers between devices, send_down(): arrived.append(lax.ppermute(sent, 'tok', backward))  25.6 us
    ppermute x12, starting transfers between devices, send_up(): received[h] = lax.ppermute(sent, 'tok', pairs)  18.1 us
    pallas_call x17, Pallas kernels, call(): pl.pallas_call(kernel, out_shape=tuple((VMEM(shape, dtype) for shape, dty...  17.3 us
    ppermute x4, waiting for transfers between devices, send_down(): arrived.append(lax.ppermute(sent, 'tok', backward))  16.6 us
    ppermute x12, waiting for transfers between devices, send_up(): received[h] = lax.ppermute(sent, 'tok', pairs)  15.5 us
    pallas_call x5, Pallas kernels, finish(): pl.pallas_call(kernel, out_shape=(jax.ShapeDtypeStruct((requests, span, w...  12.9 us
    pallas_call x4, Pallas kernels, local_sums(): pl.pallas_call(lambda *refs: local_body(order[i], *refs[:1 + n_ins], refs...  7.11 us
    pallas_call x1, Pallas kernels, shards(): pl.pallas_call(functools.partial(front_body, order), out_shape=(jax.Shape...  5.87 us
  transfers between devices with their start and end apart: 20, of which 8 were waited for; matrix products, arithmetic and copies ran while one was open for 0% of the time, Pallas kernels for 31%

profile of v6, /device:TPU:16, one launch (start us, length us, event | category | flops | bytes accessed | tf_op | source)
XLA Modules:
  0.0 139.4 jit_solution(1984282678718766615)
XLA Ops:
  0.7 5.9 %front.1 = (s32[11]{0:T(128)S(1)}, f32[4,4,128,16]{3,2,1,0:T(8,128)S(1)}, f32[4,4,16,128]{3,2,1,0:T(8,128)S(1)}, f32[4,4,16,128]{3,2,1,0:T(8,128)S(1)}, f32[4,4,...) custom-call(s32[3]{0:T(128)S(1)} %pad_add_fusion.ids, ...), custom_call_target="tpu_custom_call" | custom-call | flops 20000000000 | bytes 70000000 | tf_op jit(solution)/shard_map/front/pallas_call | solution.py:290
  7.3 2.9 %loads.1 = (bf16[2,1024,128]{2,1,0:T(8,128)(2,1)S(1)}, bf16[4,128,512]{2,1,0:T(8,128)(2,1)S(1)}, bf16[4,128,1024]{2,1,0:T(8,128)(2,1)S(1)}, bf16[4,128,1024]{2,1,0:T(8,128)(2,1)S(1)}, bf16[4,128,1024]{2,1,0:T(8,128)(2,1)S(1)}) custom-call(s32[11]{0:T(128)S(1)} %get-tuple-element.47.info_ref.refs_0_.ids_ref, f32[2,2,1024,128]{3,2,1,0:T(8,128)} %bitcast.10, ...), custom_call_target="tpu_custom_call" | custom-call | flops 12000000000 | bytes 42000000 | tf_op jit(solution)/shard_map/loads/pallas_call | solution.py:339
  10.2 1.6 %collective-permute-start.3 = (bf16[2,1024,128]{2,1,0:T(8,128)(2,1)S(1)}, bf16[2,1024,128]{2,1,0:T(8,128)(2,1)S(1)}, u32[]{:S(2)}, u32[]{:S(2)}) collective-permute-start(bf16[2,1024,128]{2,1,0:T(8,128)(2,1)S(1)} %get-tuple-element.61), channel_id=1, source_target_pairs={{0,2},{2,0},{1,3},{3,1},{4,6},{6,4},{5,7},{7,5},{8,10},{10,8},{9,1... | collective-permute-start | bytes 1572872 | tf_op jit(solution)/shard_map/ppermute | solution.py:355
  11.8 1.0 collective-permute-start.2
  12.8 2.9 %collective-permute-start.1 = (bf16[4,64,128]{2,1,0:T(8,128)(2,1)S(1)}, bf16[4,64,128]{2,1,0:T(8,128)(2,1)S(1)}, u32[]{:S(2)}, u32[]{:S(2)}) collective-permute-start(bf16[4,64,128]{2,1,0:T(8,128)(2,1)S(1)} %get-tuple-element.58.refs_1_), channel_id=1, source_target_pairs={{0,8},{4,12},{8,0},{12,4},{1,9},{5,13},{9,1},{13,5},{2,10},{6,14},... | collective-permute-start | bytes 196616 | tf_op jit(solution)/shard_map/ppermute | solution.py:352
  15.7 1.2 collective-permute-start
  17.0 1.6 %block_states.3 = (bf16[2,128,1024]{2,1,0:T(8,128)(2,1)S(1)}, bf16[2,128,1024]{2,1,0:T(8,128)(2,1)S(1)}) custom-call(bf16[4,128,1024]{2,1,0:T(8,128)(2,1)S(1)} %get-tuple-element.62.refs_0_.refs_1_, bf16[4,128,512]{2,1,0:T(8,128)(2,1)S(1)} %get-tuple-element.50.refs_1_.refs_2_, f32[4,4,128,16]{3,2,1,0:T(8,128)S(1)} %get-tuple-element.56.refs_2_, ...), custom_call_target="tpu_custom_call" | custom-call | flops 1600000000 | bytes 5600000 | tf_op jit(solution)/shard_map/block_states/pallas_call | solution.py:54
  19.9 4.1 %collective-permute-done.3.refs_5_ = bf16[2,1024,128]{2,1,0:T(8,128)(2,1)S(1)} collective-permute-done((bf16[2,1024,128]{2,1,0:T(8,128)(2,1)S(1)}, bf16[2,1024,128]{2,1,0:T(8,128)(2,1)S(1)}, u32[]{:S(2)}, u32[]{:S(2)}) %collective-permute-start.3) | collective-permute-done | bytes 524320 | tf_op jit(solution)/shard_map/ppermute | solution.py:355
  24.0 1.3 collective-permute-start.5
  25.3 2.6 %parents.1.refs_7_.refs_13_.refs_6_.refs_10_.refs_1_ = bf16[4,128,1024]{2,1,0:T(8,128)(2,1)S(1)} custom-call(s32[11]{0:T(128)S(1)} %get-tuple-element.47.info_ref.refs_0_.ids_ref, s32[8]{0:T(128)S(1)} %copy-done, s32[4]{0:T(128)S(1)} %copy-done.1, s32[4]{0:T(128)S(1)} %copy-done.2, f32[2,2,1024,128]{3,2,1,0:T(8,128)} %bitcast.11, ...), custom_call_target="tpu_custom_call" | custom-call | flops 2000000000 | bytes 7000000 | tf_op jit(solution)/shard_map/parents/pallas_call | solution.py:640
  27.9 4.6 %collective-permute-start.8 = (bf16[4,128,1024]{2,1,0:T(8,128)(2,1)S(1)}, bf16[4,128,1024]{2,1,0:T(8,128)(2,1)S(1)}, u32[]{:S(2)}, u32[]{:S(2)}) collective-permute-start(bf16[4,128,1024]{2,1,0:T(8,128)(2,1)S(1)} %parents.1.refs_7_.refs_13_.refs_6_.refs_10_.refs_1_), channel_id=1, source_target_pairs={{4,0},{8,4},{12,8},{5,1},{9,5},{13,9},{6,2},{10,6},{14,10},{7,3},{... | collective-permute-start | bytes 3145736 | tf_op jit(solution)/shard_map/ppermute | solution.py:461
  32.5 1.8 %decays.1.refs_3_.refs_6_.refs_1_.refs_5_.refs_0_ = f32[4,4,1,4096]{3,2,1,0:T(1,128)S(1)} custom-call(s32[11]{0:T(128)S(1)} %get-tuple-element.47.info_ref.refs_0_.ids_ref, bf16[4,64,128]{2,1,0:T(8,128)(2,1)S(1)} %get-tuple-element.58.refs_1_, bf16[4,64,128]{2,1,0:T(8,128)(2,1)S(1)} %collective-permute-done.refs_2_, ...), custom_call_target="tpu_custom_call" | custom-call | flops 1600000000 | bytes 5600000 | tf_op jit(solution)/shard_map/decays/pallas_call | solution.py:54
  34.3 1.6 %block_states.4 = (bf16[2,128,1024]{2,1,0:T(8,128)(2,1)S(1)}, bf16[2,128,1024]{2,1,0:T(8,128)(2,1)S(1)}) custom-call(bf16[4,128,1024]{2,1,0:T(8,128)(2,1)S(1)} %get-tuple-element.57.refs_0_.refs_1_, bf16[4,128,512]{2,1,0:T(8,128)(2,1)S(1)} %get-tuple-element.50.refs_1_.refs_2_, f32[4,4,128,16]{3,2,1,0:T(8,128)S(1)} %get-tuple-element.56.refs_2_, ...), custom_call_target="tpu_custom_call" | custom-call | flops 1600000000 | bytes 5600000 | tf_op jit(solution)/shard_map/block_states/pallas_call | solution.py:54
  35.9 1.6 %block_states.5 = (bf16[2,128,1024]{2,1,0:T(8,128)(2,1)S(1)}, bf16[2,128,1024]{2,1,0:T(8,128)(2,1)S(1)}) custom-call(bf16[4,128,1024]{2,1,0:T(8,128)(2,1)S(1)} %get-tuple-element.49.refs_0_.refs_1_, bf16[4,128,512]{2,1,0:T(8,128)(2,1)S(1)} %get-tuple-element.50.refs_1_.refs_2_, f32[4,4,128,16]{3,2,1,0:T(8,128)S(1)} %get-tuple-element.56.refs_2_, ...), custom_call_target="tpu_custom_call" | custom-call | flops 1600000000 | bytes 5600000 | tf_op jit(solution)/shard_map/block_states/pallas_call | solution.py:54
  38.1 1.3 collective-permute-start.9
  39.4 1.8 %local_sums.4 = (f32[4,128,1024]{2,1,0:T(8,128)S(1)}, bf16[4,128,1024]{2,1,0:T(8,128)(2,1)S(1)}) custom-call(s32[11]{0:T(128)S(1)} %get-tuple-element.47.info_ref.refs_0_.ids_ref, bf16[4,128,1024]{2,1,0:T(8,128)(2,1)S(1)} %get-tuple-element.70.refs_1_, bf16[4,128,512]{2,1,0:T(8,128)(2,1)S(1)} %get-tuple-element.50.refs_1_.refs_2_, ...), custom_call_target="tpu_custom_call" | custom-call | flops 4000000000 | bytes 14000000 | tf_op jit(solution)/shard_map/local_sums/pallas_call | solution.py:467
  41.2 1.2 pass_on.12.refs_9_
  42.4 1.9 %collective-permute-start.7 = (bf16[2,128,1024]{2,1,0:T(8,128)(2,1)S(1)}, bf16[2,128,1024]{2,1,0:T(8,128)(2,1)S(1)}, u32[]{:S(2)}, u32[]{:S(2)}) collective-permute-start(bf16[2,128,1024]{2,1,0:T(8,128)(2,1)S(1)} %pass_on.12.refs_9_), channel_id=1, source_target_pairs={{0,4},{4,8},{8,12},{1,5},{5,9},{9,13},{2,6},{6,10},{10,14},{3,7},{... | collective-permute-start | bytes 1572872 | tf_op jit(solution)/shard_map/ppermute | solution.py:417
  44.3 1.8 %local_sums.5 = (f32[4,128,1024]{2,1,0:T(8,128)S(1)}, bf16[4,128,1024]{2,1,0:T(8,128)(2,1)S(1)}) custom-call(s32[11]{0:T(128)S(1)} %get-tuple-element.47.info_ref.refs_0_.ids_ref, bf16[4,128,1024]{2,1,0:T(8,128)(2,1)S(1)} %get-tuple-element.62.refs_0_.refs_1_, bf16[4,128,512]{2,1,0:T(8,128)(2,1)S(1)} %get-tuple-element.50.refs_1_.refs_2_, ...), custom_call_target="tpu_custom_call" | custom-call | flops 4000000000 | bytes 14000000 | tf_op jit(solution)/shard_map/local_sums/pallas_call | solution.py:467
  46.1 6.1 %collective-permute-done.9.refs_4_.refs_11_.refs_10_.refs_6_ = bf16[2,128,1024]{2,1,0:T(8,128)(2,1)S(1)} collective-permute-done((bf16[2,128,1024]{2,1,0:T(8,128)(2,1)S(1)}, bf16[2,128,1024]{2,1,0:T(8,128)(2,1)S(1)}, u32[]{:S(2)}, u32[]{:S(2)}) %collective-permute-start.9) | collective-permute-done | bytes 524320 | tf_op jit(solution)/shard_map/ppermute | solution.py:417
  52.2 1.0 pass_on.13.refs_5_
  53.2 1.9 %collective-permute-start.10 = (bf16[2,128,1024]{2,1,0:T(8,128)(2,1)S(1)}, bf16[2,128,1024]{2,1,0:T(8,128)(2,1)S(1)}, u32[]{:S(2)}, u32[]{:S(2)}) collective-permute-start(bf16[2,128,1024]{2,1,0:T(8,128)(2,1)S(1)} %pass_on.13.refs_5_), channel_id=1, source_target_pairs={{0,4},{4,8},{8,12},{1,5},{5,9},{9,13},{2,6},{6,10},{10,14},{3,7},{... | collective-permute-start | bytes 1572872 | tf_op jit(solution)/shard_map/ppermute | solution.py:417
  55.8 12.5 %collective-permute-start.13 = (bf16[4,128,1024]{2,1,0:T(8,128)(2,1)S(1)}, bf16[4,128,1024]{2,1,0:T(8,128)(2,1)S(1)}, u32[]{:S(2)}, u32[]{:S(2)}) collective-permute-start(bf16[4,128,1024]{2,1,0:T(8,128)(2,1)S(1)} %pass_down.3.refs_9_), channel_id=1, source_target_pairs={{4,0},{8,4},{12,8},{5,1},{9,5},{13,9},{6,2},{10,6},{14,10},{7,3},{... | collective-permute-start | bytes 3145736 | tf_op jit(solution)/shard_map/ppermute | solution.py:461
  68.3 1.8 %local_sums.6 = (f32[4,128,1024]{2,1,0:T(8,128)S(1)}, bf16[4,128,1024]{2,1,0:T(8,128)(2,1)S(1)}) custom-call(s32[11]{0:T(128)S(1)} %get-tuple-element.47.info_ref.refs_0_.ids_ref, bf16[4,128,1024]{2,1,0:T(8,128)(2,1)S(1)} %get-tuple-element.57.refs_0_.refs_1_, bf16[4,128,512]{2,1,0:T(8,128)(2,1)S(1)} %get-tuple-element.50.refs_1_.refs_2_, ...), custom_call_target="tpu_custom_call" | custom-call | flops 4000000000 | bytes 14000000 | tf_op jit(solution)/shard_map/local_sums/pallas_call | solution.py:467
  70.1 0.8 pass_on.14.refs_9_
  70.9 1.9 %collective-permute-start.12 = (bf16[2,128,1024]{2,1,0:T(8,128)(2,1)S(1)}, bf16[2,128,1024]{2,1,0:T(8,128)(2,1)S(1)}, u32[]{:S(2)}, u32[]{:S(2)}) collective-permute-start(bf16[2,128,1024]{2,1,0:T(8,128)(2,1)S(1)} %pass_on.14.refs_9_), channel_id=1, source_target_pairs={{0,4},{4,8},{8,12},{1,5},{5,9},{9,13},{2,6},{6,10},{10,14},{3,7},{... | collective-permute-start | bytes 1572872 | tf_op jit(solution)/shard_map/ppermute | solution.py:417
  72.8 1.8 %local_sums.7 = (f32[4,128,1024]{2,1,0:T(8,128)S(1)}, bf16[4,128,1024]{2,1,0:T(8,128)(2,1)S(1)}) custom-call(s32[11]{0:T(128)S(1)} %get-tuple-element.47.info_ref.refs_0_.ids_ref, bf16[4,128,1024]{2,1,0:T(8,128)(2,1)S(1)} %get-tuple-element.49.refs_0_.refs_1_, bf16[4,128,512]{2,1,0:T(8,128)(2,1)S(1)} %get-tuple-element.50.refs_1_.refs_2_, ...), custom_call_target="tpu_custom_call" | custom-call | flops 4000000000 | bytes 14000000 | tf_op jit(solution)/shard_map/local_sums/pallas_call | solution.py:467
  75.7 1.9 %collective-permute-start.11 = (bf16[2,128,1024]{2,1,0:T(8,128)(2,1)S(1)}, bf16[2,128,1024]{2,1,0:T(8,128)(2,1)S(1)}, u32[]{:S(2)}, u32[]{:S(2)}) collective-permute-start(bf16[2,128,1024]{2,1,0:T(8,128)(2,1)S(1)} %pass_on.15.refs_7_), channel_id=1, source_target_pairs={{0,4},{4,8},{8,12},{1,5},{5,9},{9,13},{2,6},{6,10},{10,14},{3,7},{... | collective-permute-start | bytes 1572872 | tf_op jit(solution)/shard_map/ppermute | solution.py:417
  77.6 8.4 %collective-permute-done.13.refs_2_.refs_15_ = bf16[4,128,1024]{2,1,0:T(8,128)(2,1)S(1)} collective-permute-done((bf16[4,128,1024]{2,1,0:T(8,128)(2,1)S(1)}, bf16[4,128,1024]{2,1,0:T(8,128)(2,1)S(1)}, u32[]{:S(2)}, u32[]{:S(2)}) %collective-permute-start.13) | collective-permute-done | bytes 1048608 | tf_op jit(solution)/shard_map/ppermute | solution.py:461
  86.1 0.9 pass_down.4.refs_16_
  87.0 4.1 %collective-permute-start.16 = (bf16[4,128,1024]{2,1,0:T(8,128)(2,1)S(1)}, bf16[4,128,1024]{2,1,0:T(8,128)(2,1)S(1)}, u32[]{:S(2)}, u32[]{:S(2)}) collective-permute-start(bf16[4,128,1024]{2,1,0:T(8,128)(2,1)S(1)} %pass_down.4.refs_16_), channel_id=1, source_target_pairs={{4,0},{8,4},{12,8},{5,1},{9,5},{13,9},{6,2},{10,6},{14,10},{7,3},{... | collective-permute-start | bytes 3145736 | tf_op jit(solution)/shard_map/ppermute | solution.py:461
  91.1 2.9 %finish.5 = (bf16[4,128,4096]{2,1,0:T(8,128)(2,1)}, f32[8,128]{1,0:T(8,128)S(1)}) custom-call(s32[11]{0:T(128)S(1)} %get-tuple-element.47.info_ref.refs_0_.ids_ref, f32[4,128,1024]{2,1,0:T(8,128)S(1)} %get-tuple-element.72.refs_8_.refs_1_, bf16[4,128,1024]{2,1,0:T(8,128)(2,1)S(1)} %get-tuple-element.78.refs_2_, ...), custom_call_target="tpu_custom_call" | custom-call | flops 6000000000 | bytes 21000000 | tf_op jit(solution)/shard_map/finish/pallas_call | solution.py:565
  94.8 1.9 %collective-permute-start.15 = (bf16[2,128,1024]{2,1,0:T(8,128)(2,1)S(1)}, bf16[2,128,1024]{2,1,0:T(8,128)(2,1)S(1)}, u32[]{:S(2)}, u32[]{:S(2)}) collective-permute-start(bf16[2,128,1024]{2,1,0:T(8,128)(2,1)S(1)} %pass_on.16.refs_7_), channel_id=1, source_target_pairs={{4,8},{8,12},{5,9},{9,13},{6,10},{10,14},{7,11},{11,15},{20,24},{2... | collective-permute-start | bytes 1572872 | tf_op jit(solution)/shard_map/ppermute | solution.py:417
  96.7 1.1 collective-permute-done.11.refs_3_.refs_12_.refs_11_.refs_4_.refs_8_.refs_7_
  98.6 1.9 %collective-permute-start.14 = (bf16[2,128,1024]{2,1,0:T(8,128)(2,1)S(1)}, bf16[2,128,1024]{2,1,0:T(8,128)(2,1)S(1)}, u32[]{:S(2)}, u32[]{:S(2)}) collective-permute-start(bf16[2,128,1024]{2,1,0:T(8,128)(2,1)S(1)} %pass_on.17.refs_9_), channel_id=1, source_target_pairs={{4,8},{8,12},{5,9},{9,13},{6,10},{10,14},{7,11},{11,15},{20,24},{2... | collective-permute-start | bytes 1572872 | tf_op jit(solution)/shard_map/ppermute | solution.py:417
  100.6 8.1 %collective-permute-done.16.refs_2_.refs_16_ = bf16[4,128,1024]{2,1,0:T(8,128)(2,1)S(1)} collective-permute-done((bf16[4,128,1024]{2,1,0:T(8,128)(2,1)S(1)}, bf16[4,128,1024]{2,1,0:T(8,128)(2,1)S(1)}, u32[]{:S(2)}, u32[]{:S(2)}) %collective-permute-start.16) | collective-permute-done | bytes 1048608 | tf_op jit(solution)/shard_map/ppermute | solution.py:461
  108.7 0.9 pass_down.5.refs_17_
  109.5 4.4 %collective-permute-start.18 = (bf16[4,128,1024]{2,1,0:T(8,128)(2,1)S(1)}, bf16[4,128,1024]{2,1,0:T(8,128)(2,1)S(1)}, u32[]{:S(2)}, u32[]{:S(2)}) collective-permute-start(bf16[4,128,1024]{2,1,0:T(8,128)(2,1)S(1)} %pass_down.5.refs_17_), channel_id=1, source_target_pairs={{4,0},{8,4},{12,8},{5,1},{9,5},{13,9},{6,2},{10,6},{14,10},{7,3},{... | collective-permute-start | bytes 3145736 | tf_op jit(solution)/shard_map/ppermute | solution.py:461
  114.0 2.9 %finish.6 = (bf16[4,128,4096]{2,1,0:T(8,128)(2,1)}, f32[8,128]{1,0:T(8,128)S(1)}) custom-call(s32[11]{0:T(128)S(1)} %get-tuple-element.47.info_ref.refs_0_.ids_ref, f32[4,128,1024]{2,1,0:T(8,128)S(1)} %get-tuple-element.73.refs_8_.refs_1_, bf16[4,128,1024]{2,1,0:T(8,128)(2,1)S(1)} %get-tuple-element.80.refs_2_, ...), custom_call_target="tpu_custom_call", output_to_operand_aliasing={{0}: (18, {})} | custom-call | flops 6000000000 | bytes 21000000 | tf_op jit(solution)/shard_map/finish/pallas_call | solution.py:565
  116.9 1.0 pass_on.18.refs_4_
  117.9 1.3 collective-permute-start.19
  120.1 1.3 collective-permute-start.17
  121.4 2.6 %finish.7 = (bf16[4,128,4096]{2,1,0:T(8,128)(2,1)}, f32[8,128]{1,0:T(8,128)S(1)}) custom-call(s32[11]{0:T(128)S(1)} %get-tuple-element.47.info_ref.refs_0_.ids_ref, f32[4,128,1024]{2,1,0:T(8,128)S(1)} %get-tuple-element.74.refs_6_.refs_1_, bf16[4,128,1024]{2,1,0:T(8,128)(2,1)S(1)} %get-tuple-element.83.refs_2_, ...), custom_call_target="tpu_custom_call", output_to_operand_aliasing={{0}: (15, {})} | custom-call | flops 6000000000 | bytes 21000000 | tf_op jit(solution)/shard_map/finish/pallas_call | solution.py:565
  124.0 7.1 %collective-permute-done.19.refs_9_ = bf16[2,128,1024]{2,1,0:T(8,128)(2,1)S(1)} collective-permute-done((bf16[2,128,1024]{2,1,0:T(8,128)(2,1)S(1)}, bf16[2,128,1024]{2,1,0:T(8,128)(2,1)S(1)}, u32[]{:S(2)}, u32[]{:S(2)}) %collective-permute-start.19) | collective-permute-done | bytes 524320 | tf_op jit(solution)/shard_map/ppermute | solution.py:417
  131.1 2.0 %finish.8 = (bf16[4,128,4096]{2,1,0:T(8,128)(2,1)}, f32[8,128]{1,0:T(8,128)S(1)}) custom-call(s32[11]{0:T(128)S(1)} %get-tuple-element.47.info_ref.refs_0_.ids_ref, f32[4,128,1024]{2,1,0:T(8,128)S(1)} %get-tuple-element.75.refs_6_.refs_1_, bf16[4,128,1024]{2,1,0:T(8,128)(2,1)S(1)} %get-tuple-element.76.refs_2_, ...), custom_call_target="tpu_custom_call", output_to_operand_aliasing={{0}: (13, {})} | custom-call | flops 6000000000 | bytes 21000000 | tf_op jit(solution)/shard_map/finish/pallas_call | solution.py:565
  133.1 2.7 %final_states.1 = (f32[4,1024,128]{2,1,0:T(8,128)}, f32[8,128]{1,0:T(8,128)S(1)}) custom-call(s32[11]{0:T(128)S(1)} %get-tuple-element.47.info_ref.refs_0_.ids_ref, f32[4,4,1,4096]{3,2,1,0:T(1,128)S(1)} %decays.1.refs_3_.refs_6_.refs_1_.refs_5_.refs_0_, bf16[4,128,1024]{2,1,0:T(8,128)(2,1)S(1)} %parents.1.refs_7_.refs_13_.refs_6_.refs_10_.refs_1_, ...), custom_call_target="tpu_custom_call" | custom-call | flops 10800000000 | bytes 37800000 | tf_op jit(solution)/shard_map/final_states/pallas_call | solution.py:623
  135.7 1.0 collective-permute-done.17.refs_9_
  136.7 2.5 %finish.9 = (bf16[4,128,4096]{2,1,0:T(8,128)(2,1)}, f32[8,128]{1,0:T(8,128)}) custom-call(s32[11]{0:T(128)S(1)} %get-tuple-element.47.info_ref.refs_0_.ids_ref, f32[4,128,1024]{2,1,0:T(8,128)S(1)} %get-tuple-element.75.refs_6_.refs_1_, bf16[4,128,1024]{2,1,0:T(8,128)(2,1)S(1)} %get-tuple-element.76.refs_2_, ...), custom_call_target="tpu_custom_call", output_to_operand_aliasing={{0}: (13, {})} | custom-call | flops 6000000000 | bytes 21000000 | tf_op jit(solution)/shard_map/finish/pallas_call | solution.py:565
  (29 shorter events, 6.8 us)
Async XLA Ops:
  6.6 12.0 %collective-permute-start.4 = (bf16[2,128,1024]{2,1,0:T(8,128)(2,1)S(1)}, bf16[2,128,1024]{2,1,0:T(8,128)(2,1)S(1)}, u32[]{:S(2)}, u32[]{:S(2)}) collective-permute-start(bf16[2,128,1024]{2,1,0:T(8,128)(2,1)S(1)} %get-tuple-element.64.refs_2_.refs_3_.refs_9_), channel_id=1, source_target_pairs={{0,4},{1,5},{2,6},{3,7},{16,20},{17,21},{18,22},{19,23}} | collective-permute-start | bytes 1572872 | tf_op jit(solution)/shard_map/ppermute | solution.py:417
  10.2 13.7 %collective-permute-start.3 = (bf16[2,1024,128]{2,1,0:T(8,128)(2,1)S(1)}, bf16[2,1024,128]{2,1,0:T(8,128)(2,1)S(1)}, u32[]{:S(2)}, u32[]{:S(2)}) collective-permute-start(bf16[2,1024,128]{2,1,0:T(8,128)(2,1)S(1)} %get-tuple-element.61), channel_id=1, source_target_pairs={{0,2},{2,0},{1,3},{3,1},{4,6},{6,4},{5,7},{7,5},{8,10},{10,8},{9,1... | collective-permute-start | bytes 1572872 | tf_op jit(solution)/shard_map/ppermute | solution.py:355
  11.8 16.1 %collective-permute-start.2 = (bf16[4,64,128]{2,1,0:T(8,128)(2,1)S(1)}, bf16[4,64,128]{2,1,0:T(8,128)(2,1)S(1)}, u32[]{:S(2)}, u32[]{:S(2)}) collective-permute-start(bf16[4,64,128]{2,1,0:T(8,128)(2,1)S(1)} %get-tuple-element.58.refs_1_), channel_id=1, source_target_pairs={{0,12},{4,0},{8,4},{12,8},{1,13},{5,1},{9,5},{13,9},{2,14},{6,2},{... | collective-permute-start | bytes 196616 | tf_op jit(solution)/shard_map/ppermute | solution.py:352
  12.8 19.6 %collective-permute-start.1 = (bf16[4,64,128]{2,1,0:T(8,128)(2,1)S(1)}, bf16[4,64,128]{2,1,0:T(8,128)(2,1)S(1)}, u32[]{:S(2)}, u32[]{:S(2)}) collective-permute-start(bf16[4,64,128]{2,1,0:T(8,128)(2,1)S(1)} %get-tuple-element.58.refs_1_), channel_id=1, source_target_pairs={{0,8},{4,12},{8,0},{12,4},{1,9},{5,13},{9,1},{13,5},{2,10},{6,14},... | collective-permute-start | bytes 196616 | tf_op jit(solution)/shard_map/ppermute | solution.py:352
  15.7 16.8 %collective-permute-start = (bf16[4,64,128]{2,1,0:T(8,128)(2,1)S(1)}, bf16[4,64,128]{2,1,0:T(8,128)(2,1)S(1)}, u32[]{:S(2)}, u32[]{:S(2)}) collective-permute-start(bf16[4,64,128]{2,1,0:T(8,128)(2,1)S(1)} %get-tuple-element.58.refs_1_), channel_id=1, source_target_pairs={{0,4},{4,8},{8,12},{12,0},{1,5},{5,9},{9,13},{13,1},{2,6},{6,10},{... | collective-permute-start | bytes 196616 | tf_op jit(solution)/shard_map/ppermute | solution.py:352
  18.6 18.9 %collective-permute-start.6 = (bf16[2,128,1024]{2,1,0:T(8,128)(2,1)S(1)}, bf16[2,128,1024]{2,1,0:T(8,128)(2,1)S(1)}, u32[]{:S(2)}, u32[]{:S(2)}) collective-permute-start(bf16[2,128,1024]{2,1,0:T(8,128)(2,1)S(1)} %get-tuple-element.48._.refs_2_.refs_3_.refs_4_.refs_10_), channel_id=1, source_target_pairs={{0,4},{1,5},{2,6},{3,7},{16,20},{17,21},{18,22},{19,23}} | collective-permute-start | bytes 1572872 | tf_op jit(solution)/shard_map/ppermute | solution.py:417
  19.3 5.9 %copy-start = (s32[8]{0:T(128)S(1)}, s32[8]{0:T(128)}, u32[]{:S(2)}) copy-start(s32[8]{0:T(128)} %refs_1_.1) | copy-start | bytes 100
  19.3 5.9 %copy-start.1 = (s32[4]{0:T(128)S(1)}, s32[4]{0:T(128)}, u32[]{:S(2)}) copy-start(s32[4]{0:T(128)} %refs_2_.1) | copy-start | bytes 52
  19.3 5.9 %copy-start.2 = (s32[4]{0:T(128)S(1)}, s32[4]{0:T(128)}, u32[]{:S(2)}) copy-start(s32[4]{0:T(128)} %refs_3_.1) | copy-start | bytes 52
  24.0 17.2 %collective-permute-start.5 = (bf16[2,128,1024]{2,1,0:T(8,128)(2,1)S(1)}, bf16[2,128,1024]{2,1,0:T(8,128)(2,1)S(1)}, u32[]{:S(2)}, u32[]{:S(2)}) collective-permute-start(bf16[2,128,1024]{2,1,0:T(8,128)(2,1)S(1)} %pass_on.10.refs_6_), channel_id=1, source_target_pairs={{0,4},{4,8},{1,5},{5,9},{2,6},{6,10},{3,7},{7,11},{16,20},{20,24},... | collective-permute-start | bytes 1572872 | tf_op jit(solution)/shard_map/ppermute | solution.py:417
  27.9 27.2 %collective-permute-start.8 = (bf16[4,128,1024]{2,1,0:T(8,128)(2,1)S(1)}, bf16[4,128,1024]{2,1,0:T(8,128)(2,1)S(1)}, u32[]{:S(2)}, u32[]{:S(2)}) collective-permute-start(bf16[4,128,1024]{2,1,0:T(8,128)(2,1)S(1)} %parents.1.refs_7_.refs_13_.refs_6_.refs_10_.refs_1_), channel_id=1, source_target_pairs={{4,0},{8,4},{12,8},{5,1},{9,5},{13,9},{6,2},{10,6},{14,10},{7,3},{... | collective-permute-start | bytes 3145736 | tf_op jit(solution)/shard_map/ppermute | solution.py:461
  38.1 14.1 %collective-permute-start.9 = (bf16[2,128,1024]{2,1,0:T(8,128)(2,1)S(1)}, bf16[2,128,1024]{2,1,0:T(8,128)(2,1)S(1)}, u32[]{:S(2)}, u32[]{:S(2)}) collective-permute-start(bf16[2,128,1024]{2,1,0:T(8,128)(2,1)S(1)} %pass_on.11.refs_9_), channel_id=1, source_target_pairs={{0,4},{4,8},{1,5},{5,9},{2,6},{6,10},{3,7},{7,11},{16,20},{20,24},... | collective-permute-start | bytes 1572872 | tf_op jit(solution)/shard_map/ppermute | solution.py:417
  42.4 27.7 %collective-permute-start.7 = (bf16[2,128,1024]{2,1,0:T(8,128)(2,1)S(1)}, bf16[2,128,1024]{2,1,0:T(8,128)(2,1)S(1)}, u32[]{:S(2)}, u32[]{:S(2)}) collective-permute-start(bf16[2,128,1024]{2,1,0:T(8,128)(2,1)S(1)} %pass_on.12.refs_9_), channel_id=1, source_target_pairs={{0,4},{4,8},{8,12},{1,5},{5,9},{9,13},{2,6},{6,10},{10,14},{3,7},{... | collective-permute-start | bytes 1572872 | tf_op jit(solution)/shard_map/ppermute | solution.py:417
  53.2 21.7 %collective-permute-start.10 = (bf16[2,128,1024]{2,1,0:T(8,128)(2,1)S(1)}, bf16[2,128,1024]{2,1,0:T(8,128)(2,1)S(1)}, u32[]{:S(2)}, u32[]{:S(2)}) collective-permute-start(bf16[2,128,1024]{2,1,0:T(8,128)(2,1)S(1)} %pass_on.13.refs_5_), channel_id=1, source_target_pairs={{0,4},{4,8},{8,12},{1,5},{5,9},{9,13},{2,6},{6,10},{10,14},{3,7},{... | collective-permute-start | bytes 1572872 | tf_op jit(solution)/shard_map/ppermute | solution.py:417
  55.8 30.3 %collective-permute-start.13 = (bf16[4,128,1024]{2,1,0:T(8,128)(2,1)S(1)}, bf16[4,128,1024]{2,1,0:T(8,128)(2,1)S(1)}, u32[]{:S(2)}, u32[]{:S(2)}) collective-permute-start(bf16[4,128,1024]{2,1,0:T(8,128)(2,1)S(1)} %pass_down.3.refs_9_), channel_id=1, source_target_pairs={{4,0},{8,4},{12,8},{5,1},{9,5},{13,9},{6,2},{10,6},{14,10},{7,3},{... | collective-permute-start | bytes 3145736 | tf_op jit(solution)/shard_map/ppermute | solution.py:461
  70.9 23.1 %collective-permute-start.12 = (bf16[2,128,1024]{2,1,0:T(8,128)(2,1)S(1)}, bf16[2,128,1024]{2,1,0:T(8,128)(2,1)S(1)}, u32[]{:S(2)}, u32[]{:S(2)}) collective-permute-start(bf16[2,128,1024]{2,1,0:T(8,128)(2,1)S(1)} %pass_on.14.refs_9_), channel_id=1, source_target_pairs={{0,4},{4,8},{8,12},{1,5},{5,9},{9,13},{2,6},{6,10},{10,14},{3,7},{... | collective-permute-start | bytes 1572872 | tf_op jit(solution)/shard_map/ppermute | solution.py:417
  75.7 22.1 %collective-permute-start.11 = (bf16[2,128,1024]{2,1,0:T(8,128)(2,1)S(1)}, bf16[2,128,1024]{2,1,0:T(8,128)(2,1)S(1)}, u32[]{:S(2)}, u32[]{:S(2)}) collective-permute-start(bf16[2,128,1024]{2,1,0:T(8,128)(2,1)S(1)} %pass_on.15.refs_7_), channel_id=1, source_target_pairs={{0,4},{4,8},{8,12},{1,5},{5,9},{9,13},{2,6},{6,10},{10,14},{3,7},{... | collective-permute-start | bytes 1572872 | tf_op jit(solution)/shard_map/ppermute | solution.py:417
  87.0 21.7 %collective-permute-start.16 = (bf16[4,128,1024]{2,1,0:T(8,128)(2,1)S(1)}, bf16[4,128,1024]{2,1,0:T(8,128)(2,1)S(1)}, u32[]{:S(2)}, u32[]{:S(2)}) collective-permute-start(bf16[4,128,1024]{2,1,0:T(8,128)(2,1)S(1)} %pass_down.4.refs_16_), channel_id=1, source_target_pairs={{4,0},{8,4},{12,8},{5,1},{9,5},{13,9},{6,2},{10,6},{14,10},{7,3},{... | collective-permute-start | bytes 3145736 | tf_op jit(solution)/shard_map/ppermute | solution.py:461
  94.8 22.1 %collective-permute-start.15 = (bf16[2,128,1024]{2,1,0:T(8,128)(2,1)S(1)}, bf16[2,128,1024]{2,1,0:T(8,128)(2,1)S(1)}, u32[]{:S(2)}, u32[]{:S(2)}) collective-permute-start(bf16[2,128,1024]{2,1,0:T(8,128)(2,1)S(1)} %pass_on.16.refs_7_), channel_id=1, source_target_pairs={{4,8},{8,12},{5,9},{9,13},{6,10},{10,14},{7,11},{11,15},{20,24},{2... | collective-permute-start | bytes 1572872 | tf_op jit(solution)/shard_map/ppermute | solution.py:417
  98.6 20.6 %collective-permute-start.14 = (bf16[2,128,1024]{2,1,0:T(8,128)(2,1)S(1)}, bf16[2,128,1024]{2,1,0:T(8,128)(2,1)S(1)}, u32[]{:S(2)}, u32[]{:S(2)}) collective-permute-start(bf16[2,128,1024]{2,1,0:T(8,128)(2,1)S(1)} %pass_on.17.refs_9_), channel_id=1, source_target_pairs={{4,8},{8,12},{5,9},{9,13},{6,10},{10,14},{7,11},{11,15},{20,24},{2... | collective-permute-start | bytes 1572872 | tf_op jit(solution)/shard_map/ppermute | solution.py:417
  109.5 23.5 %collective-permute-start.18 = (bf16[4,128,1024]{2,1,0:T(8,128)(2,1)S(1)}, bf16[4,128,1024]{2,1,0:T(8,128)(2,1)S(1)}, u32[]{:S(2)}, u32[]{:S(2)}) collective-permute-start(bf16[4,128,1024]{2,1,0:T(8,128)(2,1)S(1)} %pass_down.5.refs_17_), channel_id=1, source_target_pairs={{4,0},{8,4},{12,8},{5,1},{9,5},{13,9},{6,2},{10,6},{14,10},{7,3},{... | collective-permute-start | bytes 3145736 | tf_op jit(solution)/shard_map/ppermute | solution.py:461
  117.9 13.2 %collective-permute-start.19 = (bf16[2,128,1024]{2,1,0:T(8,128)(2,1)S(1)}, bf16[2,128,1024]{2,1,0:T(8,128)(2,1)S(1)}, u32[]{:S(2)}, u32[]{:S(2)}) collective-permute-start(bf16[2,128,1024]{2,1,0:T(8,128)(2,1)S(1)} %pass_on.18.refs_4_), channel_id=1, source_target_pairs={{8,12},{9,13},{10,14},{11,15},{24,28},{25,29},{26,30},{27,31}} | collective-permute-start | bytes 1572872 | tf_op jit(solution)/shard_map/ppermute | solution.py:417
  120.1 16.7 %collective-permute-start.17 = (bf16[2,128,1024]{2,1,0:T(8,128)(2,1)S(1)}, bf16[2,128,1024]{2,1,0:T(8,128)(2,1)S(1)}, u32[]{:S(2)}, u32[]{:S(2)}) collective-permute-start(bf16[2,128,1024]{2,1,0:T(8,128)(2,1)S(1)} %pass_on.19.refs_14_), channel_id=1, source_target_pairs={{8,12},{9,13},{10,14},{11,15},{24,28},{25,29},{26,30},{27,31}} | collective-permute-start | bytes 1572872 | tf_op jit(solution)/shard_map/ppermute | solution.py:417
